TPU v7x, 512 devices: a whole 4x8x8 slice. The times are simulated.
512 devices in a mesh: river: 16 (over y_hi, x, core), hours: 32 (over y_lo, z).
Axes of the slice: x: 4, y: 8 (y_hi: 2, y_lo: 4; y = y_hi * 4 + y_lo), z: 8, core: 2. Of those that a mesh axis runs over, the one named last changes fastest.
Arguments:
- release: float32 [160, 512, 512], P('river', 'hours'), may hold values from 0 to 1
- storage_dual: float32 [160, 512, 512], P('river', 'hours'), may hold values from -3 to 3
- demand_dual: float32 [512, 512], P('hours'), may hold values from -1 to 0
- cost: float32 [160, 512, 512], P('river', 'hours'), may hold values from -1.8 to 1.8
- inflow: float32 [160, 512, 512], P('river', 'hours'), may hold values from 0 to 1.2
- demand: float32 [512, 512], P('hours'), may hold values from 4.427189 to 8.221922
- storage_start: float32 [160], P('river'), may hold values from -0.5 to 0.5
- storage_low: float32 [160], P('river'), may hold values from -2 to -0.5
- storage_high: float32 [160], P('river'), may hold values from 0.5 to 2
- release_cap: float32 [160], P('river'), may hold values from 0.5 to 1.5
- efficiency: float32 [160], P('river'), may hold values from 0.5 to 1.5
- downstream: int32 [160], P('river'), may hold values from -1 to 159, as said below
- travel_delay: int32 [160], P('river'), may hold values from 1 to 6
Outputs:
- release_new: float32 [160, 512, 512], P('river', 'hours')
- storage_dual_new: float32 [160, 512, 512], P('river', 'hours')
- demand_dual_new: float32 [512, 512], P('hours')
- storage_excess: float32 [160, 512, 512], P('river', 'hours')
Inputs may be any that keep to these rules, and one draw needn't show every extreme that they name: Each reservoir's downstream index is -1 or lies 1 to 10 positions after its own index.
All inputs are finite; a program needn't handle non-finite values.
Results may differ from a plain program's by a relative error of at most 0.00013.
Values sent between devices are 32-bit elements; how exact they have to be, the bound alone decides.
A program may use at most 64 MiB of HBM per device.

v0:
```python
import math

import jax
import jax.numpy as jnp
from jax import lax
from jax.sharding import PartitionSpec as P

DMAX = 6


primal_step = 1.0
dual_step = 0.1


def passed_along(block, axis, distance):
    devices = range(lax.axis_size(axis))
    route = [(i - distance, i) for i in devices if i - distance in devices]
    return lax.ppermute(block, axis, route)


def prefix(part, axis, combine, identity, reverse):
    count = lax.axis_size(axis)
    place = lax.axis_index(axis)
    ahead = count - 1 - place if reverse else place
    gathered = lax.all_gather(part, axis)
    state = jnp.zeros_like(part) + jnp.asarray(identity, part.dtype)

    def one(turn, state):
        source = count - 1 - turn if reverse else turn
        return combine(state, lax.dynamic_index_in_dim(gathered, source, 0, False))

    return lax.fori_loop(0, ahead, one, state)


def add_pair(earlier_part, later_part):
    return earlier_part + later_part


def hold_back(field, travel_delay, earlier_rim):
    length = field.shape[1]
    extended = jnp.concatenate([earlier_rim, field], 1)
    result = jnp.zeros_like(field)
    for lag_hours in range(1, DMAX + 1):
        window = extended[:, DMAX - lag_hours : DMAX - lag_hours + length]
        result = result + jnp.where((travel_delay == lag_hours)[:, None, None], window, 0.0)
    return result


def bring_forward(field, travel_delay, later_rim):
    length = field.shape[1]
    extended = jnp.concatenate([field, later_rim], 1)
    result = jnp.zeros_like(field)
    for lag_hours in range(1, DMAX + 1):
        window = extended[:, lag_hours : lag_hours + length]
        result = result + jnp.where((travel_delay == lag_hours)[:, None, None], window, 0.0)
    return result


def route_down(matrix, field):
    return jnp.einsum("ij,jtw->itw", matrix, field, precision=lax.Precision.HIGHEST)


def route_up(matrix, field):
    return jnp.einsum("ij,itw->jtw", matrix, field, precision=lax.Precision.HIGHEST)


def iterate(fields, statics, scales, prefix_sum, suffix_sum, from_earlier, from_later):
    release, storage_dual, demand_dual, cost, inflow, demand = fields
    (
        storage_start,
        storage_low,
        storage_high,
        release_cap,
        efficiency,
        travel_delay,
        to_own,
        to_next,
    ) = statics
    scale_time, scale_sum = scales
    suffix = suffix_sum(storage_dual)
    beyond = passed_along(suffix, "river", -1)
    at_sink = route_up(to_own, suffix) + route_up(to_next, beyond)
    later_duals = bring_forward(at_sink, travel_delay, from_later(at_sink[:, :DMAX]))
    gradient = (
        cost
        + scale_time * (later_duals - suffix)
        + scale_sum * efficiency[:, None, None] * demand_dual[None]
    )
    release_new = jnp.clip(release - primal_step * gradient, 0.0, release_cap[:, None, None])
    extrapolated = 2.0 * release_new - release
    length = extrapolated.shape[1]
    delayed = hold_back(extrapolated, travel_delay, from_earlier(extrapolated[:, length - DMAX :]))
    incoming = passed_along(route_down(to_next, delayed), "river", 1)
    routed = route_down(to_own, delayed) + incoming
    storage = storage_start[:, None, None] + scale_time * prefix_sum(inflow + routed - extrapolated)
    lower_bound = storage_low[:, None, None]
    upper_bound = storage_high[:, None, None]
    storage_dual_new = (
        storage_dual
        + dual_step * storage
        - dual_step * jnp.clip(storage_dual / dual_step + storage, lower_bound, upper_bound)
    )
    storage_excess = storage - jnp.clip(storage, lower_bound, upper_bound)
    partial_power = jnp.sum(scale_sum * efficiency[:, None, None] * extrapolated, 0)
    supplied = lax.psum(partial_power, "river")
    demand_dual_new = jnp.minimum(demand_dual + dual_step * (supplied - demand), 0.0)
    return (release_new, storage_dual_new, demand_dual_new, storage_excess)


def suffix_local(field):
    return jnp.flip(jnp.cumsum(jnp.flip(field, 1), 1), 1)


def shards(
    release,
    storage_dual,
    demand_dual,
    cost,
    inflow,
    demand,
    storage_start,
    storage_low,
    storage_high,
    release_cap,
    efficiency,
    downstream,
    travel_delay,
):
    res_dev = release.shape[0]
    scale_time = 1.0 / (release.shape[1] * lax.axis_size("hours"))
    scale_sum = 1.0 / math.sqrt(res_dev * lax.axis_size("river"))
    base_index = lax.axis_index("river") * res_dev
    target = downstream - base_index
    indices = jnp.arange(res_dev, dtype=jnp.int32)
    to_own = (target[None, :] == indices[:, None]).astype(jnp.float32)
    to_next = (target[None, :] == indices[:, None] + res_dev).astype(jnp.float32)
    statics = (
        storage_start,
        storage_low,
        storage_high,
        release_cap,
        efficiency,
        travel_delay,
        to_own,
        to_next,
    )
    scales = (scale_time, scale_sum)

    def prefix_blocks(field):
        local_sum = jnp.cumsum(field, 1)
        totals = local_sum[:, -1]
        offset = prefix(totals, "hours", add_pair, jnp.zeros_like(totals), False)
        return local_sum + offset[:, None]

    def suffix_blocks(field):
        local_sum = suffix_local(field)
        totals = local_sum[:, 0]
        offset = prefix(totals, "hours", add_pair, jnp.zeros_like(totals), True)
        return local_sum + offset[:, None]

    def earlier_block(part):
        return passed_along(part, "hours", 1)

    def later_block(part):
        return passed_along(part, "hours", -1)

    fields = (release, storage_dual, demand_dual, cost, inflow, demand)
    return iterate(
        fields, statics, scales, prefix_blocks, suffix_blocks, earlier_block, later_block
    )


def solution(mesh):
    return jax.shard_map(
        shards,
        mesh=mesh,
        in_specs=(
            P("river", "hours", None),
            P("river", "hours", None),
            P("hours", None),
            P("river", "hours", None),
            P("river", "hours", None),
            P("hours", None),
            P("river"),
            P("river"),
            P("river"),
            P("river"),
            P("river"),
            P("river"),
            P("river"),
        ),
        out_specs=(
            P("river", "hours", None),
            P("river", "hours", None),
            P("hours", None),
            P("river", "hours", None),
        ),
        check_vma=False,
    )
```

profile of v0, /device:TPU:32, one launch (start us, length us, event | category | flops | bytes accessed | tf_op | source)
XLA Modules:
  0.0 301.1 jit_solution(5361114669511193955)
XLA Ops:
  0.6 1.8 rev.7
  2.5 0.4 fusion.45
  2.9 86.1 %all-gather = f32[320,1,512]{2,1,0:T(1,128)S(1)} all-gather(f32[10,1,512]{2,1,0:T(1,128)S(1)} %copy.42), channel_id=2, replica_groups=mesh['river'=16,'hours'=32] {'hours'}, dimensions={0}, use_global_device_ids=true | all-gather | bytes 675840 | tf_op jit(solution)/shard_map/all_gather | solution.py:25
  89.0 1.6 reduce
  90.5 0.1 reshape.29
  90.7 1.2 while.22
  91.9 1.9 collective-permute-start
  93.8 0.0 copy-start.7
  93.8 0.6 copy-done.7
  94.5 0.6 copy-done.8
  95.2 0.4 fusion.49
  95.6 4.9 %collective-permute-done = f32[10,16,512]{2,0,1:T(8,128)S(1)} collective-permute-done((f32[10,16,512]{2,0,1:T(8,128)S(1)}, f32[10,16,512]{2,0,1:T(8,128)S(1)}, u32[]{:S(2)}, u32[]{:S(2)}) %collective-permute-start) | collective-permute-done | bytes 327712 | tf_op jit(solution)/shard_map/ppermute | solution.py:18
  100.5 0.5 convolution_add_fusion.1
  101.0 0.0 copy-start.12
  101.0 0.0 copy-start.2
  101.0 0.0 copy-start.4
  101.1 1.4 collective-permute-start.1
  102.5 0.0 copy-done.12
  102.5 7.7 %collective-permute-done.1 = f32[10,6,512]{2,0,1:T(8,128)S(1)} collective-permute-done((f32[10,6,512]{2,0,1:T(8,128)S(1)}, f32[10,6,512]{2,0,1:T(8,128)S(1)}, u32[]{:S(2)}, u32[]{:S(2)}) %collective-permute-start.1) | collective-permute-done | bytes 122912 | tf_op jit(solution)/shard_map/ppermute | solution.py:18
  110.2 0.0 copy-done.3
  110.2 0.0 copy-done.2
  110.2 0.0 copy-done.4
  110.2 0.6 copy-done.6
  110.9 0.8 multiply_reduce_fusion
  111.6 1.5 collective-permute-start.2
  113.1 5.1 %collective-permute-done.2 = f32[10,6,512]{2,0,1:T(8,128)S(1)} collective-permute-done((f32[10,6,512]{2,0,1:T(8,128)S(1)}, f32[10,6,512]{2,0,1:T(8,128)S(1)}, u32[]{:S(2)}, u32[]{:S(2)}) %collective-permute-start.2) | collective-permute-done | bytes 122912 | tf_op jit(solution)/shard_map/ppermute | solution.py:18
  118.2 0.3 fusion.12
  118.5 0.4 fusion.51
  118.9 1.9 collective-permute-start.3
  120.8 0.0 copy-start.1
  120.8 0.9 copy.52
  121.7 91.9 %psum.7 = f32[16,512]{1,0:T(8,128)S(1)} all-reduce(f32[16,512]{1,0:T(8,128)S(1)} %get-tuple-element.113), channel_id=1, replica_groups=mesh['river'=16,'hours'=32] {'river'}, use_global_device_ids=true, to_apply=%region_7.8 | all-reduce | flops 8192 | bytes 65536 | tf_op jit(solution)/shard_map/psum | solution.py:105
  213.7 0.0 copy-done.5
  213.7 0.6 add_minimum_fusion
  214.3 0.0 collective-permute-done.3
  214.3 0.5 fusion.1
  214.8 2.7 fusion.63
  217.6 78.7 %all-gather.1 = f32[320,1,512]{2,1,0:T(1,128)S(1)} all-gather(f32[10,1,512]{2,1,0:T(1,128)S(1)} %copy.49), channel_id=3, replica_groups=mesh['river'=16,'hours'=32] {'hours'}, dimensions={0}, use_global_device_ids=true | all-gather | bytes 675840 | tf_op jit(solution)/shard_map/all_gather | solution.py:25
  296.3 1.6 reduce.1
  297.9 0.0 copy-start
  297.9 0.1 reshape.30
  298.0 0.0 copy-start.9
  298.0 0.0 copy-start.10
  298.0 0.0 copy-start.11
  298.0 0.8 copy-done
  298.8 0.4 minimum_subtract_fusion
  299.2 0.9 copy.54
  300.1 0.9 copy.53
  (52 shorter events, 0.5 us)
Async XLA Ops:
  91.9 8.6 %collective-permute-start = (f32[10,16,512]{2,0,1:T(8,128)S(1)}, f32[10,16,512]{2,0,1:T(8,128)S(1)}, u32[]{:S(2)}, u32[]{:S(2)}) collective-permute-start(f32[10,16,512]{2,0,1:T(8,128)S(1)} %reverse_add_fusion), channel_id=1, source_target_pairs={{32,0},{64,32},{96,64},{128,96},{160,128},{192,160},{224,192},{256... | collective-permute-start | bytes 983048 | tf_op jit(solution)/shard_map/ppermute | solution.py:18
  93.8 0.7 copy-start.7
  94.5 0.7 copy-start.8
  100.5 9.7 %copy-start.3 = (f32[10,16,512]{2,1,0:T(8,128)S(1)}, f32[10,16,512]{2,1,0:T(8,128)}, u32[]{:S(2)}) copy-start(f32[10,16,512]{2,1,0:T(8,128)} %param.20) | copy-start | bytes 983044
  101.0 1.5 copy-start.12
  101.0 9.2 %copy-start.2 = (f32[10,16,512]{2,1,0:T(8,128)S(1)}, f32[10,16,512]{2,1,0:T(8,128)}, u32[]{:S(2)}) copy-start(f32[10,16,512]{2,1,0:T(8,128)} %param.17) | copy-start | bytes 983044
  101.0 9.2 %copy-start.4 = (f32[16,512]{1,0:T(8,128)S(1)}, f32[16,512]{1,0:T(8,128)}, u32[]{:S(2)}) copy-start(f32[16,512]{1,0:T(8,128)} %param.19) | copy-start | bytes 98308
  101.1 9.1 %collective-permute-start.1 = (f32[10,6,512]{2,0,1:T(8,128)S(1)}, f32[10,6,512]{2,0,1:T(8,128)S(1)}, u32[]{:S(2)}, u32[]{:S(2)}) collective-permute-start(f32[10,6,512]{2,0,1:T(8,128)S(1)} %slice.66), channel_id=1, source_target_pairs={{1,0},{2,1},{3,2},{4,3},{5,4},{6,5},{7,6},{8,7},{9,8},{10,9},{11,1... | collective-permute-start | bytes 368648 | tf_op jit(solution)/shard_map/ppermute | solution.py:18
  110.2 0.7 copy-start.6
  111.6 6.5 %collective-permute-start.2 = (f32[10,6,512]{2,0,1:T(8,128)S(1)}, f32[10,6,512]{2,0,1:T(8,128)S(1)}, u32[]{:S(2)}, u32[]{:S(2)}) collective-permute-start(f32[10,6,512]{2,0,1:T(8,128)S(1)} %slice.77), channel_id=1, source_target_pairs={{0,1},{1,2},{2,3},{3,4},{4,5},{5,6},{6,7},{7,8},{8,9},{9,10},{10,1... | collective-permute-start | bytes 368648 | tf_op jit(solution)/shard_map/ppermute | solution.py:18
  118.9 95.4 %collective-permute-start.3 = (f32[10,16,512]{2,0,1:T(8,128)S(1)}, f32[10,16,512]{2,0,1:T(8,128)S(1)}, u32[]{:S(2)}, u32[]{:S(2)}) collective-permute-start(f32[10,16,512]{2,0,1:T(8,128)S(1)} %fusion.51), channel_id=1, source_target_pairs={{0,32},{32,64},{64,96},{96,128},{128,160},{160,192},{192,224},{224... | collective-permute-start | bytes 983048 | tf_op jit(solution)/shard_map/ppermute | solution.py:18
  120.8 93.5 %copy-start.1 = (f32[10,16,512]{2,1,0:T(8,128)S(1)}, f32[10,16,512]{2,1,0:T(8,128)}, u32[]{:S(2)}) copy-start(f32[10,16,512]{2,1,0:T(8,128)} %param.21) | copy-start | bytes 983044
  121.7 91.9 %copy-start.5 = (f32[16,512]{1,0:T(8,128)S(1)}, f32[16,512]{1,0:T(8,128)}, u32[]{:S(2)}) copy-start(f32[16,512]{1,0:T(8,128)} %param.22) | copy-start | bytes 98308
  297.9 1.0 copy-start
  298.0 0.8 copy-start.9
  298.0 0.8 copy-start.10
  298.0 0.8 copy-start.11
where the time goes:
time: 301 us
  blocking collectives  257 us (85%)
  waiting for transfers between devices  17.7 us (6%)
  other arithmetic  8.6 us (3%)
  local copies, waits for them, and re-layouts  7.67 us (3%)
  starting transfers between devices  6.72 us (2%)
    all_gather x2, blocking collectives, prefix(): gathered = lax.all_gather(part, axis)  165 us
    psum x1, blocking collectives, iterate(): supplied = lax.psum(partial_power, 'river')  91.9 us
    ppermute x4, waiting for transfers between devices, passed_along(): return lax.ppermute(block, axis, route)  17.7 us
    ppermute x4, starting transfers between devices, passed_along(): return lax.ppermute(block, axis, route)  6.72 us
  transfers between devices with their start and end apart: 4, of which 3 were waited for; matrix products, arithmetic and copies ran while one was open for 1% of the time, Pallas kernels for 0%

commit v1 on v0

--- a/solution.py
+++ b/solution.py
@@ -1,8 +1,11 @@
+import functools
 import math
 
 import jax
 import jax.numpy as jnp
 from jax import lax
+from jax.experimental import pallas as pl
+from jax.experimental.pallas import tpu as pltpu
 from jax.sharding import PartitionSpec as P
 
 DMAX = 6
@@ -18,18 +21,102 @@
     return lax.ppermute(block, axis, route)
 
 
-def prefix(part, axis, combine, identity, reverse):
-    count = lax.axis_size(axis)
-    place = lax.axis_index(axis)
-    ahead = count - 1 - place if reverse else place
-    gathered = lax.all_gather(part, axis)
-    state = jnp.zeros_like(part) + jnp.asarray(identity, part.dtype)
-
-    def one(turn, state):
-        source = count - 1 - turn if reverse else turn
-        return combine(state, lax.dynamic_index_in_dim(gathered, source, 0, False))
-
-    return lax.fori_loop(0, ahead, one, state)
+def exchange_kernel(n, axis, other, mode, x_ref, out_ref, slots, send_sem, recv_sem):
+    me = lax.axis_index(axis)
+    fixed = lax.axis_index(other)
+
+    def device(p):
+        return (fixed, p) if axis == "hours" else (p, fixed)
+
+    def wanted(src, dst):
+        if mode == "prefix":
+            return src < dst
+        if mode == "suffix":
+            return src > dst
+        return src != dst
+
+    barrier = pltpu.get_barrier_semaphore()
+
+    def greet(i, carry):
+        p = lax.rem(me + 1 + i, n)
+        pl.semaphore_signal(barrier, 1, device_id=device(p), device_id_type=pl.DeviceIdType.MESH)
+        return carry
+
+    lax.fori_loop(0, n - 1, greet, 0)
+    pl.semaphore_wait(barrier, n - 1)
+
+    def outgoing(p):
+        return pltpu.make_async_remote_copy(
+            src_ref=x_ref,
+            dst_ref=slots.at[me],
+            send_sem=send_sem.at[p],
+            recv_sem=recv_sem.at[me],
+            device_id=device(p),
+            device_id_type=pl.DeviceIdType.MESH,
+        )
+
+    def incoming(p):
+        return pltpu.make_async_remote_copy(
+            src_ref=x_ref,
+            dst_ref=slots.at[p],
+            send_sem=send_sem.at[p],
+            recv_sem=recv_sem.at[p],
+            device_id=device(p),
+            device_id_type=pl.DeviceIdType.MESH,
+        )
+
+    def send(i, carry):
+        p = lax.rem(me + 1 + i, n)
+
+        @pl.when(wanted(me, p))
+        def _():
+            outgoing(p).start()
+
+        return carry
+
+    lax.fori_loop(0, n - 1, send, 0)
+
+    def settle(i, carry):
+        p = lax.rem(me + 1 + i, n)
+
+        @pl.when(wanted(me, p))
+        def _():
+            outgoing(p).wait_send()
+
+        @pl.when(wanted(p, me))
+        def _():
+            incoming(p).wait_recv()
+
+        return carry
+
+    lax.fori_loop(0, n - 1, settle, 0)
+    start = x_ref[...] if mode == "sum" else jnp.zeros_like(x_ref[...])
+
+    def total(i, acc):
+        p = lax.rem(me + 1 + i, n)
+        return acc + jnp.where(wanted(p, me), slots[p], 0.0)
+
+    out_ref[...] = lax.fori_loop(0, n - 1, total, start)
+
+
+IDS = {"prefix": 0, "suffix": 1, "sum": 2}
+
+
+def exchange(part, axis, mode):
+    n = lax.axis_size(axis)
+    other = "river" if axis == "hours" else "hours"
+    return pl.pallas_call(
+        functools.partial(exchange_kernel, n, axis, other, mode),
+        out_shape=jax.ShapeDtypeStruct(part.shape, part.dtype),
+        in_specs=[pl.BlockSpec(memory_space=pltpu.VMEM)],
+        out_specs=pl.BlockSpec(memory_space=pltpu.VMEM),
+        scratch_shapes=[
+            pltpu.VMEM((n,) + part.shape, part.dtype),
+            pltpu.SemaphoreType.DMA((n,)),
+            pltpu.SemaphoreType.DMA((n,)),
+        ],
+        compiler_params=pltpu.CompilerParams(collective_id=IDS[mode], has_side_effects=True),
+    )(part)
 
 
 def add_pair(earlier_part, later_part):
@@ -102,7 +189,7 @@
     )
     storage_excess = storage - jnp.clip(storage, lower_bound, upper_bound)
     partial_power = jnp.sum(scale_sum * efficiency[:, None, None] * extrapolated, 0)
-    supplied = lax.psum(partial_power, "river")
+    supplied = exchange(partial_power, "river", "sum")
     demand_dual_new = jnp.minimum(demand_dual + dual_step * (supplied - demand), 0.0)
     return (release_new, storage_dual_new, demand_dual_new, storage_excess)
 
@@ -149,13 +236,13 @@
     def prefix_blocks(field):
         local_sum = jnp.cumsum(field, 1)
         totals = local_sum[:, -1]
-        offset = prefix(totals, "hours", add_pair, jnp.zeros_like(totals), False)
+        offset = exchange(totals, "hours", "prefix")
         return local_sum + offset[:, None]
 
     def suffix_blocks(field):
         local_sum = suffix_local(field)
         totals = local_sum[:, 0]
-        offset = prefix(totals, "hours", add_pair, jnp.zeros_like(totals), True)
+        offset = exchange(totals, "hours", "suffix")
         return local_sum + offset[:, None]
 
     def earlier_block(part):

time: 301 us -> 152 us (0.50)
  the two profiles are of different devices: /device:TPU:32 before, /device:TPU:442 now
where the time goes in v1:
time: 152 us; the launch traced here: 151 us
  Pallas kernels  106 us (70%)
  waiting for transfers between devices  19.2 us (13%)
  local copies, waits for them, and re-layouts  7.86 us (5%)
  starting transfers between devices  7.81 us (5%)
  other arithmetic  7.3 us (5%)
  matrix products  1.9 us (1%)
    pallas_call x3, Pallas kernels, exchange(): pl.pallas_call(functools.partial(exchange_kernel, n, axis, other, mode),...  106 us
    ppermute x4, waiting for transfers between devices, passed_along(): return lax.ppermute(block, axis, route)  19.2 us
    ppermute x4, starting transfers between devices, passed_along(): return lax.ppermute(block, axis, route)  7.81 us
    unnamed x33, local copies, waits for them, and re-layouts  4.75 us
  transfers between devices with their start and end apart: 4, of which 3 were waited for; matrix products, arithmetic and copies ran while one was open for 1% of the time, Pallas kernels for 13%

profile of v1, /device:TPU:442, one launch (start us, length us, event | category | flops | bytes accessed | tf_op | source)
XLA Modules:
  0.0 150.8 jit_solution(17935891088574383553)
XLA Ops:
  0.6 1.8 %rev.7 = f32[10,16,512]{2,1,0:T(8,128)S(1)} reverse(f32[10,16,512]{2,1,0:T(8,128)} %param.14), dimensions={1} | reverse | bytes 655360 | tf_op jit(solution)/shard_map/jit(_flip)/rev | solution.py:198
  2.5 0.4 fusion.45
  2.9 0.6 slice_bitcast_fusion.1.x_ref
  3.5 31.0 %shard_map.156 = f32[10,512]{1,0:T(8,128)} custom-call(f32[10,512]{1,0:T(8,128)} %slice_bitcast_fusion.1.x_ref), custom_call_target="tpu_custom_call" | custom-call | tf_op jit(solution)/shard_map/pallas_call | solution.py:108
  34.5 0.8 reverse_add_fusion
  35.3 1.9 %collective-permute-start = (f32[10,16,512]{2,0,1:T(8,128)S(1)}, f32[10,16,512]{2,0,1:T(8,128)S(1)}, u32[]{:S(2)}, u32[]{:S(2)}) collective-permute-start(f32[10,16,512]{2,0,1:T(8,128)S(1)} %reverse_add_fusion), channel_id=1, source_target_pairs={{32,0},{64,32},{96,64},{128,96},{160,128},{192,160},{224,192},{256... | collective-permute-start | bytes 983048 | tf_op jit(solution)/shard_map/ppermute | solution.py:21
  37.3 0.0 copy-start.9
  37.3 0.6 copy-done.9
  38.0 0.6 copy-done.10
  38.6 0.4 fusion.49
  39.0 4.9 %collective-permute-done = f32[10,16,512]{2,0,1:T(8,128)S(1)} collective-permute-done((f32[10,16,512]{2,0,1:T(8,128)S(1)}, f32[10,16,512]{2,0,1:T(8,128)S(1)}, u32[]{:S(2)}, u32[]{:S(2)}) %collective-permute-start) | collective-permute-done | bytes 327712 | tf_op jit(solution)/shard_map/ppermute | solution.py:21
  44.0 0.5 convolution_add_fusion.1
  44.5 0.0 copy-start.2
  44.5 0.0 copy-start.4
  44.5 0.0 copy-start.5
  44.5 2.1 %collective-permute-start.1 = (f32[10,6,512]{2,0,1:T(8,128)S(1)}, f32[10,6,512]{2,0,1:T(8,128)S(1)}, u32[]{:S(2)}, u32[]{:S(2)}) collective-permute-start(f32[10,6,512]{2,0,1:T(8,128)S(1)} %slice.66), channel_id=1, source_target_pairs={{1,0},{2,1},{3,2},{4,3},{5,4},{6,5},{7,6},{8,7},{9,8},{10,9},{11,1... | collective-permute-start | bytes 368648 | tf_op jit(solution)/shard_map/ppermute | solution.py:21
  46.6 0.0 copy-done.14
  46.6 7.0 %collective-permute-done.1 = f32[10,6,512]{2,0,1:T(8,128)S(1)} collective-permute-done((f32[10,6,512]{2,0,1:T(8,128)S(1)}, f32[10,6,512]{2,0,1:T(8,128)S(1)}, u32[]{:S(2)}, u32[]{:S(2)}) %collective-permute-start.1) | collective-permute-done | bytes 122912 | tf_op jit(solution)/shard_map/ppermute | solution.py:21
  53.5 0.0 copy-done.3
  53.6 0.0 copy-done.2
  53.6 0.0 copy-done.4
  53.6 0.0 copy-done.5
  53.6 0.6 copy-done.8
  54.2 1.4 multiply_reduce_fusion
  55.6 1.9 %collective-permute-start.2 = (f32[10,6,512]{2,0,1:T(8,128)S(1)}, f32[10,6,512]{2,0,1:T(8,128)S(1)}, u32[]{:S(2)}, u32[]{:S(2)}) collective-permute-start(f32[10,6,512]{2,0,1:T(8,128)S(1)} %slice.77), channel_id=1, source_target_pairs={{0,1},{1,2},{2,3},{3,4},{4,5},{5,6},{6,7},{7,8},{8,9},{9,10},{10,1... | collective-permute-start | bytes 368648 | tf_op jit(solution)/shard_map/ppermute | solution.py:21
  57.5 7.4 %collective-permute-done.2 = f32[10,6,512]{2,0,1:T(8,128)S(1)} collective-permute-done((f32[10,6,512]{2,0,1:T(8,128)S(1)}, f32[10,6,512]{2,0,1:T(8,128)S(1)}, u32[]{:S(2)}, u32[]{:S(2)}) %collective-permute-start.2) | collective-permute-done | bytes 122912 | tf_op jit(solution)/shard_map/ppermute | solution.py:21
  64.9 0.3 fusion.12
  65.2 0.4 fusion.51
  65.6 1.9 %collective-permute-start.3 = (f32[10,16,512]{2,0,1:T(8,128)S(1)}, f32[10,16,512]{2,0,1:T(8,128)S(1)}, u32[]{:S(2)}, u32[]{:S(2)}) collective-permute-start(f32[10,16,512]{2,0,1:T(8,128)S(1)} %fusion.51), channel_id=1, source_target_pairs={{0,32},{32,64},{64,96},{96,128},{128,160},{160,192},{192,224},{224... | collective-permute-start | bytes 983048 | tf_op jit(solution)/shard_map/ppermute | solution.py:21
  67.5 19.0 %shard_map.158 = f32[16,512]{1,0:T(8,128)} custom-call(f32[16,512]{1,0:T(8,128)} %get-tuple-element.8.x_ref), custom_call_target="tpu_custom_call" | custom-call | tf_op jit(solution)/shard_map/pallas_call | solution.py:108
  86.5 0.0 copy-start.6
  86.5 0.0 copy-start.7
  86.5 0.0 copy-start.1
  86.5 0.9 copy.26
  87.4 0.0 copy-done.6
  87.4 0.0 copy-done.7
  87.4 0.6 add_minimum_fusion
  88.1 0.0 collective-permute-done.3
  88.1 0.0 copy-done.1
  88.1 0.6 fusion.1
  88.7 0.0 copy-start
  88.7 2.7 %fusion.63 = f32[10,16,512]{2,0,1:T(8,128)S(1)} fusion(f32[10,16,512]{2,0,1:T(8,128)S(1)} %fusion.1), kind=kOutput, calls=%fused_computation.105 | output fusion | flops 1228800 | bytes 655360 | tf_op jit(solution)/shard_map/jit(cumsum)/reduce_window_sum | solution.py:237
  91.4 0.6 slice_bitcast_fusion.x_ref
  92.0 55.8 %shard_map.157 = f32[10,512]{1,0:T(8,128)} custom-call(f32[10,512]{1,0:T(8,128)} %slice_bitcast_fusion.x_ref), custom_call_target="tpu_custom_call" | custom-call | tf_op jit(solution)/shard_map/pallas_call | solution.py:108
  147.8 0.0 copy-done
  147.9 1.1 minimum_subtract_fusion
  149.0 0.9 copy.28
  149.9 0.9 copy.27
  (15 shorter events, 0.1 us)
Async XLA Ops:
  35.3 8.6 %collective-permute-start = (f32[10,16,512]{2,0,1:T(8,128)S(1)}, f32[10,16,512]{2,0,1:T(8,128)S(1)}, u32[]{:S(2)}, u32[]{:S(2)}) collective-permute-start(f32[10,16,512]{2,0,1:T(8,128)S(1)} %reverse_add_fusion), channel_id=1, source_target_pairs={{32,0},{64,32},{96,64},{128,96},{160,128},{192,160},{224,192},{256... | collective-permute-start | bytes 983048 | tf_op jit(solution)/shard_map/ppermute | solution.py:21
  37.3 0.7 copy-start.9
  37.9 0.7 copy-start.10
  44.0 2.6 %copy-start.14 = (f32[10]{0:T(128)S(1)}, f32[10]{0:T(128)}, u32[]{:S(2)}) copy-start(f32[10]{0:T(128)} %param.23) | copy-start | bytes 124
  44.0 9.6 %copy-start.3 = (f32[10,16,512]{2,1,0:T(8,128)S(1)}, f32[10,16,512]{2,1,0:T(8,128)}, u32[]{:S(2)}) copy-start(f32[10,16,512]{2,1,0:T(8,128)} %param.16) | copy-start | bytes 983044
  44.5 9.1 %copy-start.2 = (f32[10,16,512]{2,1,0:T(8,128)S(1)}, f32[10,16,512]{2,1,0:T(8,128)}, u32[]{:S(2)}) copy-start(f32[10,16,512]{2,1,0:T(8,128)} %param.13) | copy-start | bytes 983044
  44.5 9.1 %copy-start.4 = (f32[10,512]{1,0:T(8,128)S(1)}, f32[10,512]{1,0:T(8,128)}, u32[]{:S(2)}) copy-start(f32[10,512]{1,0:T(8,128)} %shard_map.156) | copy-start | bytes 61444
  44.5 9.1 %copy-start.5 = (f32[16,512]{1,0:T(8,128)S(1)}, f32[16,512]{1,0:T(8,128)}, u32[]{:S(2)}) copy-start(f32[16,512]{1,0:T(8,128)} %param.15) | copy-start | bytes 98308
  44.5 9.0 %collective-permute-start.1 = (f32[10,6,512]{2,0,1:T(8,128)S(1)}, f32[10,6,512]{2,0,1:T(8,128)S(1)}, u32[]{:S(2)}, u32[]{:S(2)}) collective-permute-start(f32[10,6,512]{2,0,1:T(8,128)S(1)} %slice.66), channel_id=1, source_target_pairs={{1,0},{2,1},{3,2},{4,3},{5,4},{6,5},{7,6},{8,7},{9,8},{10,9},{11,1... | collective-permute-start | bytes 368648 | tf_op jit(solution)/shard_map/ppermute | solution.py:21
  53.5 0.7 copy-start.8
  55.6 9.3 %collective-permute-start.2 = (f32[10,6,512]{2,0,1:T(8,128)S(1)}, f32[10,6,512]{2,0,1:T(8,128)S(1)}, u32[]{:S(2)}, u32[]{:S(2)}) collective-permute-start(f32[10,6,512]{2,0,1:T(8,128)S(1)} %slice.77), channel_id=1, source_target_pairs={{0,1},{1,2},{2,3},{3,4},{4,5},{5,6},{6,7},{7,8},{8,9},{9,10},{10,1... | collective-permute-start | bytes 368648 | tf_op jit(solution)/shard_map/ppermute | solution.py:21
  65.6 22.5 %collective-permute-start.3 = (f32[10,16,512]{2,0,1:T(8,128)S(1)}, f32[10,16,512]{2,0,1:T(8,128)S(1)}, u32[]{:S(2)}, u32[]{:S(2)}) collective-permute-start(f32[10,16,512]{2,0,1:T(8,128)S(1)} %fusion.51), channel_id=1, source_target_pairs={{0,32},{32,64},{64,96},{96,128},{128,160},{160,192},{192,224},{224... | collective-permute-start | bytes 983048 | tf_op jit(solution)/shard_map/ppermute | solution.py:21
  86.5 1.0 copy-start.6
  86.5 0.9 copy-start.7
  86.5 1.6 %copy-start.1 = (f32[10,16,512]{2,1,0:T(8,128)S(1)}, f32[10,16,512]{2,1,0:T(8,128)}, u32[]{:S(2)}) copy-start(f32[10,16,512]{2,1,0:T(8,128)} %param.17) | copy-start | bytes 983044
  88.7 59.2 %copy-start = (f32[10,16,512]{2,1,0:T(8,128)S(1)}, f32[10,16,512]{2,1,0:T(8,128)}, u32[]{:S(2)}) copy-start(f32[10,16,512]{2,1,0:T(8,128)} %param.14) | copy-start | bytes 983044
  92.0 55.8 %copy-start.11 = (f32[10]{0:T(128)S(1)}, f32[10]{0:T(128)}, u32[]{:S(2)}) copy-start(f32[10]{0:T(128)} %param.20) | copy-start | bytes 124
  92.0 55.8 %copy-start.12 = (f32[10]{0:T(128)S(1)}, f32[10]{0:T(128)}, u32[]{:S(2)}) copy-start(f32[10]{0:T(128)} %param.21) | copy-start | bytes 124
  92.0 55.8 %copy-start.13 = (f32[10]{0:T(128)S(1)}, f32[10]{0:T(128)}, u32[]{:S(2)}) copy-start(f32[10]{0:T(128)} %param.19) | copy-start | bytes 124

commit v2 on v0

--- a/solution.py
+++ b/solution.py
@@ -1,8 +1,11 @@
+import functools
 import math
 
 import jax
 import jax.numpy as jnp
 from jax import lax
+from jax.experimental import pallas as pl
+from jax.experimental.pallas import tpu as pltpu
 from jax.sharding import PartitionSpec as P
 
 DMAX = 6
@@ -18,18 +21,122 @@
     return lax.ppermute(block, axis, route)
 
 
-def prefix(part, axis, combine, identity, reverse):
-    count = lax.axis_size(axis)
-    place = lax.axis_index(axis)
-    ahead = count - 1 - place if reverse else place
-    gathered = lax.all_gather(part, axis)
-    state = jnp.zeros_like(part) + jnp.asarray(identity, part.dtype)
-
-    def one(turn, state):
-        source = count - 1 - turn if reverse else turn
-        return combine(state, lax.dynamic_index_in_dim(gathered, source, 0, False))
-
-    return lax.fori_loop(0, ahead, one, state)
+MESH = pl.DeviceIdType.MESH
+
+
+def two_level_kernel(inner, outer, axis, other, mode, x_ref, out_ref, near, far, group, s1, r1, s2, r2):
+    me = lax.axis_index(axis)
+    fixed = lax.axis_index(other)
+    o = me // inner
+    i = me % inner
+
+    def device(p):
+        return (fixed, p) if axis == "hours" else (p, fixed)
+
+    def wanted(src, dst):
+        if mode == "prefix":
+            return src < dst
+        if mode == "suffix":
+            return src > dst
+        return src != dst
+
+    barrier = pltpu.get_barrier_semaphore()
+    for step in range(1, inner):
+        pl.semaphore_signal(barrier, 1, device_id=device(o * inner + lax.rem(i + step, inner)), device_id_type=MESH)
+    for step in range(1, outer):
+        pl.semaphore_signal(barrier, 1, device_id=device(lax.rem(o + step, outer) * inner + i), device_id_type=MESH)
+    pl.semaphore_wait(barrier, inner + outer - 2)
+
+    def across(step):
+        p = lax.rem(i + step, inner)
+        return pltpu.make_async_remote_copy(
+            src_ref=x_ref, dst_ref=near.at[i], send_sem=s1.at[p], recv_sem=r1.at[i],
+            device_id=device(o * inner + p), device_id_type=MESH)
+
+    def arrived(step):
+        p = lax.rem(i + step, inner)
+        return pltpu.make_async_remote_copy(
+            src_ref=x_ref, dst_ref=near.at[p], send_sem=s1.at[p], recv_sem=r1.at[p],
+            device_id=device(o * inner + p), device_id_type=MESH)
+
+    for step in range(1, inner):
+        across(step).start()
+    for step in range(1, inner):
+        across(step).wait_send()
+        arrived(step).wait_recv()
+
+    own = x_ref[...]
+    total = own
+    part = own if mode == "sum" else jnp.zeros_like(own)
+    for step in range(1, inner):
+        p = lax.rem(i + step, inner)
+        block = near[p]
+        total = total + block
+        if mode == "sum":
+            part = part + block
+        else:
+            part = part + jnp.where(wanted(p, i), block, 0.0)
+    group[...] = total
+
+    def up(step):
+        q = lax.rem(o + step, outer)
+        return pltpu.make_async_remote_copy(
+            src_ref=group, dst_ref=far.at[o], send_sem=s2.at[q], recv_sem=r2.at[o],
+            device_id=device(q * inner + i), device_id_type=MESH)
+
+    def got(step):
+        q = lax.rem(o + step, outer)
+        return pltpu.make_async_remote_copy(
+            src_ref=group, dst_ref=far.at[q], send_sem=s2.at[q], recv_sem=r2.at[q],
+            device_id=device(q * inner + i), device_id_type=MESH)
+
+    for step in range(1, outer):
+        q = lax.rem(o + step, outer)
+
+        @pl.when(wanted(o, q))
+        def _():
+            up(step).start()
+
+    for step in range(1, outer):
+        q = lax.rem(o + step, outer)
+
+        @pl.when(wanted(o, q))
+        def _():
+            up(step).wait_send()
+
+        @pl.when(wanted(q, o))
+        def _():
+            got(step).wait_recv()
+
+    for step in range(1, outer):
+        q = lax.rem(o + step, outer)
+        part = part + jnp.where(wanted(q, o), far[q], 0.0)
+    out_ref[...] = part
+
+
+IDS = {"prefix": 0, "suffix": 1, "sum": 2}
+
+
+def two_level(part, axis, mode, inner):
+    n = lax.axis_size(axis)
+    outer = n // inner
+    other = "river" if axis == "hours" else "hours"
+    return pl.pallas_call(
+        functools.partial(two_level_kernel, inner, outer, axis, other, mode),
+        out_shape=jax.ShapeDtypeStruct(part.shape, part.dtype),
+        in_specs=[pl.BlockSpec(memory_space=pltpu.VMEM)],
+        out_specs=pl.BlockSpec(memory_space=pltpu.VMEM),
+        scratch_shapes=[
+            pltpu.VMEM((inner,) + part.shape, part.dtype),
+            pltpu.VMEM((outer,) + part.shape, part.dtype),
+            pltpu.VMEM(part.shape, part.dtype),
+            pltpu.SemaphoreType.DMA((inner,)),
+            pltpu.SemaphoreType.DMA((inner,)),
+            pltpu.SemaphoreType.DMA((outer,)),
+            pltpu.SemaphoreType.DMA((outer,)),
+        ],
+        compiler_params=pltpu.CompilerParams(collective_id=IDS[mode], has_side_effects=True),
+    )(part)
 
 
 def add_pair(earlier_part, later_part):
@@ -102,7 +209,7 @@
     )
     storage_excess = storage - jnp.clip(storage, lower_bound, upper_bound)
     partial_power = jnp.sum(scale_sum * efficiency[:, None, None] * extrapolated, 0)
-    supplied = lax.psum(partial_power, "river")
+    supplied = two_level(partial_power, "river", "sum", 8)
     demand_dual_new = jnp.minimum(demand_dual + dual_step * (supplied - demand), 0.0)
     return (release_new, storage_dual_new, demand_dual_new, storage_excess)
 
@@ -149,13 +256,13 @@
     def prefix_blocks(field):
         local_sum = jnp.cumsum(field, 1)
         totals = local_sum[:, -1]
-        offset = prefix(totals, "hours", add_pair, jnp.zeros_like(totals), False)
+        offset = two_level(totals, "hours", "prefix", 8)
         return local_sum + offset[:, None]
 
     def suffix_blocks(field):
         local_sum = suffix_local(field)
         totals = local_sum[:, 0]
-        offset = prefix(totals, "hours", add_pair, jnp.zeros_like(totals), True)
+        offset = two_level(totals, "hours", "suffix", 8)
         return local_sum + offset[:, None]
 
     def earlier_block(part):

time: 301 us -> 114 us (0.38)
  the two profiles are of different devices: /device:TPU:32 before, /device:TPU:30 now
where the time goes in v2:
time: 114 us; the launch traced here: 113 us
  Pallas kernels  60 us (53%)
  starting transfers between devices  19.7 us (17%)
  waiting for transfers between devices  15.5 us (14%)
  local copies, waits for them, and re-layouts  7.86 us (7%)
  other arithmetic  7.3 us (6%)
  matrix products  1.9 us (2%)
    pallas_call x3, Pallas kernels, two_level(): pl.pallas_call(functools.partial(two_level_kernel, inner, outer, axis, ot...  60 us
    ppermute x4, starting transfers between devices, passed_along(): return lax.ppermute(block, axis, route)  19.7 us
    ppermute x4, waiting for transfers between devices, passed_along(): return lax.ppermute(block, axis, route)  15.5 us
    unnamed x33, local copies, waits for them, and re-layouts  4.75 us
    another operation x1, other arithmetic, prefix_blocks(): local_sum = jnp.cumsum(field, 1)  2.71 us
  transfers between devices with their start and end apart: 4, of which 3 were waited for; matrix products, arithmetic and copies ran while one was open for 2% of the time, Pallas kernels for 16%

profile of v2, /device:TPU:30, one launch (start us, length us, event | category | flops | bytes accessed | tf_op | source)
XLA Modules:
  0.0 113.2 jit_solution(12572793794946326693)
XLA Ops:
  0.6 1.8 %rev.7 = f32[10,16,512]{2,1,0:T(8,128)S(1)} reverse(f32[10,16,512]{2,1,0:T(8,128)} %param.14), dimensions={1} | reverse | bytes 655360 | tf_op jit(solution)/shard_map/jit(_flip)/rev | solution.py:218
  2.5 0.4 fusion.45
  2.9 0.6 slice_bitcast_fusion.1.x_ref
  3.5 21.6 %shard_map.156 = f32[10,512]{1,0:T(8,128)} custom-call(f32[10,512]{1,0:T(8,128)} %slice_bitcast_fusion.1.x_ref), custom_call_target="tpu_custom_call" | custom-call | tf_op jit(solution)/shard_map/pallas_call | solution.py:124
  25.1 0.8 reverse_add_fusion
  25.9 1.9 %collective-permute-start = (f32[10,16,512]{2,0,1:T(8,128)S(1)}, f32[10,16,512]{2,0,1:T(8,128)S(1)}, u32[]{:S(2)}, u32[]{:S(2)}) collective-permute-start(f32[10,16,512]{2,0,1:T(8,128)S(1)} %reverse_add_fusion), channel_id=1, source_target_pairs={{32,0},{64,32},{96,64},{128,96},{160,128},{192,160},{224,192},{256... | collective-permute-start | bytes 983048 | tf_op jit(solution)/shard_map/ppermute | solution.py:21
  27.9 0.0 copy-start.9
  27.9 0.6 copy-done.9
  28.5 0.6 copy-done.10
  29.2 0.4 fusion.49
  29.6 4.9 %collective-permute-done = f32[10,16,512]{2,0,1:T(8,128)S(1)} collective-permute-done((f32[10,16,512]{2,0,1:T(8,128)S(1)}, f32[10,16,512]{2,0,1:T(8,128)S(1)}, u32[]{:S(2)}, u32[]{:S(2)}) %collective-permute-start) | collective-permute-done | bytes 327712 | tf_op jit(solution)/shard_map/ppermute | solution.py:21
  34.5 0.5 convolution_add_fusion.1
  35.0 0.0 copy-start.2
  35.1 0.0 copy-start.4
  35.1 0.0 copy-start.5
  35.1 5.2 %collective-permute-start.1 = (f32[10,6,512]{2,0,1:T(8,128)S(1)}, f32[10,6,512]{2,0,1:T(8,128)S(1)}, u32[]{:S(2)}, u32[]{:S(2)}) collective-permute-start(f32[10,6,512]{2,0,1:T(8,128)S(1)} %slice.66), channel_id=1, source_target_pairs={{1,0},{2,1},{3,2},{4,3},{5,4},{6,5},{7,6},{8,7},{9,8},{10,9},{11,1... | collective-permute-start | bytes 368648 | tf_op jit(solution)/shard_map/ppermute | solution.py:21
  40.3 0.0 copy-done.14
  40.3 3.1 %collective-permute-done.1 = f32[10,6,512]{2,0,1:T(8,128)S(1)} collective-permute-done((f32[10,6,512]{2,0,1:T(8,128)S(1)}, f32[10,6,512]{2,0,1:T(8,128)S(1)}, u32[]{:S(2)}, u32[]{:S(2)}) %collective-permute-start.1) | collective-permute-done | bytes 122912 | tf_op jit(solution)/shard_map/ppermute | solution.py:21
  43.5 0.0 copy-done.3
  43.5 0.0 copy-done.2
  43.5 0.0 copy-done.4
  43.5 0.0 copy-done.5
  43.5 0.6 copy-done.8
  44.1 1.4 %multiply_reduce_fusion = (f32[16,512]{1,0:T(8,128)}, f32[10,16,512]{2,0,1:T(8,128)S(1)}, f32[10,16,512]{2,0,1:T(8,128)S(1)}) fusion(f32[10]{0:T(128)S(1)} %broadcast_multiply_fusion, f32[10,16,512]{2,1,0:T(8,128)S(1)} %copy-done.2, f32[16,512]{1,0:T(8,128)S(1)} %copy-done.5, f32[10,6,512]{2,0,1:T(8,128)S(1)} %collective-permute-done.1, ...), kind=kLoop, calls=%fused_computation.76 | loop fusion | flops 2449408 | bytes 2175116 | tf_op jit(solution)/shard_map/reduce_sum | solution.py:211
  45.5 2.7 %collective-permute-start.2 = (f32[10,6,512]{2,0,1:T(8,128)S(1)}, f32[10,6,512]{2,0,1:T(8,128)S(1)}, u32[]{:S(2)}, u32[]{:S(2)}) collective-permute-start(f32[10,6,512]{2,0,1:T(8,128)S(1)} %slice.77), channel_id=1, source_target_pairs={{0,1},{1,2},{2,3},{3,4},{4,5},{5,6},{6,7},{7,8},{8,9},{9,10},{10,1... | collective-permute-start | bytes 368648 | tf_op jit(solution)/shard_map/ppermute | solution.py:21
  48.2 7.5 %collective-permute-done.2 = f32[10,6,512]{2,0,1:T(8,128)S(1)} collective-permute-done((f32[10,6,512]{2,0,1:T(8,128)S(1)}, f32[10,6,512]{2,0,1:T(8,128)S(1)}, u32[]{:S(2)}, u32[]{:S(2)}) %collective-permute-start.2) | collective-permute-done | bytes 122912 | tf_op jit(solution)/shard_map/ppermute | solution.py:21
  55.6 0.3 fusion.12
  55.9 0.4 fusion.51
  56.3 9.9 %collective-permute-start.3 = (f32[10,16,512]{2,0,1:T(8,128)S(1)}, f32[10,16,512]{2,0,1:T(8,128)S(1)}, u32[]{:S(2)}, u32[]{:S(2)}) collective-permute-start(f32[10,16,512]{2,0,1:T(8,128)S(1)} %fusion.51), channel_id=1, source_target_pairs={{0,32},{32,64},{64,96},{96,128},{128,160},{160,192},{192,224},{224... | collective-permute-start | bytes 983048 | tf_op jit(solution)/shard_map/ppermute | solution.py:21
  66.2 17.7 %shard_map.158 = f32[16,512]{1,0:T(8,128)} custom-call(f32[16,512]{1,0:T(8,128)} %get-tuple-element.8.x_ref), custom_call_target="tpu_custom_call" | custom-call | tf_op jit(solution)/shard_map/pallas_call | solution.py:124
  83.9 0.0 copy-start.6
  83.9 0.0 copy-start.7
  83.9 0.0 copy-start.1
  83.9 0.9 copy.26
  84.9 0.0 copy-done.6
  84.9 0.0 copy-done.7
  84.9 0.6 add_minimum_fusion
  85.5 0.0 collective-permute-done.3
  85.5 0.0 copy-done.1
  85.5 0.6 fusion.1
  86.1 0.0 copy-start
  86.1 2.7 %fusion.63 = f32[10,16,512]{2,0,1:T(8,128)S(1)} fusion(f32[10,16,512]{2,0,1:T(8,128)S(1)} %fusion.1), kind=kOutput, calls=%fused_computation.105 | output fusion | flops 1228800 | bytes 655360 | tf_op jit(solution)/shard_map/jit(cumsum)/reduce_window_sum | solution.py:257
  88.8 0.6 slice_bitcast_fusion.x_ref
  89.4 20.7 %shard_map.157 = f32[10,512]{1,0:T(8,128)} custom-call(f32[10,512]{1,0:T(8,128)} %slice_bitcast_fusion.x_ref), custom_call_target="tpu_custom_call" | custom-call | tf_op jit(solution)/shard_map/pallas_call | solution.py:124
  110.1 0.0 copy-done
  110.2 1.1 minimum_subtract_fusion
  111.3 0.9 copy.28
  112.2 0.9 copy.27
  (15 shorter events, 0.1 us)
Async XLA Ops:
  25.9 8.6 %collective-permute-start = (f32[10,16,512]{2,0,1:T(8,128)S(1)}, f32[10,16,512]{2,0,1:T(8,128)S(1)}, u32[]{:S(2)}, u32[]{:S(2)}) collective-permute-start(f32[10,16,512]{2,0,1:T(8,128)S(1)} %reverse_add_fusion), channel_id=1, source_target_pairs={{32,0},{64,32},{96,64},{128,96},{160,128},{192,160},{224,192},{256... | collective-permute-start | bytes 983048 | tf_op jit(solution)/shard_map/ppermute | solution.py:21
  27.9 0.7 copy-start.9
  28.5 0.7 copy-start.10
  34.5 5.8 %copy-start.14 = (f32[10]{0:T(128)S(1)}, f32[10]{0:T(128)}, u32[]{:S(2)}) copy-start(f32[10]{0:T(128)} %param.23) | copy-start | bytes 124
  34.5 8.9 %copy-start.3 = (f32[10,16,512]{2,1,0:T(8,128)S(1)}, f32[10,16,512]{2,1,0:T(8,128)}, u32[]{:S(2)}) copy-start(f32[10,16,512]{2,1,0:T(8,128)} %param.16) | copy-start | bytes 983044
  35.0 8.4 %copy-start.2 = (f32[10,16,512]{2,1,0:T(8,128)S(1)}, f32[10,16,512]{2,1,0:T(8,128)}, u32[]{:S(2)}) copy-start(f32[10,16,512]{2,1,0:T(8,128)} %param.13) | copy-start | bytes 983044
  35.1 8.4 %copy-start.4 = (f32[10,512]{1,0:T(8,128)S(1)}, f32[10,512]{1,0:T(8,128)}, u32[]{:S(2)}) copy-start(f32[10,512]{1,0:T(8,128)} %shard_map.156) | copy-start | bytes 61444
  35.1 8.4 %copy-start.5 = (f32[16,512]{1,0:T(8,128)S(1)}, f32[16,512]{1,0:T(8,128)}, u32[]{:S(2)}) copy-start(f32[16,512]{1,0:T(8,128)} %param.15) | copy-start | bytes 98308
  35.1 8.4 %collective-permute-start.1 = (f32[10,6,512]{2,0,1:T(8,128)S(1)}, f32[10,6,512]{2,0,1:T(8,128)S(1)}, u32[]{:S(2)}, u32[]{:S(2)}) collective-permute-start(f32[10,6,512]{2,0,1:T(8,128)S(1)} %slice.66), channel_id=1, source_target_pairs={{1,0},{2,1},{3,2},{4,3},{5,4},{6,5},{7,6},{8,7},{9,8},{10,9},{11,1... | collective-permute-start | bytes 368648 | tf_op jit(solution)/shard_map/ppermute | solution.py:21
  43.5 0.7 copy-start.8
  45.5 10.1 %collective-permute-start.2 = (f32[10,6,512]{2,0,1:T(8,128)S(1)}, f32[10,6,512]{2,0,1:T(8,128)S(1)}, u32[]{:S(2)}, u32[]{:S(2)}) collective-permute-start(f32[10,6,512]{2,0,1:T(8,128)S(1)} %slice.77), channel_id=1, source_target_pairs={{0,1},{1,2},{2,3},{3,4},{4,5},{5,6},{6,7},{7,8},{8,9},{9,10},{10,1... | collective-permute-start | bytes 368648 | tf_op jit(solution)/shard_map/ppermute | solution.py:21
  56.3 29.1 %collective-permute-start.3 = (f32[10,16,512]{2,0,1:T(8,128)S(1)}, f32[10,16,512]{2,0,1:T(8,128)S(1)}, u32[]{:S(2)}, u32[]{:S(2)}) collective-permute-start(f32[10,16,512]{2,0,1:T(8,128)S(1)} %fusion.51), channel_id=1, source_target_pairs={{0,32},{32,64},{64,96},{96,128},{128,160},{160,192},{192,224},{224... | collective-permute-start | bytes 983048 | tf_op jit(solution)/shard_map/ppermute | solution.py:21
  83.9 1.0 copy-start.6
  83.9 0.9 copy-start.7
  83.9 1.6 %copy-start.1 = (f32[10,16,512]{2,1,0:T(8,128)S(1)}, f32[10,16,512]{2,1,0:T(8,128)}, u32[]{:S(2)}) copy-start(f32[10,16,512]{2,1,0:T(8,128)} %param.17) | copy-start | bytes 983044
  86.1 24.1 %copy-start = (f32[10,16,512]{2,1,0:T(8,128)S(1)}, f32[10,16,512]{2,1,0:T(8,128)}, u32[]{:S(2)}) copy-start(f32[10,16,512]{2,1,0:T(8,128)} %param.14) | copy-start | bytes 983044
  89.4 20.7 %copy-start.11 = (f32[10]{0:T(128)S(1)}, f32[10]{0:T(128)}, u32[]{:S(2)}) copy-start(f32[10]{0:T(128)} %param.20) | copy-start | bytes 124
  89.4 20.7 %copy-start.12 = (f32[10]{0:T(128)S(1)}, f32[10]{0:T(128)}, u32[]{:S(2)}) copy-start(f32[10]{0:T(128)} %param.21) | copy-start | bytes 124
  89.4 20.7 %copy-start.13 = (f32[10]{0:T(128)S(1)}, f32[10]{0:T(128)}, u32[]{:S(2)}) copy-start(f32[10]{0:T(128)} %param.19) | copy-start | bytes 124

commit v3 on v0

--- a/solution.py
+++ b/solution.py
@@ -1,8 +1,11 @@
+import functools
 import math
 
 import jax
 import jax.numpy as jnp
 from jax import lax
+from jax.experimental import pallas as pl
+from jax.experimental.pallas import tpu as pltpu
 from jax.sharding import PartitionSpec as P
 
 DMAX = 6
@@ -18,18 +21,138 @@
     return lax.ppermute(block, axis, route)
 
 
-def prefix(part, axis, combine, identity, reverse):
-    count = lax.axis_size(axis)
-    place = lax.axis_index(axis)
-    ahead = count - 1 - place if reverse else place
-    gathered = lax.all_gather(part, axis)
-    state = jnp.zeros_like(part) + jnp.asarray(identity, part.dtype)
-
-    def one(turn, state):
-        source = count - 1 - turn if reverse else turn
-        return combine(state, lax.dynamic_index_in_dim(gathered, source, 0, False))
-
-    return lax.fori_loop(0, ahead, one, state)
+MESH = pl.DeviceIdType.MESH
+
+
+def wanted(mode, src, dst):
+    if mode == "prefix":
+        return src < dst
+    if mode == "suffix":
+        return src > dst
+    return src != dst
+
+
+class Job:
+    def __init__(self, axis, mode, inner, n):
+        self.axis, self.mode, self.inner = axis, mode, inner
+        self.outer = n // inner
+        self.other = "river" if axis == "hours" else "hours"
+
+    def place(self):
+        me = lax.axis_index(self.axis)
+        self.fixed = lax.axis_index(self.other)
+        self.o = me // self.inner
+        self.i = me % self.inner
+
+    def device(self, p):
+        return (self.fixed, p) if self.axis == "hours" else (p, self.fixed)
+
+    def peers(self):
+        inner, outer, o, i = self.inner, self.outer, self.o, self.i
+        near = [self.device(o * inner + lax.rem(i + s, inner)) for s in range(1, inner)]
+        far = [self.device(lax.rem(o + s, outer) * inner + i) for s in range(1, outer)]
+        return near + far
+
+
+def multi_kernel(jobs, *refs):
+    count = len(jobs)
+    ins, outs, rest = refs[:count], refs[count:2 * count], refs[2 * count:]
+    for job in jobs:
+        job.place()
+    barrier = pltpu.get_barrier_semaphore()
+    partners = 0
+    for job in jobs:
+        for dev in job.peers():
+            pl.semaphore_signal(barrier, 1, device_id=dev, device_id_type=MESH)
+            partners += 1
+    pl.semaphore_wait(barrier, partners)
+
+    def across(job, x_ref, near, s1, r1, p, landing):
+        return pltpu.make_async_remote_copy(
+            src_ref=x_ref, dst_ref=near.at[landing], send_sem=s1.at[p], recv_sem=r1.at[landing],
+            device_id=job.device(job.o * job.inner + p), device_id_type=MESH)
+
+    for k, job in enumerate(jobs):
+        near, far, group, s1, r1, s2, r2 = rest[7 * k:7 * k + 7]
+        for s in range(1, job.inner):
+            p = lax.rem(job.i + s, job.inner)
+            across(job, ins[k], near, s1, r1, p, job.i).start()
+    parts = []
+    for k, job in enumerate(jobs):
+        near, far, group, s1, r1, s2, r2 = rest[7 * k:7 * k + 7]
+        for s in range(1, job.inner):
+            p = lax.rem(job.i + s, job.inner)
+            across(job, ins[k], near, s1, r1, p, job.i).wait_send()
+            across(job, ins[k], near, s1, r1, p, p).wait_recv()
+        own = ins[k][...]
+        total = own
+        part = own if job.mode == "sum" else jnp.zeros_like(own)
+        for s in range(1, job.inner):
+            p = lax.rem(job.i + s, job.inner)
+            block = near[p]
+            total = total + block
+            if job.mode == "sum":
+                part = part + block
+            else:
+                part = part + jnp.where(wanted(job.mode, p, job.i), block, 0.0)
+        group[...] = total
+        parts.append(part)
+
+    def up(job, group, far, s2, r2, q, landing):
+        return pltpu.make_async_remote_copy(
+            src_ref=group, dst_ref=far.at[landing], send_sem=s2.at[q], recv_sem=r2.at[landing],
+            device_id=job.device(q * job.inner + job.i), device_id_type=MESH)
+
+    for k, job in enumerate(jobs):
+        near, far, group, s1, r1, s2, r2 = rest[7 * k:7 * k + 7]
+        for s in range(1, job.outer):
+            q = lax.rem(job.o + s, job.outer)
+
+            @pl.when(wanted(job.mode, job.o, q))
+            def _():
+                up(job, group, far, s2, r2, q, job.o).start()
+
+    for k, job in enumerate(jobs):
+        near, far, group, s1, r1, s2, r2 = rest[7 * k:7 * k + 7]
+        part = parts[k]
+        for s in range(1, job.outer):
+            q = lax.rem(job.o + s, job.outer)
+
+            @pl.when(wanted(job.mode, job.o, q))
+            def _():
+                up(job, group, far, s2, r2, q, job.o).wait_send()
+
+            @pl.when(wanted(job.mode, q, job.o))
+            def _():
+                up(job, group, far, s2, r2, q, q).wait_recv()
+
+        for s in range(1, job.outer):
+            q = lax.rem(job.o + s, job.outer)
+            part = part + jnp.where(wanted(job.mode, q, job.o), far[q], 0.0)
+        outs[k][...] = part
+
+
+def combine(parts, specs, collective):
+    jobs = [Job(axis, mode, inner, lax.axis_size(axis)) for axis, mode, inner in specs]
+    scratch = []
+    for part, job in zip(parts, jobs):
+        scratch += [
+            pltpu.VMEM((job.inner,) + part.shape, part.dtype),
+            pltpu.VMEM((job.outer,) + part.shape, part.dtype),
+            pltpu.VMEM(part.shape, part.dtype),
+            pltpu.SemaphoreType.DMA((job.inner,)),
+            pltpu.SemaphoreType.DMA((job.inner,)),
+            pltpu.SemaphoreType.DMA((job.outer,)),
+            pltpu.SemaphoreType.DMA((job.outer,)),
+        ]
+    return pl.pallas_call(
+        functools.partial(multi_kernel, jobs),
+        out_shape=[jax.ShapeDtypeStruct(part.shape, part.dtype) for part in parts],
+        in_specs=[pl.BlockSpec(memory_space=pltpu.VMEM)] * len(parts),
+        out_specs=[pl.BlockSpec(memory_space=pltpu.VMEM)] * len(parts),
+        scratch_shapes=scratch,
+        compiler_params=pltpu.CompilerParams(collective_id=collective, has_side_effects=True),
+    )(*parts)
 
 
 def add_pair(earlier_part, later_part):
@@ -64,7 +187,7 @@
     return jnp.einsum("ij,itw->jtw", matrix, field, precision=lax.Precision.HIGHEST)
 
 
-def iterate(fields, statics, scales, prefix_sum, suffix_sum, from_earlier, from_later):
+def iterate(fields, statics, scales, suffix_sum, from_earlier, from_later):
     release, storage_dual, demand_dual, cost, inflow, demand = fields
     (
         storage_start,
@@ -92,7 +215,12 @@
     delayed = hold_back(extrapolated, travel_delay, from_earlier(extrapolated[:, length - DMAX :]))
     incoming = passed_along(route_down(to_next, delayed), "river", 1)
     routed = route_down(to_own, delayed) + incoming
-    storage = storage_start[:, None, None] + scale_time * prefix_sum(inflow + routed - extrapolated)
+    local_sum = jnp.cumsum(inflow + routed - extrapolated, 1)
+    partial_power = jnp.sum(scale_sum * efficiency[:, None, None] * extrapolated, 0)
+    offset, supplied = combine(
+        [local_sum[:, -1], partial_power], [("hours", "prefix", 8), ("river", "sum", 8)], 1
+    )
+    storage = storage_start[:, None, None] + scale_time * (local_sum + offset[:, None])
     lower_bound = storage_low[:, None, None]
     upper_bound = storage_high[:, None, None]
     storage_dual_new = (
@@ -101,8 +229,6 @@
         - dual_step * jnp.clip(storage_dual / dual_step + storage, lower_bound, upper_bound)
     )
     storage_excess = storage - jnp.clip(storage, lower_bound, upper_bound)
-    partial_power = jnp.sum(scale_sum * efficiency[:, None, None] * extrapolated, 0)
-    supplied = lax.psum(partial_power, "river")
     demand_dual_new = jnp.minimum(demand_dual + dual_step * (supplied - demand), 0.0)
     return (release_new, storage_dual_new, demand_dual_new, storage_excess)
 
@@ -146,16 +272,10 @@
     )
     scales = (scale_time, scale_sum)
 
-    def prefix_blocks(field):
-        local_sum = jnp.cumsum(field, 1)
-        totals = local_sum[:, -1]
-        offset = prefix(totals, "hours", add_pair, jnp.zeros_like(totals), False)
-        return local_sum + offset[:, None]
-
     def suffix_blocks(field):
         local_sum = suffix_local(field)
         totals = local_sum[:, 0]
-        offset = prefix(totals, "hours", add_pair, jnp.zeros_like(totals), True)
+        (offset,) = combine([totals], [("hours", "suffix", 8)], 0)
         return local_sum + offset[:, None]
 
     def earlier_block(part):
@@ -166,7 +286,7 @@
 
     fields = (release, storage_dual, demand_dual, cost, inflow, demand)
     return iterate(
-        fields, statics, scales, prefix_blocks, suffix_blocks, earlier_block, later_block
+        fields, statics, scales, suffix_blocks, earlier_block, later_block
     )
 
 

time: 301 us -> 113 us (0.38)
  the two profiles are of different devices: /device:TPU:32 before, /device:TPU:8 now
where the time goes in v3:
time: 113 us
  Pallas kernels  67.7 us (60%)
  starting transfers between devices  15 us (13%)
  waiting for transfers between devices  11.4 us (10%)
  local copies, waits for them, and re-layouts  8.5 us (8%)
  other arithmetic  7.3 us (6%)
  matrix products  1.9 us (2%)
    pallas_call x2, Pallas kernels, combine(): pl.pallas_call(functools.partial(multi_kernel, jobs), out_shape=[jax.Shap...  67.7 us
    ppermute x4, starting transfers between devices, passed_along(): return lax.ppermute(block, axis, route)  15 us
    ppermute x4, waiting for transfers between devices, passed_along(): return lax.ppermute(block, axis, route)  11.4 us
    unnamed x33, local copies, waits for them, and re-layouts  5.39 us
    another operation x1, other arithmetic, iterate(): local_sum = jnp.cumsum(inflow + routed - extrapolated, 1)  2.71 us
  transfers between devices with their start and end apart: 4, of which 4 were waited for; matrix products, arithmetic and copies ran while one was open for 1% of the time, Pallas kernels for 0%

profile of v3, /device:TPU:8, one launch (start us, length us, event | category | flops | bytes accessed | tf_op | source)
XLA Modules:
  0.0 112.7 jit_solution(4390541412140656083)
XLA Ops:
  0.6 1.8 %rev.7 = f32[10,16,512]{2,1,0:T(8,128)S(1)} reverse(f32[10,16,512]{2,1,0:T(8,128)} %param.14), dimensions={1} | reverse | bytes 655360 | tf_op jit(solution)/shard_map/jit(_flip)/rev | solution.py:237
  2.5 0.4 fusion.45
  2.9 0.6 slice_bitcast_fusion.1.refs_0_
  3.5 24.2 %shard_map.156 = f32[10,512]{1,0:T(8,128)} custom-call(f32[10,512]{1,0:T(8,128)} %slice_bitcast_fusion.1.refs_0_), custom_call_target="tpu_custom_call" | custom-call | tf_op jit(solution)/shard_map/pallas_call | solution.py:148
  27.7 0.8 reverse_add_fusion
  28.5 1.3 %collective-permute-start = (f32[10,16,512]{2,0,1:T(8,128)S(1)}, f32[10,16,512]{2,0,1:T(8,128)S(1)}, u32[]{:S(2)}, u32[]{:S(2)}) collective-permute-start(f32[10,16,512]{2,0,1:T(8,128)S(1)} %reverse_add_fusion), channel_id=1, source_target_pairs={{32,0},{64,32},{96,64},{128,96},{160,128},{192,160},{224,192},{256... | collective-permute-start | bytes 983048 | tf_op jit(solution)/shard_map/ppermute | solution.py:21
  29.8 0.0 copy-start.9
  29.9 0.6 copy-done.9
  30.5 0.6 copy-done.10
  31.2 0.4 fusion.49
  31.6 0.8 collective-permute-done
  32.3 0.5 convolution_add_fusion.1
  32.8 0.0 copy-start.2
  32.9 0.0 copy-start.4
  32.9 0.0 copy-start.5
  32.9 3.9 %collective-permute-start.1 = (f32[10,6,512]{2,0,1:T(8,128)S(1)}, f32[10,6,512]{2,0,1:T(8,128)S(1)}, u32[]{:S(2)}, u32[]{:S(2)}) collective-permute-start(f32[10,6,512]{2,0,1:T(8,128)S(1)} %slice.66), channel_id=1, source_target_pairs={{1,0},{2,1},{3,2},{4,3},{5,4},{6,5},{7,6},{8,7},{9,8},{10,9},{11,1... | collective-permute-start | bytes 368648 | tf_op jit(solution)/shard_map/ppermute | solution.py:21
  36.8 0.0 copy-done.14
  36.8 3.8 %collective-permute-done.1 = f32[10,6,512]{2,0,1:T(8,128)S(1)} collective-permute-done((f32[10,6,512]{2,0,1:T(8,128)S(1)}, f32[10,6,512]{2,0,1:T(8,128)S(1)}, u32[]{:S(2)}, u32[]{:S(2)}) %collective-permute-start.1) | collective-permute-done | bytes 122912 | tf_op jit(solution)/shard_map/ppermute | solution.py:21
  40.6 0.0 copy-done.3
  40.6 0.0 copy-done.2
  40.6 0.0 copy-done.4
  40.6 0.0 copy-done.5
  40.6 0.6 copy-done.8
  41.3 1.4 %multiply_reduce_fusion = (f32[16,512]{1,0:T(8,128)}, f32[10,16,512]{2,0,1:T(8,128)S(1)}, f32[10,16,512]{2,0,1:T(8,128)S(1)}) fusion(f32[10]{0:T(128)S(1)} %broadcast_multiply_fusion, f32[10,16,512]{2,1,0:T(8,128)S(1)} %copy-done.2, f32[16,512]{1,0:T(8,128)S(1)} %copy-done.5, f32[10,6,512]{2,0,1:T(8,128)S(1)} %collective-permute-done.1, ...), kind=kLoop, calls=%fused_computation.77 | loop fusion | flops 2449408 | bytes 2175116 | tf_op jit(solution)/shard_map/reduce_sum | solution.py:219
  42.6 3.3 %collective-permute-start.2 = (f32[10,6,512]{2,0,1:T(8,128)S(1)}, f32[10,6,512]{2,0,1:T(8,128)S(1)}, u32[]{:S(2)}, u32[]{:S(2)}) collective-permute-start(f32[10,6,512]{2,0,1:T(8,128)S(1)} %slice.77), channel_id=1, source_target_pairs={{0,1},{1,2},{2,3},{3,4},{4,5},{5,6},{6,7},{7,8},{8,9},{9,10},{10,1... | collective-permute-start | bytes 368648 | tf_op jit(solution)/shard_map/ppermute | solution.py:21
  46.0 6.3 %collective-permute-done.2 = f32[10,6,512]{2,0,1:T(8,128)S(1)} collective-permute-done((f32[10,6,512]{2,0,1:T(8,128)S(1)}, f32[10,6,512]{2,0,1:T(8,128)S(1)}, u32[]{:S(2)}, u32[]{:S(2)}) %collective-permute-start.2) | collective-permute-done | bytes 122912 | tf_op jit(solution)/shard_map/ppermute | solution.py:21
  52.3 0.3 fusion.12
  52.6 0.4 fusion.51
  53.0 6.5 %collective-permute-start.3 = (f32[10,16,512]{2,0,1:T(8,128)S(1)}, f32[10,16,512]{2,0,1:T(8,128)S(1)}, u32[]{:S(2)}, u32[]{:S(2)}) collective-permute-start(f32[10,16,512]{2,0,1:T(8,128)S(1)} %fusion.51), channel_id=1, source_target_pairs={{0,32},{32,64},{64,96},{96,128},{128,160},{160,192},{192,224},{224... | collective-permute-start | bytes 983048 | tf_op jit(solution)/shard_map/ppermute | solution.py:21
  59.5 0.0 copy-start.1
  59.5 0.9 copy.26
  60.4 0.6 collective-permute-done.3
  61.0 0.6 fusion.1
  61.6 0.0 copy-start
  61.6 2.7 %fusion.63 = f32[10,16,512]{2,0,1:T(8,128)S(1)} fusion(f32[10,16,512]{2,0,1:T(8,128)S(1)} %fusion.1), kind=kOutput, calls=%fused_computation.105 | output fusion | flops 1228800 | bytes 655360 | tf_op jit(solution)/shard_map/jit(cumsum)/reduce_window_sum | solution.py:218
  64.3 0.6 slice_bitcast_fusion.refs_0_
  64.9 43.5 %shard_map.157 = (f32[10,512]{1,0:T(8,128)}, f32[16,512]{1,0:T(8,128)}) custom-call(f32[10,512]{1,0:T(8,128)} %slice_bitcast_fusion.refs_0_, f32[16,512]{1,0:T(8,128)} %get-tuple-element.12.refs_1_), custom_call_target="tpu_custom_call" | custom-call | tf_op jit(solution)/shard_map/pallas_call | solution.py:148
  108.4 0.0 copy-start.11
  108.4 0.0 copy-start.12
  108.5 0.0 copy-start.13
  108.5 0.0 copy-done
  108.5 0.6 copy-done.11
  109.1 0.0 copy-done.12
  109.1 0.0 copy-done.13
  109.1 1.1 minimum_subtract_fusion
  110.3 0.9 copy.28
  111.2 0.9 copy.27
  112.1 0.6 add_minimum_fusion
  (14 shorter events, 0.1 us)
Async XLA Ops:
  28.5 3.8 %collective-permute-start = (f32[10,16,512]{2,0,1:T(8,128)S(1)}, f32[10,16,512]{2,0,1:T(8,128)S(1)}, u32[]{:S(2)}, u32[]{:S(2)}) collective-permute-start(f32[10,16,512]{2,0,1:T(8,128)S(1)} %reverse_add_fusion), channel_id=1, source_target_pairs={{32,0},{64,32},{96,64},{128,96},{160,128},{192,160},{224,192},{256... | collective-permute-start | bytes 983048 | tf_op jit(solution)/shard_map/ppermute | solution.py:21
  29.8 0.7 copy-start.9
  30.5 0.7 copy-start.10
  32.3 4.5 %copy-start.14 = (f32[10]{0:T(128)S(1)}, f32[10]{0:T(128)}, u32[]{:S(2)}) copy-start(f32[10]{0:T(128)} %param.23) | copy-start | bytes 124
  32.3 8.3 %copy-start.3 = (f32[10,16,512]{2,1,0:T(8,128)S(1)}, f32[10,16,512]{2,1,0:T(8,128)}, u32[]{:S(2)}) copy-start(f32[10,16,512]{2,1,0:T(8,128)} %param.16) | copy-start | bytes 983044
  32.8 7.8 %copy-start.2 = (f32[10,16,512]{2,1,0:T(8,128)S(1)}, f32[10,16,512]{2,1,0:T(8,128)}, u32[]{:S(2)}) copy-start(f32[10,16,512]{2,1,0:T(8,128)} %param.13) | copy-start | bytes 983044
  32.9 7.8 %copy-start.4 = (f32[10,512]{1,0:T(8,128)S(1)}, f32[10,512]{1,0:T(8,128)}, u32[]{:S(2)}) copy-start(f32[10,512]{1,0:T(8,128)} %shard_map.156) | copy-start | bytes 61444
  32.9 7.7 %copy-start.5 = (f32[16,512]{1,0:T(8,128)S(1)}, f32[16,512]{1,0:T(8,128)}, u32[]{:S(2)}) copy-start(f32[16,512]{1,0:T(8,128)} %param.15) | copy-start | bytes 98308
  32.9 7.7 %collective-permute-start.1 = (f32[10,6,512]{2,0,1:T(8,128)S(1)}, f32[10,6,512]{2,0,1:T(8,128)S(1)}, u32[]{:S(2)}, u32[]{:S(2)}) collective-permute-start(f32[10,6,512]{2,0,1:T(8,128)S(1)} %slice.66), channel_id=1, source_target_pairs={{1,0},{2,1},{3,2},{4,3},{5,4},{6,5},{7,6},{8,7},{9,8},{10,9},{11,1... | collective-permute-start | bytes 368648 | tf_op jit(solution)/shard_map/ppermute | solution.py:21
  40.6 0.7 copy-start.8
  42.6 9.7 %collective-permute-start.2 = (f32[10,6,512]{2,0,1:T(8,128)S(1)}, f32[10,6,512]{2,0,1:T(8,128)S(1)}, u32[]{:S(2)}, u32[]{:S(2)}) collective-permute-start(f32[10,6,512]{2,0,1:T(8,128)S(1)} %slice.77), channel_id=1, source_target_pairs={{0,1},{1,2},{2,3},{3,4},{4,5},{5,6},{6,7},{7,8},{8,9},{9,10},{10,1... | collective-permute-start | bytes 368648 | tf_op jit(solution)/shard_map/ppermute | solution.py:21
  53.0 8.0 %collective-permute-start.3 = (f32[10,16,512]{2,0,1:T(8,128)S(1)}, f32[10,16,512]{2,0,1:T(8,128)S(1)}, u32[]{:S(2)}, u32[]{:S(2)}) collective-permute-start(f32[10,16,512]{2,0,1:T(8,128)S(1)} %fusion.51), channel_id=1, source_target_pairs={{0,32},{32,64},{64,96},{96,128},{128,160},{160,192},{192,224},{224... | collective-permute-start | bytes 983048 | tf_op jit(solution)/shard_map/ppermute | solution.py:21
  59.5 1.5 %copy-start.1 = (f32[10,16,512]{2,1,0:T(8,128)S(1)}, f32[10,16,512]{2,1,0:T(8,128)}, u32[]{:S(2)}) copy-start(f32[10,16,512]{2,1,0:T(8,128)} %param.17) | copy-start | bytes 983044
  61.6 46.9 %copy-start = (f32[10,16,512]{2,1,0:T(8,128)S(1)}, f32[10,16,512]{2,1,0:T(8,128)}, u32[]{:S(2)}) copy-start(f32[10,16,512]{2,1,0:T(8,128)} %param.14) | copy-start | bytes 983044
  108.4 0.7 copy-start.11
  108.4 0.7 copy-start.12
  108.5 0.7 copy-start.13
  111.2 0.9 copy-start.6
  111.2 0.9 copy-start.7

commit v4 on v3

--- a/solution.py
+++ b/solution.py
@@ -133,6 +133,8 @@
 
 
 def combine(parts, specs, collective):
+    shapes = [part.shape for part in parts]
+    parts = [part.reshape(-1, 128) for part in parts]
     jobs = [Job(axis, mode, inner, lax.axis_size(axis)) for axis, mode, inner in specs]
     scratch = []
     for part, job in zip(parts, jobs):
@@ -145,7 +147,7 @@
             pltpu.SemaphoreType.DMA((job.outer,)),
             pltpu.SemaphoreType.DMA((job.outer,)),
         ]
-    return pl.pallas_call(
+    results = pl.pallas_call(
         functools.partial(multi_kernel, jobs),
         out_shape=[jax.ShapeDtypeStruct(part.shape, part.dtype) for part in parts],
         in_specs=[pl.BlockSpec(memory_space=pltpu.VMEM)] * len(parts),
@@ -153,6 +155,7 @@
         scratch_shapes=scratch,
         compiler_params=pltpu.CompilerParams(collective_id=collective, has_side_effects=True),
     )(*parts)
+    return [result.reshape(shape) for result, shape in zip(results, shapes)]
 
 
 def add_pair(earlier_part, later_part):

time: 113 us -> 110 us (0.973)
  Pallas kernels: 67.7 us -> 64.5 us
  other arithmetic: 7.3 us -> 5.17 us
  local copies, waits for them, and re-layouts: 8.5 us -> 10.6 us
    pallas_call x2, Pallas kernels: 67.7 us -> 64.5 us  [combine(): pl.pallas_call(functools.partial(multi_kernel, jobs), out_shape=[jax.Shap...]
    add x0 -> x2, local copies, waits for them, and re-layouts: none -> 1.47 us  [the longest x1 0.74 us: iterate(): local_sum + offset[:, None]]
    squeeze x2 -> x0, local copies, waits for them, and re-layouts: 1.24 us -> none  [the longest x1 0.62 us: suffix_blocks(): totals = local_sum[:, 0]]
    another operation x0 -> x2, local copies, waits for them, and re-layouts: none -> 1.22 us  [combine(): parts = [part.reshape(-1, 128) for part in parts]]
    unnamed x33 -> x31, local copies, waits for them, and re-layouts: 5.39 us -> 5.45 us
  transfers between devices with their start and end apart: 4 -> 4, of which waited for: 4 -> 3; matrix products, arithmetic and copies ran while one was open for 1% -> 2% of each run, Pallas kernels for 0% -> 0%
where the time goes in v4:
time: 110 us; the launch traced here: 109 us
  Pallas kernels  64.5 us (59%)
  starting transfers between devices  15.2 us (14%)
  waiting for transfers between devices  11.2 us (10%)
  local copies, waits for them, and re-layouts  10.6 us (10%)
  other arithmetic  5.17 us (5%)
  matrix products  1.89 us (2%)
    pallas_call x2, Pallas kernels, combine(): pl.pallas_call(functools.partial(multi_kernel, jobs), out_shape=[jax.Shap...  64.5 us
    ppermute x4, starting transfers between devices, passed_along(): return lax.ppermute(block, axis, route)  15.2 us
    ppermute x4, waiting for transfers between devices, passed_along(): return lax.ppermute(block, axis, route)  11.2 us
    unnamed x31, local copies, waits for them, and re-layouts  5.45 us
    another operation x1, other arithmetic, iterate(): local_sum = jnp.cumsum(inflow + routed - extrapolated, 1)  2.71 us
  transfers between devices with their start and end apart: 4, of which 3 were waited for; matrix products, arithmetic and copies ran while one was open for 2% of the time, Pallas kernels for 0%

profile of v4, /device:TPU:8, one launch (start us, length us, event | category | flops | bytes accessed | tf_op | source)
XLA Modules:
  0.0 109.5 jit_solution(144646827894611672)
XLA Ops:
  0.6 1.8 %rev.7 = f32[10,16,512]{2,1,0:T(8,128)S(1)} reverse(f32[10,16,512]{2,1,0:T(8,128)} %param.14), dimensions={1} | reverse | bytes 655360 | tf_op jit(solution)/shard_map/jit(_flip)/rev | solution.py:240
  2.5 0.4 fusion.45
  2.9 0.6 reshape_squeeze.6.refs_0_
  3.5 22.5 %shard_map.156 = f32[40,128]{1,0:T(8,128)} custom-call(f32[40,128]{1,0:T(8,128)} %reshape_squeeze.6.refs_0_), custom_call_target="tpu_custom_call" | custom-call | tf_op jit(solution)/shard_map/pallas_call | solution.py:150
  25.9 0.7 add.90
  26.7 1.3 %collective-permute-start = (f32[10,16,512]{2,0,1:T(8,128)S(1)}, f32[10,16,512]{2,0,1:T(8,128)S(1)}, u32[]{:S(2)}, u32[]{:S(2)}) collective-permute-start(f32[10,16,512]{2,0,1:T(8,128)S(1)} %reverse_add_fusion), channel_id=1, source_target_pairs={{32,0},{64,32},{96,64},{128,96},{160,128},{192,160},{224,192},{256... | collective-permute-start | bytes 983048 | tf_op jit(solution)/shard_map/ppermute | solution.py:21
  28.0 0.0 copy-start.8
  28.0 0.6 copy-done.8
  28.7 0.6 copy-done.9
  29.4 0.4 fusion.49
  29.8 0.8 collective-permute-done
  30.5 0.5 convolution_add_fusion.1
  31.0 0.0 copy-start.13
  31.0 0.0 copy-start.2
  31.1 0.0 copy-start.4
  31.1 4.5 %collective-permute-start.1 = (f32[10,6,512]{2,0,1:T(8,128)S(1)}, f32[10,6,512]{2,0,1:T(8,128)S(1)}, u32[]{:S(2)}, u32[]{:S(2)}) collective-permute-start(f32[10,6,512]{2,0,1:T(8,128)S(1)} %slice.66), channel_id=1, source_target_pairs={{1,0},{2,1},{3,2},{4,3},{5,4},{6,5},{7,6},{8,7},{9,8},{10,9},{11,1... | collective-permute-start | bytes 368648 | tf_op jit(solution)/shard_map/ppermute | solution.py:21
  35.6 0.0 copy-done.13
  35.6 3.1 %collective-permute-done.1 = f32[10,6,512]{2,0,1:T(8,128)S(1)} collective-permute-done((f32[10,6,512]{2,0,1:T(8,128)S(1)}, f32[10,6,512]{2,0,1:T(8,128)S(1)}, u32[]{:S(2)}, u32[]{:S(2)}) %collective-permute-start.1) | collective-permute-done | bytes 122912 | tf_op jit(solution)/shard_map/ppermute | solution.py:21
  38.8 0.0 copy-done.3
  38.8 0.0 copy-done.2
  38.8 0.0 copy-done.4
  38.8 0.6 copy-done.7
  39.5 0.8 multiply_reduce_fusion
  40.2 2.9 %collective-permute-start.2 = (f32[10,6,512]{2,0,1:T(8,128)S(1)}, f32[10,6,512]{2,0,1:T(8,128)S(1)}, u32[]{:S(2)}, u32[]{:S(2)}) collective-permute-start(f32[10,6,512]{2,0,1:T(8,128)S(1)} %slice.77), channel_id=1, source_target_pairs={{0,1},{1,2},{2,3},{3,4},{4,5},{5,6},{6,7},{7,8},{8,9},{9,10},{10,1... | collective-permute-start | bytes 368648 | tf_op jit(solution)/shard_map/ppermute | solution.py:21
  43.1 7.3 %collective-permute-done.2 = f32[10,6,512]{2,0,1:T(8,128)S(1)} collective-permute-done((f32[10,6,512]{2,0,1:T(8,128)S(1)}, f32[10,6,512]{2,0,1:T(8,128)S(1)}, u32[]{:S(2)}, u32[]{:S(2)}) %collective-permute-start.2) | collective-permute-done | bytes 122912 | tf_op jit(solution)/shard_map/ppermute | solution.py:21
  50.4 0.3 fusion.12
  50.6 0.4 fusion.51
  51.1 6.5 %collective-permute-start.3 = (f32[10,16,512]{2,0,1:T(8,128)S(1)}, f32[10,16,512]{2,0,1:T(8,128)S(1)}, u32[]{:S(2)}, u32[]{:S(2)}) collective-permute-start(f32[10,16,512]{2,0,1:T(8,128)S(1)} %fusion.51), channel_id=1, source_target_pairs={{0,32},{32,64},{64,96},{96,128},{128,160},{160,192},{192,224},{224... | collective-permute-start | bytes 983048 | tf_op jit(solution)/shard_map/ppermute | solution.py:21
  57.6 0.6 reshape.35.refs_1_
  58.2 0.9 copy.38
  59.1 0.0 collective-permute-done.3
  59.1 0.0 copy-done.1
  59.2 0.6 fusion.1
  59.7 0.0 copy-start
  59.7 2.7 %fusion.63 = f32[10,16,512]{2,0,1:T(8,128)S(1)} fusion(f32[10,16,512]{2,0,1:T(8,128)S(1)} %fusion.1), kind=kOutput, calls=%fused_computation.103 | output fusion | flops 1228800 | bytes 655360 | tf_op jit(solution)/shard_map/jit(cumsum)/reduce_window_sum | solution.py:221
  62.5 0.6 reshape_squeeze.7.refs_0_
  63.1 42.1 %shard_map.157 = (f32[40,128]{1,0:T(8,128)}, f32[64,128]{1,0:T(8,128)}) custom-call(f32[40,128]{1,0:T(8,128)} %reshape_squeeze.7.refs_0_, f32[64,128]{1,0:T(8,128)} %reshape.35.refs_1_), custom_call_target="tpu_custom_call" | custom-call | tf_op jit(solution)/shard_map/pallas_call | solution.py:150
  105.2 0.0 copy-start.5
  105.2 0.7 add.110
  105.9 0.0 copy-done.5
  106.0 0.0 copy-done
  106.0 0.6 copy-done.10
  106.6 0.0 copy-done.11
  106.6 0.0 copy-done.12
  106.6 0.4 minimum_subtract_fusion
  107.0 0.9 copy.40
  107.9 0.9 copy.39
  108.8 0.6 add_minimum_fusion
  (18 shorter events, 0.1 us)
Async XLA Ops:
  26.7 3.8 %collective-permute-start = (f32[10,16,512]{2,0,1:T(8,128)S(1)}, f32[10,16,512]{2,0,1:T(8,128)S(1)}, u32[]{:S(2)}, u32[]{:S(2)}) collective-permute-start(f32[10,16,512]{2,0,1:T(8,128)S(1)} %reverse_add_fusion), channel_id=1, source_target_pairs={{32,0},{64,32},{96,64},{128,96},{160,128},{192,160},{224,192},{256... | collective-permute-start | bytes 983048 | tf_op jit(solution)/shard_map/ppermute | solution.py:21
  28.0 0.7 copy-start.8
  28.7 0.7 copy-start.9
  30.5 8.3 %copy-start.3 = (f32[10,16,512]{2,1,0:T(8,128)S(1)}, f32[10,16,512]{2,1,0:T(8,128)}, u32[]{:S(2)}) copy-start(f32[10,16,512]{2,1,0:T(8,128)} %param.16) | copy-start | bytes 983044
  31.0 4.6 %copy-start.13 = (f32[10]{0:T(128)S(1)}, f32[10]{0:T(128)}, u32[]{:S(2)}) copy-start(f32[10]{0:T(128)} %param.23) | copy-start | bytes 124
  31.0 7.8 %copy-start.2 = (f32[10,16,512]{2,1,0:T(8,128)S(1)}, f32[10,16,512]{2,1,0:T(8,128)}, u32[]{:S(2)}) copy-start(f32[10,16,512]{2,1,0:T(8,128)} %param.13) | copy-start | bytes 983044
  31.1 7.7 %copy-start.4 = (f32[16,512]{1,0:T(8,128)S(1)}, f32[16,512]{1,0:T(8,128)}, u32[]{:S(2)}) copy-start(f32[16,512]{1,0:T(8,128)} %param.15) | copy-start | bytes 98308
  31.1 7.7 %collective-permute-start.1 = (f32[10,6,512]{2,0,1:T(8,128)S(1)}, f32[10,6,512]{2,0,1:T(8,128)S(1)}, u32[]{:S(2)}, u32[]{:S(2)}) collective-permute-start(f32[10,6,512]{2,0,1:T(8,128)S(1)} %slice.66), channel_id=1, source_target_pairs={{1,0},{2,1},{3,2},{4,3},{5,4},{6,5},{7,6},{8,7},{9,8},{10,9},{11,1... | collective-permute-start | bytes 368648 | tf_op jit(solution)/shard_map/ppermute | solution.py:21
  38.8 0.7 copy-start.7
  40.2 10.1 %collective-permute-start.2 = (f32[10,6,512]{2,0,1:T(8,128)S(1)}, f32[10,6,512]{2,0,1:T(8,128)S(1)}, u32[]{:S(2)}, u32[]{:S(2)}) collective-permute-start(f32[10,6,512]{2,0,1:T(8,128)S(1)} %slice.77), channel_id=1, source_target_pairs={{0,1},{1,2},{2,3},{3,4},{4,5},{5,6},{6,7},{7,8},{8,9},{9,10},{10,1... | collective-permute-start | bytes 368648 | tf_op jit(solution)/shard_map/ppermute | solution.py:21
  51.1 8.0 %collective-permute-start.3 = (f32[10,16,512]{2,0,1:T(8,128)S(1)}, f32[10,16,512]{2,0,1:T(8,128)S(1)}, u32[]{:S(2)}, u32[]{:S(2)}) collective-permute-start(f32[10,16,512]{2,0,1:T(8,128)S(1)} %fusion.51), channel_id=1, source_target_pairs={{0,32},{32,64},{64,96},{96,128},{128,160},{160,192},{192,224},{224... | collective-permute-start | bytes 983048 | tf_op jit(solution)/shard_map/ppermute | solution.py:21
  58.2 1.0 copy-start.1
  59.7 46.2 %copy-start = (f32[10,16,512]{2,1,0:T(8,128)S(1)}, f32[10,16,512]{2,1,0:T(8,128)}, u32[]{:S(2)}) copy-start(f32[10,16,512]{2,1,0:T(8,128)} %param.14) | copy-start | bytes 983044
  105.2 0.8 copy-start.5
  105.9 0.7 copy-start.10
  105.9 0.7 copy-start.11
  105.9 0.7 copy-start.12
  107.9 0.9 copy-start.6

commit v5 on v4

--- a/solution.py
+++ b/solution.py
@@ -132,6 +132,197 @@
         outs[k][...] = part
 
 
+def dual_kernel(
+    sloc_ref, t_ref, off_ref, off_next_ref, beyond_ref, rim_own_ref, rim_next_ref,
+    near, far, group, beyond_buf, rim_src_own, rim_src_next, rim_own_buf, rim_next_buf,
+    off_src, off_next_buf, s1, r1, s2, r2, sems,
+):
+    job = Job("hours", "suffix", 8, lax.axis_size("hours"))
+    job.place()
+    n_r = lax.axis_size("river")
+    n_h = lax.axis_size("hours")
+    r = lax.axis_index("river")
+    h = lax.axis_index("hours")
+    has_up, has_down = r > 0, r < n_r - 1
+    has_before, has_after = h > 0, h < n_h - 1
+
+    barrier = pltpu.get_barrier_semaphore()
+    for dev in job.peers():
+        pl.semaphore_signal(barrier, 1, device_id=dev, device_id_type=MESH)
+    for flag, dev in ((has_up, (r - 1, h)), (has_down, (r + 1, h)), (has_before, (r, h - 1)), (has_after, (r, h + 1))):
+
+        @pl.when(flag)
+        def _():
+            pl.semaphore_signal(barrier, 1, device_id=dev, device_id_type=MESH)
+
+    extra = sum(jnp.where(flag, 1, 0) for flag in (has_up, has_down, has_before, has_after))
+    pl.semaphore_wait(barrier, job.inner + job.outer - 2 + extra)
+
+    def link(src, dst, k, dev):
+        return pltpu.make_async_remote_copy(
+            src_ref=src, dst_ref=dst, send_sem=sems.at[2 * k], recv_sem=sems.at[2 * k + 1],
+            device_id=dev, device_id_type=MESH)
+
+    to_up = lambda src, dst, k: link(src, dst, k, (r - 1, h))
+    to_before = lambda src, dst, k: link(src, dst, k, (r, h - 1))
+
+    def across(p, landing):
+        return pltpu.make_async_remote_copy(
+            src_ref=t_ref, dst_ref=near.at[landing], send_sem=s1.at[p], recv_sem=r1.at[landing],
+            device_id=job.device(job.o * job.inner + p), device_id_type=MESH)
+
+    for s in range(1, job.inner):
+        across(lax.rem(job.i + s, job.inner), job.i).start()
+
+    @pl.when(has_up)
+    def _():
+        to_up(sloc_ref, beyond_buf, 0).start()
+
+    rim_src_own[...] = sloc_ref[:, 0:DMAX, :] - sloc_ref[:, 0:1, :]
+
+    @pl.when(has_before)
+    def _():
+        to_before(rim_src_own, rim_own_buf, 1).start()
+
+    for s in range(1, job.inner):
+        p = lax.rem(job.i + s, job.inner)
+        across(p, job.i).wait_send()
+        across(p, p).wait_recv()
+    own = t_ref[...]
+    total = own
+    part = jnp.zeros_like(own)
+    for s in range(1, job.inner):
+        p = lax.rem(job.i + s, job.inner)
+        block = near[p]
+        total = total + block
+        part = part + jnp.where(p > job.i, block, 0.0)
+    group[...] = total
+
+    def up(q, landing):
+        return pltpu.make_async_remote_copy(
+            src_ref=group, dst_ref=far.at[landing], send_sem=s2.at[q], recv_sem=r2.at[landing],
+            device_id=job.device(q * job.inner + job.i), device_id_type=MESH)
+
+    for s in range(1, job.outer):
+        q = lax.rem(job.o + s, job.outer)
+
+        @pl.when(job.o > q)
+        def _():
+            up(q, job.o).start()
+
+    @pl.when(has_down)
+    def _():
+        to_up(sloc_ref, beyond_buf, 0).wait_recv()
+        rim_src_next[...] = beyond_buf[:, 0:DMAX, :] - beyond_buf[:, 0:1, :]
+
+    @pl.when(jnp.logical_and(has_down, has_before))
+    def _():
+        to_before(rim_src_next, rim_next_buf, 2).start()
+
+    for s in range(1, job.outer):
+        q = lax.rem(job.o + s, job.outer)
+
+        @pl.when(job.o > q)
+        def _():
+            up(q, job.o).wait_send()
+
+        @pl.when(q > job.o)
+        def _():
+            up(q, q).wait_recv()
+
+    for s in range(1, job.outer):
+        q = lax.rem(job.o + s, job.outer)
+        part = part + jnp.where(q > job.o, far[q], 0.0)
+    off_src[...] = part
+    off_ref[...] = part
+
+    @pl.when(has_up)
+    def _():
+        to_up(off_src, off_next_buf, 3).start()
+
+    @pl.when(has_up)
+    def _():
+        to_up(sloc_ref, beyond_buf, 0).wait_send()
+        to_up(off_src, off_next_buf, 3).wait_send()
+
+    @pl.when(has_before)
+    def _():
+        to_before(rim_src_own, rim_own_buf, 1).wait_send()
+
+    @pl.when(jnp.logical_and(has_down, has_before))
+    def _():
+        to_before(rim_src_next, rim_next_buf, 2).wait_send()
+
+    @pl.when(has_after)
+    def _():
+        to_before(rim_src_own, rim_own_buf, 1).wait_recv()
+        rim_own_ref[...] = rim_own_buf[...]
+
+    @pl.when(jnp.logical_not(has_after))
+    def _():
+        rim_own_ref[...] = jnp.zeros_like(rim_own_ref)
+
+    @pl.when(jnp.logical_and(has_down, has_after))
+    def _():
+        to_before(rim_src_next, rim_next_buf, 2).wait_recv()
+        rim_next_ref[...] = rim_next_buf[...]
+
+    @pl.when(jnp.logical_not(jnp.logical_and(has_down, has_after)))
+    def _():
+        rim_next_ref[...] = jnp.zeros_like(rim_next_ref)
+
+    @pl.when(has_down)
+    def _():
+        to_up(off_src, off_next_buf, 3).wait_recv()
+        off_next_ref[...] = off_next_buf[...]
+        beyond_ref[...] = beyond_buf[...]
+
+    @pl.when(jnp.logical_not(has_down))
+    def _():
+        off_next_ref[...] = jnp.zeros_like(off_next_ref)
+        beyond_ref[...] = jnp.zeros_like(beyond_ref)
+
+
+def dual_exchange(sloc):
+    res, length, width = sloc.shape
+    t = sloc[:, 0].reshape(-1, 128)
+    inner = 8
+    outer = lax.axis_size("hours") // inner
+    rim = (res, DMAX, width)
+    vmem = pl.BlockSpec(memory_space=pltpu.VMEM)
+    off, off_next, beyond, rim_own, rim_next = pl.pallas_call(
+        dual_kernel,
+        out_shape=[
+            jax.ShapeDtypeStruct(t.shape, t.dtype),
+            jax.ShapeDtypeStruct(t.shape, t.dtype),
+            jax.ShapeDtypeStruct(sloc.shape, sloc.dtype),
+            jax.ShapeDtypeStruct(rim, sloc.dtype),
+            jax.ShapeDtypeStruct(rim, sloc.dtype),
+        ],
+        in_specs=[vmem, vmem],
+        out_specs=[vmem] * 5,
+        scratch_shapes=[
+            pltpu.VMEM((inner,) + t.shape, t.dtype),
+            pltpu.VMEM((outer,) + t.shape, t.dtype),
+            pltpu.VMEM(t.shape, t.dtype),
+            pltpu.VMEM(sloc.shape, sloc.dtype),
+            pltpu.VMEM(rim, sloc.dtype),
+            pltpu.VMEM(rim, sloc.dtype),
+            pltpu.VMEM(rim, sloc.dtype),
+            pltpu.VMEM(rim, sloc.dtype),
+            pltpu.VMEM(t.shape, t.dtype),
+            pltpu.VMEM(t.shape, t.dtype),
+            pltpu.SemaphoreType.DMA((inner,)),
+            pltpu.SemaphoreType.DMA((inner,)),
+            pltpu.SemaphoreType.DMA((outer,)),
+            pltpu.SemaphoreType.DMA((outer,)),
+            pltpu.SemaphoreType.DMA((8,)),
+        ],
+        compiler_params=pltpu.CompilerParams(collective_id=0, has_side_effects=True, vmem_limit_bytes=48 * 1024 * 1024),
+    )(sloc, t)
+    return off.reshape(res, width), off_next.reshape(res, width), beyond, rim_own, rim_next
+
+
 def combine(parts, specs, collective):
     shapes = [part.shape for part in parts]
     parts = [part.reshape(-1, 128) for part in parts]
@@ -203,10 +394,13 @@
         to_next,
     ) = statics
     scale_time, scale_sum = scales
-    suffix = suffix_sum(storage_dual)
-    beyond = passed_along(suffix, "river", -1)
-    at_sink = route_up(to_own, suffix) + route_up(to_next, beyond)
-    later_duals = bring_forward(at_sink, travel_delay, from_later(at_sink[:, :DMAX]))
+    local = suffix_local(storage_dual)
+    off, off_next, beyond, rim_own, rim_next = dual_exchange(local)
+    suffix = local + off[:, None]
+    at_sink = route_up(to_own, suffix) + route_up(to_next, beyond + off_next[:, None])
+    last = lax.axis_index("hours") == lax.axis_size("hours") - 1
+    rim_sink = route_up(to_own, rim_own + off[:, None]) + route_up(to_next, rim_next + off_next[:, None])
+    later_duals = bring_forward(at_sink, travel_delay, jnp.where(last, 0.0, rim_sink))
     gradient = (
         cost
         + scale_time * (later_duals - suffix)

time: 110 us -> 87 us (0.79)
  Pallas kernels: 64.5 us -> 55.6 us
  starting transfers between devices: 15.2 us -> 6.49 us
  waiting for transfers between devices: 11.2 us -> 6.37 us
  local copies, waits for them, and re-layouts: 10.6 us -> 8.94 us
    pallas_call x2 -> x1, Pallas kernels: 64.5 us -> 33 us  [combine(): pl.pallas_call(functools.partial(multi_kernel, jobs), out_shape=[jax.Shap...]
    pallas_call x0 -> x1, Pallas kernels: none -> 22.6 us  [dual_exchange(): pl.pallas_call(dual_kernel, out_shape=[jax.ShapeDtypeStruct(t.shape, t.dt...]
    ppermute x4 -> x2, starting transfers between devices: 15.2 us -> 6.49 us  [passed_along(): return lax.ppermute(block, axis, route)]
    ppermute x4 -> x2, waiting for transfers between devices: 11.2 us -> 6.37 us  [passed_along(): return lax.ppermute(block, axis, route)]
    another operation x1, other arithmetic: 2.71 us -> 0.39 us  [iterate(): local_sum = jnp.cumsum(inflow + routed - extrapolated, 1)]
    unnamed x31 -> x28, local copies, waits for them, and re-layouts: 5.45 us -> 3.2 us
  transfers between devices with their start and end apart: 4 -> 2, of which waited for: 3 -> 1; matrix products, arithmetic and copies ran while one was open for 2% -> 1% of each run, Pallas kernels for 0% -> 0%
where the time goes in v5:
time: 87 us; the launch traced here: 86.4 us
  Pallas kernels  55.6 us (64%)
  local copies, waits for them, and re-layouts  8.94 us (10%)
  starting transfers between devices  6.49 us (7%)
  waiting for transfers between devices  6.37 us (7%)
  other arithmetic  5.14 us (6%)
  matrix products  2.92 us (3%)
  between operations  0.92 us (1%)
    pallas_call x1, Pallas kernels, combine(): pl.pallas_call(functools.partial(multi_kernel, jobs), out_shape=[jax.Shap...  33 us
    pallas_call x1, Pallas kernels, dual_exchange(): pl.pallas_call(dual_kernel, out_shape=[jax.ShapeDtypeStruct(t.shape, t.dt...  22.6 us
    ppermute x2, starting transfers between devices, passed_along(): return lax.ppermute(block, axis, route)  6.49 us
    ppermute x2, waiting for transfers between devices, passed_along(): return lax.ppermute(block, axis, route)  6.37 us
    unnamed x28, local copies, waits for them, and re-layouts  3.2 us
    rev x2, local copies, waits for them, and re-layouts, suffix_local(): return jnp.flip(jnp.cumsum(jnp.flip(field, 1), 1), 1)  1.99 us
    dot_general x4, matrix products, route_up(): jnp.einsum('ij,itw->jtw', matrix, field, precision=lax.Precision.HIGHEST)  1.82 us
  transfers between devices with their start and end apart: 2, of which 1 were waited for; matrix products, arithmetic and copies ran while one was open for 1% of the time, Pallas kernels for 0%

profile of v5, /device:TPU:8, one launch (start us, length us, event | category | flops | bytes accessed | tf_op | source)
XLA Modules:
  0.0 86.4 jit_solution(11444497463301871479)
XLA Ops:
  0.6 1.8 %rev.7 = f32[10,16,512]{2,1,0:T(8,128)S(1)} reverse(f32[10,16,512]{2,1,0:T(8,128)} %param.14), dimensions={1} | reverse | bytes 655360 | tf_op jit(solution)/shard_map/jit(_flip)/rev | solution.py:434
  2.5 0.4 fusion.10
  2.9 0.2 copy.38
  3.1 0.6 copy-done
  3.7 0.1 rev.8.sloc_ref
  3.8 0.6 slice-done
  4.4 22.6 %shard_map.156 = (f32[40,128]{1,0:T(8,128)S(1)}, f32[40,128]{1,0:T(8,128)S(1)}, f32[10,16,512]{2,1,0:T(8,128)S(1)}, f32[10,6,512]{2,1,0:T(8,128)S(1)}, f32[10,6,512]{2,1,0:T(8,128)S(1)}) custom-call(f32[10,16,512]{2,1,0:T(8,128)S(1)} %rev.8.sloc_ref, f32[40,128]{1,0:T(8,128)S(1)} %reshape_squeeze.6.t_ref), custom_call_target="tpu_custom_call" | custom-call | tf_op jit(solution)/shard_map/pallas_call | solution.py:293
  27.2 0.0 copy-start.12
  27.2 0.6 copy-done.12
  27.9 0.3 fusion.57
  28.2 0.4 fusion.55
  28.5 0.6 fusion.6
  29.2 0.0 copy-start.11
  29.2 0.6 fusion.8
  29.7 0.1 copy-done.11
  29.8 0.6 copy-done.13
  30.5 0.4 copy_add_fusion.2
  30.8 0.0 copy-start.2
  30.9 0.0 copy-start.5
  30.9 0.2 fusion.59
  31.0 0.0 copy-start.10
  31.0 0.4 copy-done.3
  31.4 0.4 copy-done.2
  31.8 1.2 %multiply_reduce_fusion = (f32[16,512]{1,0:T(8,128)S(1)}, f32[10,16,512]{2,1,0:T(8,128)S(1)}, f32[10,16,512]{2,1,0:T(8,128)}) fusion(f32[10]{0:T(128)S(1)} %broadcast_multiply_fusion, f32[10,16,512]{2,1,0:T(8,128)S(1)} %copy-done.2, f32[16,512]{1,0:T(8,128)S(1)} %copy-done.5, f32[10,16,512]{2,1,0:T(8,128)S(1)} %copy-done.3, f32[10,6,512]{2,1,0:T(8,128)S(1)} %fusion.59, ...), kind=kLoop, calls=%fused_computation.82 | loop fusion | flops 2449408 | bytes 2175116 | tf_op jit(solution)/shard_map/reduce_sum | solution.py:416
  33.1 3.4 %collective-permute-start = (f32[10,6,512]{2,1,0:T(8,128)S(1)}, f32[10,6,512]{2,1,0:T(8,128)S(1)}, u32[]{:S(2)}, u32[]{:S(2)}) collective-permute-start(f32[10,6,512]{2,1,0:T(8,128)S(1)} %slice.72), channel_id=1, source_target_pairs={{0,1},{1,2},{2,3},{3,4},{4,5},{5,6},{6,7},{7,8},{8,9},{9,10},{10,1... | collective-permute-start | bytes 368648 | tf_op jit(solution)/shard_map/ppermute | solution.py:21
  36.5 6.3 %collective-permute-done = f32[10,6,512]{2,1,0:T(8,128)S(1)} collective-permute-done((f32[10,6,512]{2,1,0:T(8,128)S(1)}, f32[10,6,512]{2,1,0:T(8,128)S(1)}, u32[]{:S(2)}, u32[]{:S(2)}) %collective-permute-start) | collective-permute-done | bytes 122912 | tf_op jit(solution)/shard_map/ppermute | solution.py:21
  42.8 0.4 fusion.15
  43.2 0.6 fusion
  43.8 0.2 copy.53
  44.0 3.1 %collective-permute-start.1 = (f32[10,16,512]{2,1,0:T(8,128)S(1)}, f32[10,16,512]{2,1,0:T(8,128)S(1)}, u32[]{:S(2)}, u32[]{:S(2)}) collective-permute-start(f32[10,16,512]{2,1,0:T(8,128)S(1)} %copy.53), channel_id=1, source_target_pairs={{0,32},{32,64},{64,96},{96,128},{128,160},{160,192},{192,224},{224... | collective-permute-start | bytes 983048 | tf_op jit(solution)/shard_map/ppermute | solution.py:21
  47.1 0.6 reshape.36.refs_1_
  47.7 0.5 fusion.2
  48.3 0.0 collective-permute-done.1
  48.3 0.4 copy-done.4
  48.7 0.3 fusion.54
  49.0 0.0 copy-start.6
  49.0 0.4 fusion.4
  49.4 0.0 copy-start.1
  49.4 0.6 reshape_squeeze.7.refs_0_
  50.0 33.0 %shard_map.157 = (f32[40,128]{1,0:T(8,128)}, f32[64,128]{1,0:T(8,128)}) custom-call(f32[40,128]{1,0:T(8,128)} %reshape_squeeze.7.refs_0_, f32[64,128]{1,0:T(8,128)} %reshape.36.refs_1_), custom_call_target="tpu_custom_call" | custom-call | tf_op jit(solution)/shard_map/pallas_call | solution.py:341
  83.0 0.7 add.147
  83.7 0.8 reshape.37
  84.5 0.0 copy-start.8
  84.5 0.0 copy-start.9
  84.5 0.6 add_minimum_fusion
  85.2 0.0 copy-done.8
  85.2 0.0 copy-done.9
  85.2 1.2 %minimum_subtract_fusion = (f32[10,16,512]{2,1,0:T(8,128)}, f32[10,16,512]{2,1,0:T(8,128)}) fusion(f32[10]{0:T(128)S(1)} %copy-done.7, f32[10]{0:T(128)S(1)} %copy-done.8, f32[10,512]{1,0:T(8,128)S(1)} %add.147, f32[10,16,512]{2,0,1:T(8,128)S(1)} %fusion.4, f32[10]{0:T(128)S(1)} %copy-done.9, f32[10,16,512]{2,1,0:T(8,128)S(1)} %copy-done.1), kind=kLoop, calls=%fused_computation.80 | loop fusion | flops 1146880 | bytes 1331320 | tf_op jit(solution)/shard_map/sub | solution.py:428
  (22 shorter events, 0.2 us)
Async XLA Ops:
  2.9 0.8 copy-start
  3.7 0.8 slice-start
  27.2 0.7 copy-start.12
  29.2 0.7 copy-start.11
  29.8 0.7 copy-start.13
  30.5 1.0 %copy-start.3 = (f32[10,16,512]{2,1,0:T(8,128)S(1)}, f32[10,16,512]{2,1,0:T(8,128)}, u32[]{:S(2)}) copy-start(f32[10,16,512]{2,1,0:T(8,128)} %param.16) | copy-start | bytes 983044
  30.8 1.0 %copy-start.2 = (f32[10,16,512]{2,1,0:T(8,128)S(1)}, f32[10,16,512]{2,1,0:T(8,128)}, u32[]{:S(2)}) copy-start(f32[10,16,512]{2,1,0:T(8,128)} %param.13) | copy-start | bytes 983044
  30.9 1.0 %copy-start.5 = (f32[16,512]{1,0:T(8,128)S(1)}, f32[16,512]{1,0:T(8,128)}, u32[]{:S(2)}) copy-start(f32[16,512]{1,0:T(8,128)} %param.15) | copy-start | bytes 98308
  31.0 0.8 copy-start.10
  33.1 9.7 %collective-permute-start = (f32[10,6,512]{2,1,0:T(8,128)S(1)}, f32[10,6,512]{2,1,0:T(8,128)S(1)}, u32[]{:S(2)}, u32[]{:S(2)}) collective-permute-start(f32[10,6,512]{2,1,0:T(8,128)S(1)} %slice.72), channel_id=1, source_target_pairs={{0,1},{1,2},{2,3},{3,4},{4,5},{5,6},{6,7},{7,8},{8,9},{9,10},{10,1... | collective-permute-start | bytes 368648 | tf_op jit(solution)/shard_map/ppermute | solution.py:21
  44.0 4.3 %collective-permute-start.1 = (f32[10,16,512]{2,1,0:T(8,128)S(1)}, f32[10,16,512]{2,1,0:T(8,128)S(1)}, u32[]{:S(2)}, u32[]{:S(2)}) collective-permute-start(f32[10,16,512]{2,1,0:T(8,128)S(1)} %copy.53), channel_id=1, source_target_pairs={{0,32},{32,64},{64,96},{96,128},{128,160},{160,192},{192,224},{224... | collective-permute-start | bytes 983048 | tf_op jit(solution)/shard_map/ppermute | solution.py:21
  47.7 1.0 %copy-start.4 = (f32[10,16,512]{2,1,0:T(8,128)S(1)}, f32[10,16,512]{2,1,0:T(8,128)}, u32[]{:S(2)}) copy-start(f32[10,16,512]{2,1,0:T(8,128)} %param.17) | copy-start | bytes 983044
  49.0 35.5 %copy-start.6 = (f32[16,512]{1,0:T(8,128)S(1)}, f32[16,512]{1,0:T(8,128)}, u32[]{:S(2)}) copy-start(f32[16,512]{1,0:T(8,128)} %param.18) | copy-start | bytes 98308
  49.4 35.8 %copy-start.1 = (f32[10,16,512]{2,1,0:T(8,128)S(1)}, f32[10,16,512]{2,1,0:T(8,128)}, u32[]{:S(2)}) copy-start(f32[10,16,512]{2,1,0:T(8,128)} %param.14) | copy-start | bytes 983044
  84.5 0.7 copy-start.7
  84.5 0.7 copy-start.8
  84.5 0.7 copy-start.9

commit v6 on v5

--- a/solution.py
+++ b/solution.py
@@ -323,6 +323,222 @@
     return off.reshape(res, width), off_next.reshape(res, width), beyond, rim_own, rim_next
 
 
+def flow_kernel(
+    main_ref, rim_own_ref, rim_next_ref, ab_ref, power_ref,
+    incoming_ref, rim_own_in_ref, rim_next_in_ref, pa_ref, pb_up_ref, supplied_ref,
+    near_h, far_h, group_h, near_r, far_r, group_r, incoming_buf, rim_own_buf, rim_next_buf,
+    pb_src, pb_buf, s1h, r1h, s2h, r2h, s1r, r1r, s2r, r2r, sems,
+):
+    jobs = [Job("hours", "prefix", 8, lax.axis_size("hours")), Job("river", "sum", 8, lax.axis_size("river"))]
+    for job in jobs:
+        job.place()
+    n_r = lax.axis_size("river")
+    n_h = lax.axis_size("hours")
+    r = lax.axis_index("river")
+    h = lax.axis_index("hours")
+    has_up, has_down = r > 0, r < n_r - 1
+    has_before, has_after = h > 0, h < n_h - 1
+    diag_down = jnp.logical_and(has_down, has_after)
+    diag_up = jnp.logical_and(has_up, has_before)
+
+    barrier = pltpu.get_barrier_semaphore()
+    fixed = 0
+    for job in jobs:
+        for dev in job.peers():
+            pl.semaphore_signal(barrier, 1, device_id=dev, device_id_type=MESH)
+            fixed += 1
+    links = (
+        (has_up, (r - 1, h)), (has_down, (r + 1, h)), (has_before, (r, h - 1)), (has_after, (r, h + 1)),
+        (diag_down, (r + 1, h + 1)), (diag_up, (r - 1, h - 1)),
+    )
+    for flag, dev in links:
+
+        @pl.when(flag)
+        def _():
+            pl.semaphore_signal(barrier, 1, device_id=dev, device_id_type=MESH)
+
+    extra = sum(jnp.where(flag, 1, 0) for flag, _ in links)
+    pl.semaphore_wait(barrier, fixed + extra)
+
+    def link(src, dst, k, dev):
+        return pltpu.make_async_remote_copy(
+            src_ref=src, dst_ref=dst, send_sem=sems.at[2 * k], recv_sem=sems.at[2 * k + 1],
+            device_id=dev, device_id_type=MESH)
+
+    main_copy = link(main_ref, incoming_buf, 0, (r + 1, h))
+    rim_own_copy = link(rim_own_ref, rim_own_buf, 1, (r, h + 1))
+    rim_next_copy = link(rim_next_ref, rim_next_buf, 2, (r + 1, h + 1))
+    pb_copy = link(pb_src, pb_buf, 3, (r + 1, h))
+
+    @pl.when(has_down)
+    def _():
+        main_copy.start()
+
+    @pl.when(has_after)
+    def _():
+        rim_own_copy.start()
+
+    @pl.when(diag_down)
+    def _():
+        rim_next_copy.start()
+
+    bufs = [(ab_ref, near_h, far_h, group_h, s1h, r1h, s2h, r2h), (power_ref, near_r, far_r, group_r, s1r, r1r, s2r, r2r)]
+
+    def across(job, x_ref, near, s1, r1, p, landing):
+        return pltpu.make_async_remote_copy(
+            src_ref=x_ref, dst_ref=near.at[landing], send_sem=s1.at[p], recv_sem=r1.at[landing],
+            device_id=job.device(job.o * job.inner + p), device_id_type=MESH)
+
+    for job, (x_ref, near, far, group, s1, r1, s2, r2) in zip(jobs, bufs):
+        for s in range(1, job.inner):
+            across(job, x_ref, near, s1, r1, lax.rem(job.i + s, job.inner), job.i).start()
+    parts = []
+    for job, (x_ref, near, far, group, s1, r1, s2, r2) in zip(jobs, bufs):
+        for s in range(1, job.inner):
+            p = lax.rem(job.i + s, job.inner)
+            across(job, x_ref, near, s1, r1, p, job.i).wait_send()
+            across(job, x_ref, near, s1, r1, p, p).wait_recv()
+        own = x_ref[...]
+        total = own
+        part = own if job.mode == "sum" else jnp.zeros_like(own)
+        for s in range(1, job.inner):
+            p = lax.rem(job.i + s, job.inner)
+            block = near[p]
+            total = total + block
+            if job.mode == "sum":
+                part = part + block
+            else:
+                part = part + jnp.where(wanted(job.mode, p, job.i), block, 0.0)
+        group[...] = total
+        parts.append(part)
+
+    def up(job, group, far, s2, r2, q, landing):
+        return pltpu.make_async_remote_copy(
+            src_ref=group, dst_ref=far.at[landing], send_sem=s2.at[q], recv_sem=r2.at[landing],
+            device_id=job.device(q * job.inner + job.i), device_id_type=MESH)
+
+    for job, (x_ref, near, far, group, s1, r1, s2, r2) in zip(jobs, bufs):
+        for s in range(1, job.outer):
+            q = lax.rem(job.o + s, job.outer)
+
+            @pl.when(wanted(job.mode, job.o, q))
+            def _():
+                up(job, group, far, s2, r2, q, job.o).start()
+
+    results = []
+    for job, part, (x_ref, near, far, group, s1, r1, s2, r2) in zip(jobs, parts, bufs):
+        for s in range(1, job.outer):
+            q = lax.rem(job.o + s, job.outer)
+
+            @pl.when(wanted(job.mode, job.o, q))
+            def _():
+                up(job, group, far, s2, r2, q, job.o).wait_send()
+
+            @pl.when(wanted(job.mode, q, job.o))
+            def _():
+                up(job, group, far, s2, r2, q, q).wait_recv()
+
+        for s in range(1, job.outer):
+            q = lax.rem(job.o + s, job.outer)
+            part = part + jnp.where(wanted(job.mode, q, job.o), far[q], 0.0)
+        results.append(part)
+    scanned, supplied = results
+    half = pb_src.shape[0]
+    pa_ref[...] = scanned
+    supplied_ref[...] = supplied
+    pb_src[...] = scanned[half:]
+
+    @pl.when(has_down)
+    def _():
+        pb_copy.start()
+        main_copy.wait_send()
+        pb_copy.wait_send()
+
+    @pl.when(has_after)
+    def _():
+        rim_own_copy.wait_send()
+
+    @pl.when(diag_down)
+    def _():
+        rim_next_copy.wait_send()
+
+    @pl.when(has_up)
+    def _():
+        main_copy.wait_recv()
+        pb_copy.wait_recv()
+        incoming_ref[...] = incoming_buf[...]
+        pb_up_ref[...] = pb_buf[...]
+
+    @pl.when(jnp.logical_not(has_up))
+    def _():
+        incoming_ref[...] = jnp.zeros_like(incoming_ref)
+        pb_up_ref[...] = jnp.zeros_like(pb_up_ref)
+
+    @pl.when(has_before)
+    def _():
+        rim_own_copy.wait_recv()
+        rim_own_in_ref[...] = rim_own_buf[...]
+
+    @pl.when(jnp.logical_not(has_before))
+    def _():
+        rim_own_in_ref[...] = jnp.zeros_like(rim_own_in_ref)
+
+    @pl.when(diag_up)
+    def _():
+        rim_next_copy.wait_recv()
+        rim_next_in_ref[...] = rim_next_buf[...]
+
+    @pl.when(jnp.logical_not(diag_up))
+    def _():
+        rim_next_in_ref[...] = jnp.zeros_like(rim_next_in_ref)
+
+
+def flow_exchange(main_next, rim_own, rim_next, own_totals, next_totals, power):
+    res, width = own_totals.shape
+    ab = jnp.concatenate([own_totals, next_totals], 0).reshape(-1, 128)
+    flat_power = power.reshape(-1, 128)
+    half = ab.shape[0] // 2
+    inner = 8
+    outer_h = lax.axis_size("hours") // inner
+    outer_r = lax.axis_size("river") // inner
+    vmem = pl.BlockSpec(memory_space=pltpu.VMEM)
+    shape = lambda a: jax.ShapeDtypeStruct(a.shape, a.dtype)
+    incoming, rim_own_in, rim_next_in, pa, pb_up, supplied = pl.pallas_call(
+        flow_kernel,
+        out_shape=[
+            shape(main_next), shape(rim_own), shape(rim_next), shape(ab),
+            jax.ShapeDtypeStruct((half, 128), ab.dtype), shape(flat_power),
+        ],
+        in_specs=[vmem] * 5,
+        out_specs=[vmem] * 6,
+        scratch_shapes=[
+            pltpu.VMEM((inner,) + ab.shape, ab.dtype),
+            pltpu.VMEM((outer_h,) + ab.shape, ab.dtype),
+            pltpu.VMEM(ab.shape, ab.dtype),
+            pltpu.VMEM((inner,) + flat_power.shape, ab.dtype),
+            pltpu.VMEM((outer_r,) + flat_power.shape, ab.dtype),
+            pltpu.VMEM(flat_power.shape, ab.dtype),
+            pltpu.VMEM(main_next.shape, ab.dtype),
+            pltpu.VMEM(rim_own.shape, ab.dtype),
+            pltpu.VMEM(rim_next.shape, ab.dtype),
+            pltpu.VMEM((half, 128), ab.dtype),
+            pltpu.VMEM((half, 128), ab.dtype),
+            pltpu.SemaphoreType.DMA((inner,)),
+            pltpu.SemaphoreType.DMA((inner,)),
+            pltpu.SemaphoreType.DMA((outer_h,)),
+            pltpu.SemaphoreType.DMA((outer_h,)),
+            pltpu.SemaphoreType.DMA((inner,)),
+            pltpu.SemaphoreType.DMA((inner,)),
+            pltpu.SemaphoreType.DMA((outer_r,)),
+            pltpu.SemaphoreType.DMA((outer_r,)),
+            pltpu.SemaphoreType.DMA((8,)),
+        ],
+        compiler_params=pltpu.CompilerParams(collective_id=1, has_side_effects=True, vmem_limit_bytes=48 * 1024 * 1024),
+    )(main_next, rim_own, rim_next, ab, flat_power)
+    offset = pa[:half].reshape(res, width) + pb_up.reshape(res, width)
+    return incoming, rim_own_in, rim_next_in, offset, supplied.reshape(power.shape)
+
+
 def combine(parts, specs, collective):
     shapes = [part.shape for part in parts]
     parts = [part.reshape(-1, 128) for part in parts]
@@ -409,14 +625,23 @@
     release_new = jnp.clip(release - primal_step * gradient, 0.0, release_cap[:, None, None])
     extrapolated = 2.0 * release_new - release
     length = extrapolated.shape[1]
-    delayed = hold_back(extrapolated, travel_delay, from_earlier(extrapolated[:, length - DMAX :]))
-    incoming = passed_along(route_down(to_next, delayed), "river", 1)
-    routed = route_down(to_own, delayed) + incoming
-    local_sum = jnp.cumsum(inflow + routed - extrapolated, 1)
+    tail = extrapolated[:, length - DMAX :]
+    settled = hold_back(extrapolated, travel_delay, jnp.zeros_like(tail))
+    rim_delayed = hold_back(jnp.zeros_like(extrapolated), travel_delay, tail)[:, :DMAX]
+    main_own = route_down(to_own, settled)
+    main_next = route_down(to_next, settled)
+    rim_own = route_down(to_own, rim_delayed)
+    rim_next = route_down(to_next, rim_delayed)
+    base = inflow + main_own - extrapolated
+    own_totals = jnp.sum(base, 1) + jnp.sum(rim_own, 1)
+    next_totals = jnp.sum(main_next, 1) + jnp.sum(rim_next, 1)
     partial_power = jnp.sum(scale_sum * efficiency[:, None, None] * extrapolated, 0)
-    offset, supplied = combine(
-        [local_sum[:, -1], partial_power], [("hours", "prefix", 8), ("river", "sum", 8)], 1
+    incoming, rim_own_in, rim_next_in, offset, supplied = flow_exchange(
+        main_next, rim_own, rim_next, own_totals, next_totals, partial_power
     )
+    arrived = jnp.concatenate([rim_own_in + rim_next_in, jnp.zeros_like(base[:, DMAX:])], 1)
+    local_sum = jnp.cumsum(base + incoming + arrived, 1)
+    offset = offset - jnp.sum(rim_own_in, 1) - jnp.sum(rim_next_in, 1)
     storage = storage_start[:, None, None] + scale_time * (local_sum + offset[:, None])
     lower_bound = storage_low[:, None, None]
     upper_bound = storage_high[:, None, None]

time: 87 us -> 78 us (0.90)
  the two profiles are of different devices: /device:TPU:8 before, /device:TPU:56 now
where the time goes in v6:
time: 78 us; the launch traced here: 77.6 us
  Pallas kernels  60.8 us (78%)
  local copies, waits for them, and re-layouts  6.83 us (9%)
  other arithmetic  5.4 us (7%)
  matrix products  3.52 us (5%)
  between operations  1.05 us (1%)
    pallas_call x1, Pallas kernels, flow_exchange(): pl.pallas_call(flow_kernel, out_shape=[shape(main_next), shape(rim_own),...  37.6 us
    pallas_call x1, Pallas kernels, dual_exchange(): pl.pallas_call(dual_kernel, out_shape=[jax.ShapeDtypeStruct(t.shape, t.dt...  23.2 us
    unnamed x26, local copies, waits for them, and re-layouts  4.04 us
    rev x2, local copies, waits for them, and re-layouts, suffix_local(): return jnp.flip(jnp.cumsum(jnp.flip(field, 1), 1), 1)  2 us
    dot_general x4, matrix products, route_up(): jnp.einsum('ij,itw->jtw', matrix, field, precision=lax.Precision.HIGHEST)  1.82 us
    dot_general x4, matrix products, route_down(): jnp.einsum('ij,jtw->itw', matrix, field, precision=lax.Precision.HIGHEST)  1.69 us

profile of v6, /device:TPU:56, one launch (start us, length us, event | category | flops | bytes accessed | tf_op | source)
XLA Modules:
  0.0 77.6 jit_solution(1835633658244951302)
XLA Ops:
  0.6 1.8 %rev.7 = f32[10,16,512]{2,1,0:T(8,128)S(1)} reverse(f32[10,16,512]{2,1,0:T(8,128)} %param.14), dimensions={1} | reverse | bytes 655360 | tf_op jit(solution)/shard_map/jit(_flip)/rev | solution.py:659
  2.5 0.4 fusion.10
  2.9 0.2 copy.42
  3.1 0.2 rev.8.sloc_ref
  3.3 23.2 %shard_map.156 = (f32[40,128]{1,0:T(8,128)S(1)}, f32[40,128]{1,0:T(8,128)S(1)}, f32[10,16,512]{2,1,0:T(8,128)S(1)}, f32[10,6,512]{2,1,0:T(8,128)S(1)}, f32[10,6,512]{2,1,0:T(8,128)S(1)}) custom-call(f32[10,16,512]{2,1,0:T(8,128)S(1)} %rev.8.sloc_ref, f32[40,128]{1,0:T(8,128)S(1)} %reshape_squeeze.3.t_ref), custom_call_target="tpu_custom_call" | custom-call | tf_op jit(solution)/shard_map/pallas_call | solution.py:293
  26.6 0.0 copy-start.11
  26.6 0.6 copy-done.11
  27.2 0.4 fusion.53
  27.6 0.3 fusion.55
  27.9 0.2 fusion.62
  28.1 0.6 fusion.6
  28.8 0.6 fusion.8
  29.3 0.0 copy-start.10
  29.3 0.0 copy-start.1
  29.4 0.0 copy-start.2
  29.4 0.0 copy-start.4
  29.4 0.4 copy_add_fusion.2
  29.8 0.2 copy-done.10
  30.0 0.7 copy-done.12
  30.7 0.6 copy-done.9
  31.3 1.2 %multiply_reduce_fusion = (f32[16,512]{1,0:T(8,128)S(1)}, f32[10,16,512]{2,1,0:T(8,128)S(1)}, f32[10,16,512]{2,1,0:T(8,128)}) fusion(f32[10]{0:T(128)S(1)} %broadcast_multiply_fusion, f32[10,16,512]{2,1,0:T(8,128)S(1)} %copy-done.1, f32[16,512]{1,0:T(8,128)S(1)} %copy-done.4, f32[10,16,512]{2,1,0:T(8,128)S(1)} %copy-done.2, f32[10,6,512]{2,1,0:T(8,128)S(1)} %fusion.62, ...), kind=kLoop, calls=%fused_computation.78 | loop fusion | flops 2449408 | bytes 2175116 | tf_op jit(solution)/shard_map/reduce_sum | solution.py:638
  32.6 0.3 fusion.39
  32.9 0.0 copy-start.3
  32.9 0.5 fusion.2
  33.4 0.4 copy-done.3
  33.8 0.3 fusion.89
  34.1 0.2 pad_slice_fusion.5
  34.3 0.1 fusion.57
  34.5 0.3 fusion.94
  34.8 0.3 fusion.93
  35.1 0.6 fusion.92
  35.7 0.1 copy.62.rim_next_ref
  35.8 0.1 copy.61.rim_own_ref
  35.9 0.2 copy.60.main_ref
  36.1 37.6 %shard_map.157 = (f32[10,16,512]{2,1,0:T(8,128)S(1)}, f32[10,6,512]{2,1,0:T(8,128)S(1)}, f32[10,6,512]{2,1,0:T(8,128)S(1)}, f32[80,128]{1,0:T(8,128)S(1)}, f32[40,128]{1,0:T(8,128)S(1)}, /*index=5*/f32[64,128]{1,0:T(8,128)S(1)}) custom-call(f32[10,16,512]{2,1,0:T(8,128)S(1)} %copy.60.main_ref, f32[10,6,512]{2,1,0:T(8,128)S(1)} %copy.61.rim_own_ref, ...), custom_call_target="tpu_custom_call" | custom-call | tf_op jit(solution)/shard_map/pallas_call | solution.py:506
  73.7 0.1 fusion.91
  73.8 0.1 pad_add_fusion
  73.9 0.0 copy-start
  73.9 0.4 fusion.4
  74.3 0.0 copy-start.6
  74.3 0.0 copy-start.7
  74.4 0.5 copy-done
  74.8 0.1 copy-done.6
  75.0 0.0 copy-done.7
  75.0 0.0 copy-done.8
  75.0 1.2 %minimum_subtract_fusion = (f32[10,16,512]{2,1,0:T(8,128)}, f32[10,16,512]{2,1,0:T(8,128)}) fusion(f32[10]{0:T(128)S(1)} %copy-done.6, f32[10]{0:T(128)S(1)} %copy-done.7, f32[10,512]{1,0:T(8,128)S(1)} %subtract_subtract_fusion, f32[10,16,512]{2,0,1:T(8,128)S(1)} %fusion.4, f32[10]{0:T(128)S(1)} %copy-done.8, f32[10,16,512]{2,1,0:T(8,128)S(1)} %copy-done), kind=kLoop, calls=%fused_computation.75 | loop fusion | flops 1146880 | bytes 1331320 | tf_op jit(solution)/shard_map/sub | solution.py:653
  76.2 0.7 copy-done.5
  77.0 0.6 add_minimum_fusion
  (27 shorter events, 0.2 us)
Async XLA Ops:
  26.6 0.7 copy-start.11
  29.3 0.7 copy-start.10
  29.3 1.3 %copy-start.1 = (f32[10,16,512]{2,1,0:T(8,128)S(1)}, f32[10,16,512]{2,1,0:T(8,128)}, u32[]{:S(2)}) copy-start(f32[10,16,512]{2,1,0:T(8,128)} %param.13) | copy-start | bytes 983044
  29.4 1.3 %copy-start.2 = (f32[10,16,512]{2,1,0:T(8,128)S(1)}, f32[10,16,512]{2,1,0:T(8,128)}, u32[]{:S(2)}) copy-start(f32[10,16,512]{2,1,0:T(8,128)} %param.16) | copy-start | bytes 983044
  29.4 1.3 %copy-start.4 = (f32[16,512]{1,0:T(8,128)S(1)}, f32[16,512]{1,0:T(8,128)}, u32[]{:S(2)}) copy-start(f32[16,512]{1,0:T(8,128)} %param.15) | copy-start | bytes 98308
  30.0 0.7 copy-start.12
  30.7 0.7 copy-start.9
  32.9 1.0 %copy-start.3 = (f32[10,16,512]{2,1,0:T(8,128)S(1)}, f32[10,16,512]{2,1,0:T(8,128)}, u32[]{:S(2)}) copy-start(f32[10,16,512]{2,1,0:T(8,128)} %param.17) | copy-start | bytes 983044
  73.9 1.0 %copy-start = (f32[10,16,512]{2,1,0:T(8,128)S(1)}, f32[10,16,512]{2,1,0:T(8,128)}, u32[]{:S(2)}) copy-start(f32[10,16,512]{2,1,0:T(8,128)} %param.14) | copy-start | bytes 983044
  74.3 0.7 copy-start.6
  74.3 0.7 copy-start.7
  74.3 0.7 copy-start.8
  76.2 0.8 copy-start.5

commit v7 on v6

--- a/solution.py
+++ b/solution.py
@@ -324,10 +324,10 @@
 
 
 def flow_kernel(
-    main_ref, rim_own_ref, rim_next_ref, ab_ref, power_ref,
-    incoming_ref, rim_own_in_ref, rim_next_in_ref, pa_ref, pb_up_ref, supplied_ref,
+    main_ref, rim_own_ref, rim_next_ref, a_ref, b_ref, power_ref,
+    incoming_ref, rim_own_in_ref, rim_next_in_ref, pa_ref, supplied_ref,
     near_h, far_h, group_h, near_r, far_r, group_r, incoming_buf, rim_own_buf, rim_next_buf,
-    pb_src, pb_buf, s1h, r1h, s2h, r2h, s1r, r1r, s2r, r2r, sems,
+    a_src, b_buf, s1h, r1h, s2h, r2h, s1r, r1r, s2r, r2r, sems,
 ):
     jobs = [Job("hours", "prefix", 8, lax.axis_size("hours")), Job("river", "sum", 8, lax.axis_size("river"))]
     for job in jobs:
@@ -368,10 +368,11 @@
     main_copy = link(main_ref, incoming_buf, 0, (r + 1, h))
     rim_own_copy = link(rim_own_ref, rim_own_buf, 1, (r, h + 1))
     rim_next_copy = link(rim_next_ref, rim_next_buf, 2, (r + 1, h + 1))
-    pb_copy = link(pb_src, pb_buf, 3, (r + 1, h))
+    b_copy = link(b_ref, b_buf, 3, (r + 1, h))
 
     @pl.when(has_down)
     def _():
+        b_copy.start()
         main_copy.start()
 
     @pl.when(has_after)
@@ -382,14 +383,25 @@
     def _():
         rim_next_copy.start()
 
-    bufs = [(ab_ref, near_h, far_h, group_h, s1h, r1h, s2h, r2h), (power_ref, near_r, far_r, group_r, s1r, r1r, s2r, r2r)]
+    bufs = [(a_src, near_h, far_h, group_h, s1h, r1h, s2h, r2h), (power_ref, near_r, far_r, group_r, s1r, r1r, s2r, r2r)]
 
     def across(job, x_ref, near, s1, r1, p, landing):
         return pltpu.make_async_remote_copy(
             src_ref=x_ref, dst_ref=near.at[landing], send_sem=s1.at[p], recv_sem=r1.at[landing],
             device_id=job.device(job.o * job.inner + p), device_id_type=MESH)
 
-    for job, (x_ref, near, far, group, s1, r1, s2, r2) in zip(jobs, bufs):
+    for job, (x_ref, near, far, group, s1, r1, s2, r2) in zip(jobs[::-1], bufs[::-1]):
+        if job.axis == "hours":
+
+            @pl.when(has_up)
+            def _():
+                b_copy.wait_recv()
+                a_src[...] = a_ref[...] + b_buf[...]
+
+            @pl.when(jnp.logical_not(has_up))
+            def _():
+                a_src[...] = a_ref[...]
+
         for s in range(1, job.inner):
             across(job, x_ref, near, s1, r1, lax.rem(job.i + s, job.inner), job.i).start()
     parts = []
@@ -443,16 +455,13 @@
             part = part + jnp.where(wanted(job.mode, q, job.o), far[q], 0.0)
         results.append(part)
     scanned, supplied = results
-    half = pb_src.shape[0]
     pa_ref[...] = scanned
     supplied_ref[...] = supplied
-    pb_src[...] = scanned[half:]
 
     @pl.when(has_down)
     def _():
-        pb_copy.start()
         main_copy.wait_send()
-        pb_copy.wait_send()
+        b_copy.wait_send()
 
     @pl.when(has_after)
     def _():
@@ -465,14 +474,11 @@
     @pl.when(has_up)
     def _():
         main_copy.wait_recv()
-        pb_copy.wait_recv()
         incoming_ref[...] = incoming_buf[...]
-        pb_up_ref[...] = pb_buf[...]
 
     @pl.when(jnp.logical_not(has_up))
     def _():
         incoming_ref[...] = jnp.zeros_like(incoming_ref)
-        pb_up_ref[...] = jnp.zeros_like(pb_up_ref)
 
     @pl.when(has_before)
     def _():
@@ -495,34 +501,31 @@
 
 def flow_exchange(main_next, rim_own, rim_next, own_totals, next_totals, power):
     res, width = own_totals.shape
-    ab = jnp.concatenate([own_totals, next_totals], 0).reshape(-1, 128)
+    a = own_totals.reshape(-1, 128)
+    b = next_totals.reshape(-1, 128)
     flat_power = power.reshape(-1, 128)
-    half = ab.shape[0] // 2
     inner = 8
     outer_h = lax.axis_size("hours") // inner
     outer_r = lax.axis_size("river") // inner
     vmem = pl.BlockSpec(memory_space=pltpu.VMEM)
-    shape = lambda a: jax.ShapeDtypeStruct(a.shape, a.dtype)
-    incoming, rim_own_in, rim_next_in, pa, pb_up, supplied = pl.pallas_call(
+    shape = lambda x: jax.ShapeDtypeStruct(x.shape, x.dtype)
+    incoming, rim_own_in, rim_next_in, pa, supplied = pl.pallas_call(
         flow_kernel,
-        out_shape=[
-            shape(main_next), shape(rim_own), shape(rim_next), shape(ab),
-            jax.ShapeDtypeStruct((half, 128), ab.dtype), shape(flat_power),
-        ],
-        in_specs=[vmem] * 5,
-        out_specs=[vmem] * 6,
+        out_shape=[shape(main_next), shape(rim_own), shape(rim_next), shape(a), shape(flat_power)],
+        in_specs=[vmem] * 6,
+        out_specs=[vmem] * 5,
         scratch_shapes=[
-            pltpu.VMEM((inner,) + ab.shape, ab.dtype),
-            pltpu.VMEM((outer_h,) + ab.shape, ab.dtype),
-            pltpu.VMEM(ab.shape, ab.dtype),
-            pltpu.VMEM((inner,) + flat_power.shape, ab.dtype),
-            pltpu.VMEM((outer_r,) + flat_power.shape, ab.dtype),
-            pltpu.VMEM(flat_power.shape, ab.dtype),
-            pltpu.VMEM(main_next.shape, ab.dtype),
-            pltpu.VMEM(rim_own.shape, ab.dtype),
-            pltpu.VMEM(rim_next.shape, ab.dtype),
-            pltpu.VMEM((half, 128), ab.dtype),
-            pltpu.VMEM((half, 128), ab.dtype),
+            pltpu.VMEM((inner,) + a.shape, a.dtype),
+            pltpu.VMEM((outer_h,) + a.shape, a.dtype),
+            pltpu.VMEM(a.shape, a.dtype),
+            pltpu.VMEM((inner,) + flat_power.shape, a.dtype),
+            pltpu.VMEM((outer_r,) + flat_power.shape, a.dtype),
+            pltpu.VMEM(flat_power.shape, a.dtype),
+            pltpu.VMEM(main_next.shape, a.dtype),
+            pltpu.VMEM(rim_own.shape, a.dtype),
+            pltpu.VMEM(rim_next.shape, a.dtype),
+            pltpu.VMEM(a.shape, a.dtype),
+            pltpu.VMEM(a.shape, a.dtype),
             pltpu.SemaphoreType.DMA((inner,)),
             pltpu.SemaphoreType.DMA((inner,)),
             pltpu.SemaphoreType.DMA((outer_h,)),
@@ -534,9 +537,8 @@
             pltpu.SemaphoreType.DMA((8,)),
         ],
         compiler_params=pltpu.CompilerParams(collective_id=1, has_side_effects=True, vmem_limit_bytes=48 * 1024 * 1024),
-    )(main_next, rim_own, rim_next, ab, flat_power)
-    offset = pa[:half].reshape(res, width) + pb_up.reshape(res, width)
-    return incoming, rim_own_in, rim_next_in, offset, supplied.reshape(power.shape)
+    )(main_next, rim_own, rim_next, a, b, flat_power)
+    return incoming, rim_own_in, rim_next_in, pa.reshape(res, width), supplied.reshape(power.shape)
 
 
 def combine(parts, specs, collective):

time: 78 us -> 72.2 us (0.926)
  the two profiles are of different devices: /device:TPU:56 before, /device:TPU:8 now
where the time goes in v7:
time: 72.2 us; the launch traced here: 71.8 us
  Pallas kernels  55 us (76%)
  local copies, waits for them, and re-layouts  6.87 us (10%)
  other arithmetic  5.39 us (7%)
  matrix products  3.52 us (5%)
  between operations  1.04 us (1%)
    pallas_call x1, Pallas kernels, flow_exchange(): pl.pallas_call(flow_kernel, out_shape=[shape(main_next), shape(rim_own),...  32.4 us
    pallas_call x1, Pallas kernels, dual_exchange(): pl.pallas_call(dual_kernel, out_shape=[jax.ShapeDtypeStruct(t.shape, t.dt...  22.6 us
    unnamed x26, local copies, waits for them, and re-layouts  4.04 us
    rev x2, local copies, waits for them, and re-layouts, suffix_local(): return jnp.flip(jnp.cumsum(jnp.flip(field, 1), 1), 1)  2 us
    dot_general x4, matrix products, route_up(): jnp.einsum('ij,itw->jtw', matrix, field, precision=lax.Precision.HIGHEST)  1.83 us
    dot_general x4, matrix products, route_down(): jnp.einsum('ij,jtw->itw', matrix, field, precision=lax.Precision.HIGHEST)  1.69 us

profile of v7, /device:TPU:8, one launch (start us, length us, event | category | flops | bytes accessed | tf_op | source)
XLA Modules:
  0.0 71.8 jit_solution(2183874933573557929)
XLA Ops:
  0.6 1.8 %rev.7 = f32[10,16,512]{2,1,0:T(8,128)S(1)} reverse(f32[10,16,512]{2,1,0:T(8,128)} %param.14), dimensions={1} | reverse | bytes 655360 | tf_op jit(solution)/shard_map/jit(_flip)/rev | solution.py:661
  2.5 0.4 fusion.10
  2.9 0.2 copy.42
  3.1 0.2 rev.8.sloc_ref
  3.3 22.6 %shard_map.156 = (f32[40,128]{1,0:T(8,128)S(1)}, f32[40,128]{1,0:T(8,128)S(1)}, f32[10,16,512]{2,1,0:T(8,128)S(1)}, f32[10,6,512]{2,1,0:T(8,128)S(1)}, f32[10,6,512]{2,1,0:T(8,128)S(1)}) custom-call(f32[10,16,512]{2,1,0:T(8,128)S(1)} %rev.8.sloc_ref, f32[40,128]{1,0:T(8,128)S(1)} %reshape_squeeze.3.t_ref), custom_call_target="tpu_custom_call" | custom-call | tf_op jit(solution)/shard_map/pallas_call | solution.py:293
  26.0 0.0 copy-start.11
  26.0 0.6 copy-done.11
  26.6 0.4 fusion.53
  27.0 0.3 fusion.55
  27.3 0.2 fusion.62
  27.5 0.6 fusion.6
  28.2 0.6 fusion.8
  28.7 0.0 copy-start.10
  28.7 0.0 copy-start.1
  28.8 0.0 copy-start.2
  28.8 0.0 copy-start.4
  28.8 0.4 copy_add_fusion.2
  29.2 0.2 copy-done.10
  29.4 0.7 copy-done.12
  30.1 0.6 copy-done.9
  30.7 1.2 %multiply_reduce_fusion = (f32[16,512]{1,0:T(8,128)S(1)}, f32[10,16,512]{2,1,0:T(8,128)S(1)}, f32[10,16,512]{2,1,0:T(8,128)}) fusion(f32[10]{0:T(128)S(1)} %broadcast_multiply_fusion, f32[10,16,512]{2,1,0:T(8,128)S(1)} %copy-done.1, f32[16,512]{1,0:T(8,128)S(1)} %copy-done.4, f32[10,16,512]{2,1,0:T(8,128)S(1)} %copy-done.2, f32[10,6,512]{2,1,0:T(8,128)S(1)} %fusion.62, ...), kind=kLoop, calls=%fused_computation.78 | loop fusion | flops 2449408 | bytes 2175116 | tf_op jit(solution)/shard_map/reduce_sum | solution.py:640
  32.0 0.2 pad_slice_fusion.5
  32.2 0.1 fusion.57
  32.4 0.3 fusion.94
  32.7 0.3 fusion.39
  33.0 0.6 fusion.93
  33.6 0.0 copy-start.3
  33.6 0.5 fusion.2
  34.1 0.4 copy-done.3
  34.5 0.3 fusion.89
  34.8 0.3 fusion.92
  35.1 0.1 copy.62.rim_next_ref
  35.2 0.1 copy.61.rim_own_ref
  35.3 0.2 copy.60.main_ref
  35.5 32.4 %shard_map.157 = (f32[10,16,512]{2,1,0:T(8,128)S(1)}, f32[10,6,512]{2,1,0:T(8,128)S(1)}, f32[10,6,512]{2,1,0:T(8,128)S(1)}, f32[40,128]{1,0:T(8,128)S(1)}, f32[64,128]{1,0:T(8,128)S(1)}) custom-call(f32[10,16,512]{2,1,0:T(8,128)S(1)} %copy.60.main_ref, f32[10,6,512]{2,1,0:T(8,128)S(1)} %copy.61.rim_own_ref, f32[10,6,512]{2,1,0:T(8,128)S(1)} %copy.62.rim_next_ref, ...), custom_call_target="tpu_custom_call" | custom-call | tf_op jit(solution)/shard_map/pallas_call | solution.py:512
  67.9 0.1 fusion.91
  68.0 0.1 pad_add_fusion
  68.1 0.0 copy-start
  68.1 0.4 fusion.4
  68.5 0.0 copy-start.6
  68.5 0.0 copy-start.7
  68.6 0.5 copy-done
  69.1 0.1 copy-done.6
  69.2 0.0 copy-done.7
  69.2 0.0 copy-done.8
  69.2 1.2 %minimum_subtract_fusion = (f32[10,16,512]{2,1,0:T(8,128)}, f32[10,16,512]{2,1,0:T(8,128)}) fusion(f32[10]{0:T(128)S(1)} %copy-done.6, f32[10]{0:T(128)S(1)} %copy-done.7, f32[10,512]{1,0:T(8,128)S(1)} %subtract_subtract_fusion, f32[10,16,512]{2,0,1:T(8,128)S(1)} %fusion.4, f32[10]{0:T(128)S(1)} %copy-done.8, f32[10,16,512]{2,1,0:T(8,128)S(1)} %copy-done), kind=kLoop, calls=%fused_computation.75 | loop fusion | flops 1146880 | bytes 1331320 | tf_op jit(solution)/shard_map/sub | solution.py:655
  70.4 0.7 %copy-done.5 = f32[16,512]{1,0:T(8,128)S(1)} copy-done((f32[16,512]{1,0:T(8,128)S(1)}, f32[16,512]{1,0:T(8,128)}, u32[]{:S(2)}) %copy-start.5) | copy-done | bytes 32792
  71.2 0.6 add_minimum_fusion
  (26 shorter events, 0.2 us)
Async XLA Ops:
  26.0 0.7 copy-start.11
  28.7 0.7 copy-start.10
  28.7 1.3 %copy-start.1 = (f32[10,16,512]{2,1,0:T(8,128)S(1)}, f32[10,16,512]{2,1,0:T(8,128)}, u32[]{:S(2)}) copy-start(f32[10,16,512]{2,1,0:T(8,128)} %param.13) | copy-start | bytes 983044
  28.8 1.3 %copy-start.2 = (f32[10,16,512]{2,1,0:T(8,128)S(1)}, f32[10,16,512]{2,1,0:T(8,128)}, u32[]{:S(2)}) copy-start(f32[10,16,512]{2,1,0:T(8,128)} %param.16) | copy-start | bytes 983044
  28.8 1.3 %copy-start.4 = (f32[16,512]{1,0:T(8,128)S(1)}, f32[16,512]{1,0:T(8,128)}, u32[]{:S(2)}) copy-start(f32[16,512]{1,0:T(8,128)} %param.15) | copy-start | bytes 98308
  29.4 0.7 copy-start.12
  30.1 0.7 copy-start.9
  33.6 1.0 %copy-start.3 = (f32[10,16,512]{2,1,0:T(8,128)S(1)}, f32[10,16,512]{2,1,0:T(8,128)}, u32[]{:S(2)}) copy-start(f32[10,16,512]{2,1,0:T(8,128)} %param.17) | copy-start | bytes 983044
  68.1 1.0 %copy-start = (f32[10,16,512]{2,1,0:T(8,128)S(1)}, f32[10,16,512]{2,1,0:T(8,128)}, u32[]{:S(2)}) copy-start(f32[10,16,512]{2,1,0:T(8,128)} %param.14) | copy-start | bytes 983044
  68.5 0.7 copy-start.6
  68.5 0.7 copy-start.7
  68.5 0.7 copy-start.8
  70.4 0.8 %copy-start.5 = (f32[16,512]{1,0:T(8,128)S(1)}, f32[16,512]{1,0:T(8,128)}, u32[]{:S(2)}) copy-start(f32[16,512]{1,0:T(8,128)} %param.18) | copy-start | bytes 98308

commit v8 on v7

--- a/solution.py
+++ b/solution.py
@@ -326,7 +326,7 @@
 def flow_kernel(
     main_ref, rim_own_ref, rim_next_ref, a_ref, b_ref, power_ref,
     incoming_ref, rim_own_in_ref, rim_next_in_ref, pa_ref, supplied_ref,
-    near_h, far_h, group_h, near_r, far_r, group_r, incoming_buf, rim_own_buf, rim_next_buf,
+    near_h, far_h, group_h, rs_buf, red, x_buf, full, incoming_buf, rim_own_buf, rim_next_buf,
     a_src, b_buf, s1h, r1h, s2h, r2h, s1r, r1r, s2r, r2r, sems,
 ):
     jobs = [Job("hours", "prefix", 8, lax.axis_size("hours")), Job("river", "sum", 8, lax.axis_size("river"))]
@@ -383,14 +383,24 @@
     def _():
         rim_next_copy.start()
 
-    bufs = [(a_src, near_h, far_h, group_h, s1h, r1h, s2h, r2h), (power_ref, near_r, far_r, group_r, s1r, r1r, s2r, r2r)]
+    bufs = [(a_src, near_h, far_h, group_h, s1h, r1h, s2h, r2h)]
+    river = jobs.pop()
+    tile = rs_buf.shape[1]
+
+    def scatter(c, landing):
+        return pltpu.make_async_remote_copy(
+            src_ref=power_ref.at[pl.ds(c * tile, tile)], dst_ref=rs_buf.at[landing], send_sem=s1r.at[c],
+            recv_sem=r1r.at[landing], device_id=river.device(river.o * river.inner + c), device_id_type=MESH)
+
+    for s in range(1, river.inner):
+        scatter(lax.rem(river.i + s, river.inner), river.i).start()
 
     def across(job, x_ref, near, s1, r1, p, landing):
         return pltpu.make_async_remote_copy(
             src_ref=x_ref, dst_ref=near.at[landing], send_sem=s1.at[p], recv_sem=r1.at[landing],
             device_id=job.device(job.o * job.inner + p), device_id_type=MESH)
 
-    for job, (x_ref, near, far, group, s1, r1, s2, r2) in zip(jobs[::-1], bufs[::-1]):
+    for job, (x_ref, near, far, group, s1, r1, s2, r2) in zip(jobs, bufs):
         if job.axis == "hours":
 
             @pl.when(has_up)
@@ -454,9 +464,38 @@
             q = lax.rem(job.o + s, job.outer)
             part = part + jnp.where(wanted(job.mode, q, job.o), far[q], 0.0)
         results.append(part)
-    scanned, supplied = results
+    (scanned,) = results
     pa_ref[...] = scanned
-    supplied_ref[...] = supplied
+
+    for s in range(1, river.inner):
+        c = lax.rem(river.i + s, river.inner)
+        scatter(c, river.i).wait_send()
+        scatter(c, c).wait_recv()
+    mine = power_ref[pl.ds(river.i * tile, tile)]
+    for s in range(1, river.inner):
+        mine = mine + rs_buf[lax.rem(river.i + s, river.inner)]
+    red[...] = mine
+    partner = river.device(lax.rem(river.o + 1, river.outer) * river.inner + river.i)
+    swap = pltpu.make_async_remote_copy(
+        src_ref=red, dst_ref=x_buf, send_sem=s2r.at[0], recv_sem=r2r.at[0], device_id=partner, device_id_type=MESH)
+    swap.start()
+    swap.wait_send()
+    swap.wait_recv()
+    full[river.i] = mine + x_buf[...]
+
+    def gather(c, landing):
+        return pltpu.make_async_remote_copy(
+            src_ref=full.at[river.i], dst_ref=full.at[landing], send_sem=s2r.at[1 + c], recv_sem=r1r.at[river.inner + landing],
+            device_id=river.device(river.o * river.inner + c), device_id_type=MESH)
+
+    for s in range(1, river.inner):
+        gather(lax.rem(river.i + s, river.inner), river.i).start()
+    for s in range(1, river.inner):
+        c = lax.rem(river.i + s, river.inner)
+        gather(c, river.i).wait_send()
+        gather(c, c).wait_recv()
+    for c in range(river.inner):
+        supplied_ref[pl.ds(c * tile, tile)] = full[c]
 
     @pl.when(has_down)
     def _():
@@ -518,9 +557,10 @@
             pltpu.VMEM((inner,) + a.shape, a.dtype),
             pltpu.VMEM((outer_h,) + a.shape, a.dtype),
             pltpu.VMEM(a.shape, a.dtype),
-            pltpu.VMEM((inner,) + flat_power.shape, a.dtype),
-            pltpu.VMEM((outer_r,) + flat_power.shape, a.dtype),
-            pltpu.VMEM(flat_power.shape, a.dtype),
+            pltpu.VMEM((inner, flat_power.shape[0] // inner, 128), a.dtype),
+            pltpu.VMEM((flat_power.shape[0] // inner, 128), a.dtype),
+            pltpu.VMEM((flat_power.shape[0] // inner, 128), a.dtype),
+            pltpu.VMEM((inner, flat_power.shape[0] // inner, 128), a.dtype),
             pltpu.VMEM(main_next.shape, a.dtype),
             pltpu.VMEM(rim_own.shape, a.dtype),
             pltpu.VMEM(rim_next.shape, a.dtype),
@@ -531,9 +571,9 @@
             pltpu.SemaphoreType.DMA((outer_h,)),
             pltpu.SemaphoreType.DMA((outer_h,)),
             pltpu.SemaphoreType.DMA((inner,)),
-            pltpu.SemaphoreType.DMA((inner,)),
-            pltpu.SemaphoreType.DMA((outer_r,)),
-            pltpu.SemaphoreType.DMA((outer_r,)),
+            pltpu.SemaphoreType.DMA((2 * inner,)),
+            pltpu.SemaphoreType.DMA((inner + 1,)),
+            pltpu.SemaphoreType.DMA((1,)),
             pltpu.SemaphoreType.DMA((8,)),
         ],
         compiler_params=pltpu.CompilerParams(collective_id=1, has_side_effects=True, vmem_limit_bytes=48 * 1024 * 1024),

time: 72.2 us -> 76.9 us (1.065)
  the two profiles are of different devices: /device:TPU:8 before, /device:TPU:25 now
where the time goes in v8:
time: 76.9 us; the launch traced here: 76.5 us
  Pallas kernels  59.7 us (78%)
  local copies, waits for them, and re-layouts  6.87 us (9%)
  other arithmetic  5.39 us (7%)
  matrix products  3.52 us (5%)
  between operations  1.04 us (1%)
    pallas_call x1, Pallas kernels, flow_exchange(): pl.pallas_call(flow_kernel, out_shape=[shape(main_next), shape(rim_own),...  37 us
    pallas_call x1, Pallas kernels, dual_exchange(): pl.pallas_call(dual_kernel, out_shape=[jax.ShapeDtypeStruct(t.shape, t.dt...  22.7 us
    unnamed x26, local copies, waits for them, and re-layouts  4.04 us
    rev x2, local copies, waits for them, and re-layouts, suffix_local(): return jnp.flip(jnp.cumsum(jnp.flip(field, 1), 1), 1)  2 us
    dot_general x4, matrix products, route_up(): jnp.einsum('ij,itw->jtw', matrix, field, precision=lax.Precision.HIGHEST)  1.83 us
    dot_general x4, matrix products, route_down(): jnp.einsum('ij,jtw->itw', matrix, field, precision=lax.Precision.HIGHEST)  1.69 us

profile of v8, /device:TPU:25, one launch (start us, length us, event | category | flops | bytes accessed | tf_op | source)
XLA Modules:
  0.0 76.5 jit_solution(12423631446612060478)
XLA Ops:
  0.6 1.8 %rev.7 = f32[10,16,512]{2,1,0:T(8,128)S(1)} reverse(f32[10,16,512]{2,1,0:T(8,128)} %param.14), dimensions={1} | reverse | bytes 655360 | tf_op jit(solution)/shard_map/jit(_flip)/rev | solution.py:701
  2.5 0.4 fusion.10
  2.9 0.2 copy.42
  3.1 0.2 rev.8.sloc_ref
  3.3 22.7 %shard_map.156 = (f32[40,128]{1,0:T(8,128)S(1)}, f32[40,128]{1,0:T(8,128)S(1)}, f32[10,16,512]{2,1,0:T(8,128)S(1)}, f32[10,6,512]{2,1,0:T(8,128)S(1)}, f32[10,6,512]{2,1,0:T(8,128)S(1)}) custom-call(f32[10,16,512]{2,1,0:T(8,128)S(1)} %rev.8.sloc_ref, f32[40,128]{1,0:T(8,128)S(1)} %reshape_squeeze.3.t_ref), custom_call_target="tpu_custom_call" | custom-call | tf_op jit(solution)/shard_map/pallas_call | solution.py:293
  26.0 0.0 copy-start.11
  26.0 0.6 copy-done.11
  26.7 0.4 fusion.53
  27.0 0.3 fusion.55
  27.3 0.2 fusion.62
  27.6 0.6 fusion.6
  28.2 0.6 fusion.8
  28.8 0.0 copy-start.10
  28.8 0.0 copy-start.1
  28.8 0.0 copy-start.2
  28.8 0.0 copy-start.4
  28.8 0.4 copy_add_fusion.2
  29.2 0.2 copy-done.10
  29.5 0.7 copy-done.12
  30.1 0.6 copy-done.9
  30.8 1.2 %multiply_reduce_fusion = (f32[16,512]{1,0:T(8,128)S(1)}, f32[10,16,512]{2,1,0:T(8,128)S(1)}, f32[10,16,512]{2,1,0:T(8,128)}) fusion(f32[10]{0:T(128)S(1)} %broadcast_multiply_fusion, f32[10,16,512]{2,1,0:T(8,128)S(1)} %copy-done.1, f32[16,512]{1,0:T(8,128)S(1)} %copy-done.4, f32[10,16,512]{2,1,0:T(8,128)S(1)} %copy-done.2, f32[10,6,512]{2,1,0:T(8,128)S(1)} %fusion.62, ...), kind=kLoop, calls=%fused_computation.78 | loop fusion | flops 2449408 | bytes 2175116 | tf_op jit(solution)/shard_map/reduce_sum | solution.py:680
  32.0 0.2 pad_slice_fusion.5
  32.3 0.1 fusion.57
  32.4 0.3 fusion.94
  32.7 0.3 fusion.39
  33.0 0.6 fusion.93
  33.6 0.0 copy-start.3
  33.6 0.5 fusion.2
  34.2 0.4 copy-done.3
  34.6 0.3 fusion.89
  34.9 0.3 fusion.92
  35.2 0.1 copy.62.rim_next_ref
  35.3 0.1 copy.61.rim_own_ref
  35.4 0.2 copy.60.main_ref
  35.6 37.0 %shard_map.157 = (f32[10,16,512]{2,1,0:T(8,128)S(1)}, f32[10,6,512]{2,1,0:T(8,128)S(1)}, f32[10,6,512]{2,1,0:T(8,128)S(1)}, f32[40,128]{1,0:T(8,128)S(1)}, f32[64,128]{1,0:T(8,128)S(1)}) custom-call(f32[10,16,512]{2,1,0:T(8,128)S(1)} %copy.60.main_ref, f32[10,6,512]{2,1,0:T(8,128)S(1)} %copy.61.rim_own_ref, f32[10,6,512]{2,1,0:T(8,128)S(1)} %copy.62.rim_next_ref, ...), custom_call_target="tpu_custom_call" | custom-call | tf_op jit(solution)/shard_map/pallas_call | solution.py:551
  72.6 0.1 fusion.91
  72.7 0.1 pad_add_fusion
  72.8 0.0 copy-start
  72.8 0.4 fusion.4
  73.2 0.0 copy-start.6
  73.2 0.0 copy-start.7
  73.2 0.5 copy-done
  73.7 0.1 copy-done.6
  73.9 0.0 copy-done.7
  73.9 0.0 copy-done.8
  73.9 1.2 %minimum_subtract_fusion = (f32[10,16,512]{2,1,0:T(8,128)}, f32[10,16,512]{2,1,0:T(8,128)}) fusion(f32[10]{0:T(128)S(1)} %copy-done.6, f32[10]{0:T(128)S(1)} %copy-done.7, f32[10,512]{1,0:T(8,128)S(1)} %subtract_subtract_fusion, f32[10,16,512]{2,0,1:T(8,128)S(1)} %fusion.4, f32[10]{0:T(128)S(1)} %copy-done.8, f32[10,16,512]{2,1,0:T(8,128)S(1)} %copy-done), kind=kLoop, calls=%fused_computation.75 | loop fusion | flops 1146880 | bytes 1331320 | tf_op jit(solution)/shard_map/sub | solution.py:695
  75.1 0.7 copy-done.5
  75.9 0.6 add_minimum_fusion
  (26 shorter events, 0.2 us)
Async XLA Ops:
  26.0 0.7 copy-start.11
  28.8 0.7 copy-start.10
  28.8 1.3 %copy-start.1 = (f32[10,16,512]{2,1,0:T(8,128)S(1)}, f32[10,16,512]{2,1,0:T(8,128)}, u32[]{:S(2)}) copy-start(f32[10,16,512]{2,1,0:T(8,128)} %param.13) | copy-start | bytes 983044
  28.8 1.3 %copy-start.2 = (f32[10,16,512]{2,1,0:T(8,128)S(1)}, f32[10,16,512]{2,1,0:T(8,128)}, u32[]{:S(2)}) copy-start(f32[10,16,512]{2,1,0:T(8,128)} %param.16) | copy-start | bytes 983044
  28.8 1.3 %copy-start.4 = (f32[16,512]{1,0:T(8,128)S(1)}, f32[16,512]{1,0:T(8,128)}, u32[]{:S(2)}) copy-start(f32[16,512]{1,0:T(8,128)} %param.15) | copy-start | bytes 98308
  29.5 0.7 copy-start.12
  30.1 0.7 copy-start.9
  33.6 1.0 %copy-start.3 = (f32[10,16,512]{2,1,0:T(8,128)S(1)}, f32[10,16,512]{2,1,0:T(8,128)}, u32[]{:S(2)}) copy-start(f32[10,16,512]{2,1,0:T(8,128)} %param.17) | copy-start | bytes 983044
  72.8 1.0 %copy-start = (f32[10,16,512]{2,1,0:T(8,128)S(1)}, f32[10,16,512]{2,1,0:T(8,128)}, u32[]{:S(2)}) copy-start(f32[10,16,512]{2,1,0:T(8,128)} %param.14) | copy-start | bytes 983044
  73.2 0.7 copy-start.6
  73.2 0.7 copy-start.7
  73.2 0.7 copy-start.8
  75.1 0.8 copy-start.5

commit v9 on v7

--- a/solution.py
+++ b/solution.py
@@ -658,7 +658,7 @@
 
 
 def suffix_local(field):
-    return jnp.flip(jnp.cumsum(jnp.flip(field, 1), 1), 1)
+    return lax.cumsum(field, 1, reverse=True)
 
 
 def shards(

time: 72.2 us -> 71.3 us (0.988)
  local copies, waits for them, and re-layouts: 6.87 us -> 4.87 us
  other arithmetic: 5.39 us -> 6.58 us
    rev x2 -> x0, local copies, waits for them, and re-layouts: 2 us -> none  [suffix_local(): return jnp.flip(jnp.cumsum(jnp.flip(field, 1), 1), 1)]
    another operation x1, other arithmetic: 0.38 us -> 1.21 us  [suffix_local(): return lax.cumsum(field, 1, reverse=True)]
where the time goes in v9:
time: 71.3 us; the launch traced here: 71 us
  Pallas kernels  55 us (77%)
  other arithmetic  6.58 us (9%)
  local copies, waits for them, and re-layouts  4.87 us (7%)
  matrix products  3.51 us (5%)
  between operations  1.02 us (1%)
    pallas_call x1, Pallas kernels, flow_exchange(): pl.pallas_call(flow_kernel, out_shape=[shape(main_next), shape(rim_own),...  32.4 us
    pallas_call x1, Pallas kernels, dual_exchange(): pl.pallas_call(dual_kernel, out_shape=[jax.ShapeDtypeStruct(t.shape, t.dt...  22.6 us
    unnamed x26, local copies, waits for them, and re-layouts  4.04 us
    dot_general x4, matrix products, route_up(): jnp.einsum('ij,itw->jtw', matrix, field, precision=lax.Precision.HIGHEST)  1.83 us
    dot_general x4, matrix products, route_down(): jnp.einsum('ij,jtw->itw', matrix, field, precision=lax.Precision.HIGHEST)  1.69 us

profile of v9, /device:TPU:8, one launch (start us, length us, event | category | flops | bytes accessed | tf_op | source)
XLA Modules:
  0.0 71.0 jit_solution(5499966844034529359)
XLA Ops:
  0.6 1.2 %fusion.10 = f32[10,16,512]{2,0,1:T(8,128)S(1)} fusion(f32[10,16,512]{2,1,0:T(8,128)} %param.14), kind=kOutput, calls=%fused_computation.32 | output fusion | flops 1228800 | bytes 655360 | tf_op jit(solution)/shard_map/suffix_local/reduce_window_sum | solution.py:661
  1.8 0.2 copy.44.sloc_ref
  2.1 22.6 %shard_map.156 = (f32[40,128]{1,0:T(8,128)S(1)}, f32[40,128]{1,0:T(8,128)S(1)}, f32[10,16,512]{2,1,0:T(8,128)S(1)}, f32[10,6,512]{2,1,0:T(8,128)S(1)}, f32[10,6,512]{2,1,0:T(8,128)S(1)}) custom-call(f32[10,16,512]{2,1,0:T(8,128)S(1)} %copy.44.sloc_ref, f32[40,128]{1,0:T(8,128)S(1)} %reshape_squeeze.3.t_ref), custom_call_target="tpu_custom_call" | custom-call | tf_op jit(solution)/shard_map/pallas_call | solution.py:293
  24.7 0.1 broadcast_add_fusion.2
  24.8 0.0 copy-start.11
  24.8 0.6 copy-done.11
  25.5 0.4 fusion.53
  25.8 0.3 fusion.55
  26.1 0.2 fusion.62
  26.3 0.6 fusion.6
  27.0 0.2 broadcast_add_fusion.1
  27.2 0.6 fusion.8
  27.7 0.0 copy-start.10
  27.7 0.0 copy-start.1
  27.8 0.0 copy-start.2
  27.8 0.0 copy-start.4
  27.8 0.4 copy_add_fusion.2
  28.1 0.2 copy-done.10
  28.4 0.7 copy-done.12
  29.1 0.6 copy-done.9
  29.7 1.4 %multiply_reduce_fusion = (f32[16,512]{1,0:T(8,128)S(1)}, f32[10,16,512]{2,1,0:T(8,128)S(1)}, f32[10,16,512]{2,1,0:T(8,128)}) fusion(f32[10]{0:T(128)S(1)} %broadcast_multiply_fusion, f32[10,16,512]{2,1,0:T(8,128)S(1)} %copy-done.1, f32[16,512]{1,0:T(8,128)S(1)} %copy-done.4, f32[10,16,512]{2,1,0:T(8,128)S(1)} %copy-done.2, f32[10,6,512]{2,1,0:T(8,128)S(1)} %fusion.62, ...), kind=kLoop, calls=%fused_computation.78 | loop fusion | flops 2449408 | bytes 2175116 | tf_op jit(solution)/shard_map/reduce_sum | solution.py:640
  31.1 0.2 pad_slice_fusion.5
  31.4 0.1 fusion.57
  31.5 0.3 fusion.94
  31.8 0.3 fusion.39
  32.1 0.6 fusion.93
  32.7 0.0 copy-start.3
  32.7 0.5 fusion.2
  33.3 0.4 copy-done.3
  33.7 0.3 fusion.89
  34.0 0.3 fusion.92
  34.3 0.1 copy.64.rim_next_ref
  34.4 0.1 copy.63.rim_own_ref
  34.5 0.2 copy.62.main_ref
  34.7 32.4 %shard_map.157 = (f32[10,16,512]{2,1,0:T(8,128)S(1)}, f32[10,6,512]{2,1,0:T(8,128)S(1)}, f32[10,6,512]{2,1,0:T(8,128)S(1)}, f32[40,128]{1,0:T(8,128)S(1)}, f32[64,128]{1,0:T(8,128)S(1)}) custom-call(f32[10,16,512]{2,1,0:T(8,128)S(1)} %copy.62.main_ref, f32[10,6,512]{2,1,0:T(8,128)S(1)} %copy.63.rim_own_ref, f32[10,6,512]{2,1,0:T(8,128)S(1)} %copy.64.rim_next_ref, ...), custom_call_target="tpu_custom_call" | custom-call | tf_op jit(solution)/shard_map/pallas_call | solution.py:512
  67.1 0.1 fusion.91
  67.2 0.1 pad_add_fusion
  67.2 0.0 copy-start
  67.3 0.4 fusion.4
  67.7 0.0 copy-start.7
  67.7 0.0 copy-start.8
  67.7 0.5 copy-done
  68.2 0.1 copy-done.6
  68.3 0.0 copy-done.7
  68.4 0.0 copy-done.8
  68.4 1.2 %minimum_subtract_fusion = (f32[10,16,512]{2,1,0:T(8,128)}, f32[10,16,512]{2,1,0:T(8,128)}) fusion(f32[10]{0:T(128)S(1)} %copy-done.6, f32[10]{0:T(128)S(1)} %copy-done.7, f32[10,512]{1,0:T(8,128)S(1)} %subtract_subtract_fusion, f32[10,16,512]{2,0,1:T(8,128)S(1)} %fusion.4, f32[10]{0:T(128)S(1)} %copy-done.8, f32[10,16,512]{2,1,0:T(8,128)S(1)} %copy-done), kind=kLoop, calls=%fused_computation.75 | loop fusion | flops 1146880 | bytes 1331320 | tf_op jit(solution)/shard_map/sub | solution.py:655
  69.6 0.7 %copy-done.5 = f32[16,512]{1,0:T(8,128)S(1)} copy-done((f32[16,512]{1,0:T(8,128)S(1)}, f32[16,512]{1,0:T(8,128)}, u32[]{:S(2)}) %copy-start.5) | copy-done | bytes 32792
  70.3 0.6 add_minimum_fusion
  (24 shorter events, 0.2 us)
Async XLA Ops:
  24.8 0.7 copy-start.11
  27.7 0.7 copy-start.10
  27.7 1.3 %copy-start.1 = (f32[10,16,512]{2,1,0:T(8,128)S(1)}, f32[10,16,512]{2,1,0:T(8,128)}, u32[]{:S(2)}) copy-start(f32[10,16,512]{2,1,0:T(8,128)} %param.13) | copy-start | bytes 983044
  27.8 1.3 %copy-start.2 = (f32[10,16,512]{2,1,0:T(8,128)S(1)}, f32[10,16,512]{2,1,0:T(8,128)}, u32[]{:S(2)}) copy-start(f32[10,16,512]{2,1,0:T(8,128)} %param.16) | copy-start | bytes 983044
  27.8 1.3 %copy-start.4 = (f32[16,512]{1,0:T(8,128)S(1)}, f32[16,512]{1,0:T(8,128)}, u32[]{:S(2)}) copy-start(f32[16,512]{1,0:T(8,128)} %param.15) | copy-start | bytes 98308
  28.4 0.7 copy-start.12
  29.0 0.7 copy-start.9
  32.7 1.0 %copy-start.3 = (f32[10,16,512]{2,1,0:T(8,128)S(1)}, f32[10,16,512]{2,1,0:T(8,128)}, u32[]{:S(2)}) copy-start(f32[10,16,512]{2,1,0:T(8,128)} %param.17) | copy-start | bytes 983044
  67.2 1.0 %copy-start = (f32[10,16,512]{2,1,0:T(8,128)S(1)}, f32[10,16,512]{2,1,0:T(8,128)}, u32[]{:S(2)}) copy-start(f32[10,16,512]{2,1,0:T(8,128)} %param.14) | copy-start | bytes 983044
  67.7 0.7 copy-start.6
  67.7 0.7 copy-start.7
  67.7 0.7 copy-start.8
  69.6 0.8 %copy-start.5 = (f32[16,512]{1,0:T(8,128)S(1)}, f32[16,512]{1,0:T(8,128)}, u32[]{:S(2)}) copy-start(f32[16,512]{1,0:T(8,128)} %param.18) | copy-start | bytes 98308

commit v10 on v9

--- a/solution.py
+++ b/solution.py
@@ -9,6 +9,7 @@
 from jax.sharding import PartitionSpec as P
 
 DMAX = 6
+HOURS_INNER = 4
 
 
 primal_step = 1.0
@@ -137,7 +138,7 @@
     near, far, group, beyond_buf, rim_src_own, rim_src_next, rim_own_buf, rim_next_buf,
     off_src, off_next_buf, s1, r1, s2, r2, sems,
 ):
-    job = Job("hours", "suffix", 8, lax.axis_size("hours"))
+    job = Job("hours", "suffix", HOURS_INNER, lax.axis_size("hours"))
     job.place()
     n_r = lax.axis_size("river")
     n_h = lax.axis_size("hours")
@@ -286,7 +287,7 @@
 def dual_exchange(sloc):
     res, length, width = sloc.shape
     t = sloc[:, 0].reshape(-1, 128)
-    inner = 8
+    inner = HOURS_INNER
     outer = lax.axis_size("hours") // inner
     rim = (res, DMAX, width)
     vmem = pl.BlockSpec(memory_space=pltpu.VMEM)
@@ -329,7 +330,7 @@
     near_h, far_h, group_h, near_r, far_r, group_r, incoming_buf, rim_own_buf, rim_next_buf,
     a_src, b_buf, s1h, r1h, s2h, r2h, s1r, r1r, s2r, r2r, sems,
 ):
-    jobs = [Job("hours", "prefix", 8, lax.axis_size("hours")), Job("river", "sum", 8, lax.axis_size("river"))]
+    jobs = [Job("hours", "prefix", HOURS_INNER, lax.axis_size("hours")), Job("river", "sum", 8, lax.axis_size("river"))]
     for job in jobs:
         job.place()
     n_r = lax.axis_size("river")
@@ -504,8 +505,9 @@
     a = own_totals.reshape(-1, 128)
     b = next_totals.reshape(-1, 128)
     flat_power = power.reshape(-1, 128)
+    inner_h = HOURS_INNER
     inner = 8
-    outer_h = lax.axis_size("hours") // inner
+    outer_h = lax.axis_size("hours") // inner_h
     outer_r = lax.axis_size("river") // inner
     vmem = pl.BlockSpec(memory_space=pltpu.VMEM)
     shape = lambda x: jax.ShapeDtypeStruct(x.shape, x.dtype)
@@ -515,7 +517,7 @@
         in_specs=[vmem] * 6,
         out_specs=[vmem] * 5,
         scratch_shapes=[
-            pltpu.VMEM((inner,) + a.shape, a.dtype),
+            pltpu.VMEM((inner_h,) + a.shape, a.dtype),
             pltpu.VMEM((outer_h,) + a.shape, a.dtype),
             pltpu.VMEM(a.shape, a.dtype),
             pltpu.VMEM((inner,) + flat_power.shape, a.dtype),
@@ -526,8 +528,8 @@
             pltpu.VMEM(rim_next.shape, a.dtype),
             pltpu.VMEM(a.shape, a.dtype),
             pltpu.VMEM(a.shape, a.dtype),
-            pltpu.SemaphoreType.DMA((inner,)),
-            pltpu.SemaphoreType.DMA((inner,)),
+            pltpu.SemaphoreType.DMA((inner_h,)),
+            pltpu.SemaphoreType.DMA((inner_h,)),
             pltpu.SemaphoreType.DMA((outer_h,)),
             pltpu.SemaphoreType.DMA((outer_h,)),
             pltpu.SemaphoreType.DMA((inner,)),

time: 71.3 us -> 75.2 us (1.055)
  the two profiles are of different devices: /device:TPU:8 before, /device:TPU:112 now
where the time goes in v10:
time: 75.2 us; the launch traced here: 74.8 us
  Pallas kernels  58.8 us (78%)
  other arithmetic  6.58 us (9%)
  local copies, waits for them, and re-layouts  4.87 us (6%)
  matrix products  3.52 us (5%)
  between operations  1.02 us (1%)
    pallas_call x1, Pallas kernels, flow_exchange(): pl.pallas_call(flow_kernel, out_shape=[shape(main_next), shape(rim_own),...  35.8 us
    pallas_call x1, Pallas kernels, dual_exchange(): pl.pallas_call(dual_kernel, out_shape=[jax.ShapeDtypeStruct(t.shape, t.dt...  23 us
    unnamed x26, local copies, waits for them, and re-layouts  4.04 us
    dot_general x4, matrix products, route_up(): jnp.einsum('ij,itw->jtw', matrix, field, precision=lax.Precision.HIGHEST)  1.82 us
    dot_general x4, matrix products, route_down(): jnp.einsum('ij,jtw->itw', matrix, field, precision=lax.Precision.HIGHEST)  1.69 us

profile of v10, /device:TPU:112, one launch (start us, length us, event | category | flops | bytes accessed | tf_op | source)
XLA Modules:
  0.0 74.8 jit_solution(15744005087152734360)
XLA Ops:
  0.6 1.2 %fusion.10 = f32[10,16,512]{2,0,1:T(8,128)S(1)} fusion(f32[10,16,512]{2,1,0:T(8,128)} %param.14), kind=kOutput, calls=%fused_computation.32 | output fusion | flops 1228800 | bytes 655360 | tf_op jit(solution)/shard_map/suffix_local/reduce_window_sum | solution.py:663
  1.8 0.2 copy.44.sloc_ref
  2.1 23.0 %shard_map.156 = (f32[40,128]{1,0:T(8,128)S(1)}, f32[40,128]{1,0:T(8,128)S(1)}, f32[10,16,512]{2,1,0:T(8,128)S(1)}, f32[10,6,512]{2,1,0:T(8,128)S(1)}, f32[10,6,512]{2,1,0:T(8,128)S(1)}) custom-call(f32[10,16,512]{2,1,0:T(8,128)S(1)} %copy.44.sloc_ref, f32[40,128]{1,0:T(8,128)S(1)} %reshape_squeeze.3.t_ref), custom_call_target="tpu_custom_call" | custom-call | tf_op jit(solution)/shard_map/pallas_call | solution.py:294
  25.1 0.1 broadcast_add_fusion.2
  25.2 0.0 copy-start.11
  25.2 0.6 copy-done.11
  25.9 0.4 fusion.53
  26.2 0.3 fusion.55
  26.5 0.2 fusion.62
  26.7 0.6 fusion.6
  27.4 0.2 broadcast_add_fusion.1
  27.6 0.6 fusion.8
  28.1 0.0 copy-start.10
  28.1 0.0 copy-start.1
  28.2 0.0 copy-start.2
  28.2 0.0 copy-start.4
  28.2 0.4 copy_add_fusion.2
  28.6 0.2 copy-done.10
  28.8 0.7 copy-done.12
  29.5 0.6 copy-done.9
  30.1 1.4 %multiply_reduce_fusion = (f32[16,512]{1,0:T(8,128)S(1)}, f32[10,16,512]{2,1,0:T(8,128)S(1)}, f32[10,16,512]{2,1,0:T(8,128)}) fusion(f32[10]{0:T(128)S(1)} %broadcast_multiply_fusion, f32[10,16,512]{2,1,0:T(8,128)S(1)} %copy-done.1, f32[16,512]{1,0:T(8,128)S(1)} %copy-done.4, f32[10,16,512]{2,1,0:T(8,128)S(1)} %copy-done.2, f32[10,6,512]{2,1,0:T(8,128)S(1)} %fusion.62, ...), kind=kLoop, calls=%fused_computation.78 | loop fusion | flops 2449408 | bytes 2175116 | tf_op jit(solution)/shard_map/reduce_sum | solution.py:642
  31.5 0.2 pad_slice_fusion.5
  31.8 0.1 fusion.57
  31.9 0.3 fusion.94
  32.2 0.3 fusion.39
  32.5 0.6 fusion.93
  33.1 0.0 copy-start.3
  33.1 0.5 fusion.2
  33.7 0.4 copy-done.3
  34.1 0.3 fusion.89
  34.4 0.3 fusion.92
  34.7 0.1 copy.64.rim_next_ref
  34.8 0.1 copy.63.rim_own_ref
  34.9 0.2 copy.62.main_ref
  35.1 35.8 %shard_map.157 = (f32[10,16,512]{2,1,0:T(8,128)S(1)}, f32[10,6,512]{2,1,0:T(8,128)S(1)}, f32[10,6,512]{2,1,0:T(8,128)S(1)}, f32[40,128]{1,0:T(8,128)S(1)}, f32[64,128]{1,0:T(8,128)S(1)}) custom-call(f32[10,16,512]{2,1,0:T(8,128)S(1)} %copy.62.main_ref, f32[10,6,512]{2,1,0:T(8,128)S(1)} %copy.63.rim_own_ref, f32[10,6,512]{2,1,0:T(8,128)S(1)} %copy.64.rim_next_ref, ...), custom_call_target="tpu_custom_call" | custom-call | tf_op jit(solution)/shard_map/pallas_call | solution.py:514
  70.9 0.1 fusion.91
  71.0 0.1 pad_add_fusion
  71.1 0.0 copy-start
  71.1 0.4 fusion.4
  71.5 0.0 copy-start.6
  71.5 0.0 copy-start.7
  71.6 0.5 copy-done
  72.1 0.1 copy-done.6
  72.2 0.0 copy-done.7
  72.2 0.0 copy-done.8
  72.2 1.2 %minimum_subtract_fusion = (f32[10,16,512]{2,1,0:T(8,128)}, f32[10,16,512]{2,1,0:T(8,128)}) fusion(f32[10]{0:T(128)S(1)} %copy-done.6, f32[10]{0:T(128)S(1)} %copy-done.7, f32[10,512]{1,0:T(8,128)S(1)} %subtract_subtract_fusion, f32[10,16,512]{2,0,1:T(8,128)S(1)} %fusion.4, f32[10]{0:T(128)S(1)} %copy-done.8, f32[10,16,512]{2,1,0:T(8,128)S(1)} %copy-done), kind=kLoop, calls=%fused_computation.75 | loop fusion | flops 1146880 | bytes 1331320 | tf_op jit(solution)/shard_map/sub | solution.py:657
  73.4 0.7 copy-done.5
  74.2 0.6 add_minimum_fusion
  (24 shorter events, 0.2 us)
Async XLA Ops:
  25.2 0.7 copy-start.11
  28.1 0.7 copy-start.10
  28.1 1.3 %copy-start.1 = (f32[10,16,512]{2,1,0:T(8,128)S(1)}, f32[10,16,512]{2,1,0:T(8,128)}, u32[]{:S(2)}) copy-start(f32[10,16,512]{2,1,0:T(8,128)} %param.13) | copy-start | bytes 983044
  28.2 1.3 %copy-start.2 = (f32[10,16,512]{2,1,0:T(8,128)S(1)}, f32[10,16,512]{2,1,0:T(8,128)}, u32[]{:S(2)}) copy-start(f32[10,16,512]{2,1,0:T(8,128)} %param.16) | copy-start | bytes 983044
  28.2 1.3 %copy-start.4 = (f32[16,512]{1,0:T(8,128)S(1)}, f32[16,512]{1,0:T(8,128)}, u32[]{:S(2)}) copy-start(f32[16,512]{1,0:T(8,128)} %param.15) | copy-start | bytes 98308
  28.8 0.7 copy-start.12
  29.5 0.7 copy-start.9
  33.1 1.0 %copy-start.3 = (f32[10,16,512]{2,1,0:T(8,128)S(1)}, f32[10,16,512]{2,1,0:T(8,128)}, u32[]{:S(2)}) copy-start(f32[10,16,512]{2,1,0:T(8,128)} %param.17) | copy-start | bytes 983044
  71.1 1.0 %copy-start = (f32[10,16,512]{2,1,0:T(8,128)S(1)}, f32[10,16,512]{2,1,0:T(8,128)}, u32[]{:S(2)}) copy-start(f32[10,16,512]{2,1,0:T(8,128)} %param.14) | copy-start | bytes 983044
  71.5 0.7 copy-start.6
  71.5 0.7 copy-start.7
  71.5 0.7 copy-start.8
  73.4 0.8 %copy-start.5 = (f32[16,512]{1,0:T(8,128)S(1)}, f32[16,512]{1,0:T(8,128)}, u32[]{:S(2)}) copy-start(f32[16,512]{1,0:T(8,128)} %param.18) | copy-start | bytes 98308

commit v11 on v9

--- a/solution.py
+++ b/solution.py
@@ -135,7 +135,7 @@
 def dual_kernel(
     sloc_ref, t_ref, off_ref, off_next_ref, beyond_ref, rim_own_ref, rim_next_ref,
     near, far, group, beyond_buf, rim_src_own, rim_src_next, rim_own_buf, rim_next_buf,
-    off_src, off_next_buf, s1, r1, s2, r2, sems,
+    s_src, tn_buf, s1, r1, s2, r2, sems,
 ):
     job = Job("hours", "suffix", 8, lax.axis_size("hours"))
     job.place()
@@ -168,15 +168,30 @@
 
     def across(p, landing):
         return pltpu.make_async_remote_copy(
-            src_ref=t_ref, dst_ref=near.at[landing], send_sem=s1.at[p], recv_sem=r1.at[landing],
+            src_ref=s_src, dst_ref=near.at[landing], send_sem=s1.at[p], recv_sem=r1.at[landing],
             device_id=job.device(job.o * job.inner + p), device_id_type=MESH)
+
+    t_copy = to_up(t_ref, tn_buf, 3)
+    half = t_ref.shape[0]
+
+    @pl.when(has_up)
+    def _():
+        t_copy.start()
+        to_up(sloc_ref, beyond_buf, 0).start()
+
+    s_src[0:half] = t_ref[...]
+
+    @pl.when(has_down)
+    def _():
+        t_copy.wait_recv()
+        s_src[half:] = tn_buf[...]
+
+    @pl.when(jnp.logical_not(has_down))
+    def _():
+        s_src[half:] = jnp.zeros_like(tn_buf)
 
     for s in range(1, job.inner):
         across(lax.rem(job.i + s, job.inner), job.i).start()
-
-    @pl.when(has_up)
-    def _():
-        to_up(sloc_ref, beyond_buf, 0).start()
 
     rim_src_own[...] = sloc_ref[:, 0:DMAX, :] - sloc_ref[:, 0:1, :]
 
@@ -188,7 +203,7 @@
         p = lax.rem(job.i + s, job.inner)
         across(p, job.i).wait_send()
         across(p, p).wait_recv()
-    own = t_ref[...]
+    own = s_src[...]
     total = own
     part = jnp.zeros_like(own)
     for s in range(1, job.inner):
@@ -233,17 +248,13 @@
     for s in range(1, job.outer):
         q = lax.rem(job.o + s, job.outer)
         part = part + jnp.where(q > job.o, far[q], 0.0)
-    off_src[...] = part
-    off_ref[...] = part
+    off_ref[...] = part[:half]
+    off_next_ref[...] = part[half:]
 
     @pl.when(has_up)
     def _():
-        to_up(off_src, off_next_buf, 3).start()
-
-    @pl.when(has_up)
-    def _():
         to_up(sloc_ref, beyond_buf, 0).wait_send()
-        to_up(off_src, off_next_buf, 3).wait_send()
+        t_copy.wait_send()
 
     @pl.when(has_before)
     def _():
@@ -273,13 +284,10 @@
 
     @pl.when(has_down)
     def _():
-        to_up(off_src, off_next_buf, 3).wait_recv()
-        off_next_ref[...] = off_next_buf[...]
         beyond_ref[...] = beyond_buf[...]
 
     @pl.when(jnp.logical_not(has_down))
     def _():
-        off_next_ref[...] = jnp.zeros_like(off_next_ref)
         beyond_ref[...] = jnp.zeros_like(beyond_ref)
 
 
@@ -302,15 +310,15 @@
         in_specs=[vmem, vmem],
         out_specs=[vmem] * 5,
         scratch_shapes=[
-            pltpu.VMEM((inner,) + t.shape, t.dtype),
-            pltpu.VMEM((outer,) + t.shape, t.dtype),
-            pltpu.VMEM(t.shape, t.dtype),
+            pltpu.VMEM((inner, 2 * t.shape[0], 128), t.dtype),
+            pltpu.VMEM((outer, 2 * t.shape[0], 128), t.dtype),
+            pltpu.VMEM((2 * t.shape[0], 128), t.dtype),
             pltpu.VMEM(sloc.shape, sloc.dtype),
             pltpu.VMEM(rim, sloc.dtype),
             pltpu.VMEM(rim, sloc.dtype),
             pltpu.VMEM(rim, sloc.dtype),
             pltpu.VMEM(rim, sloc.dtype),
-            pltpu.VMEM(t.shape, t.dtype),
+            pltpu.VMEM((2 * t.shape[0], 128), t.dtype),
             pltpu.VMEM(t.shape, t.dtype),
             pltpu.SemaphoreType.DMA((inner,)),
             pltpu.SemaphoreType.DMA((inner,)),

time: 71.3 us -> 74.9 us (1.050)
  Pallas kernels: 55 us -> 58.5 us
    pallas_call x1, Pallas kernels: 22.6 us -> 27.7 us  [dual_exchange(): pl.pallas_call(dual_kernel, out_shape=[jax.ShapeDtypeStruct(t.shape, t.dt...]
    pallas_call x1, Pallas kernels: 32.4 us -> 30.9 us  [flow_exchange(): pl.pallas_call(flow_kernel, out_shape=[shape(main_next), shape(rim_own),...]
where the time goes in v11:
time: 74.9 us; the launch traced here: 74.5 us
  Pallas kernels  58.5 us (78%)
  other arithmetic  6.58 us (9%)
  local copies, waits for them, and re-layouts  4.87 us (7%)
  matrix products  3.52 us (5%)
  between operations  1.02 us (1%)
    pallas_call x1, Pallas kernels, flow_exchange(): pl.pallas_call(flow_kernel, out_shape=[shape(main_next), shape(rim_own),...  30.9 us
    pallas_call x1, Pallas kernels, dual_exchange(): pl.pallas_call(dual_kernel, out_shape=[jax.ShapeDtypeStruct(t.shape, t.dt...  27.7 us
    unnamed x26, local copies, waits for them, and re-layouts  4.04 us
    dot_general x4, matrix products, route_up(): jnp.einsum('ij,itw->jtw', matrix, field, precision=lax.Precision.HIGHEST)  1.82 us
    dot_general x4, matrix products, route_down(): jnp.einsum('ij,jtw->itw', matrix, field, precision=lax.Precision.HIGHEST)  1.69 us

profile of v11, /device:TPU:8, one launch (start us, length us, event | category | flops | bytes accessed | tf_op | source)
XLA Modules:
  0.0 74.5 jit_solution(17112595258943375797)
XLA Ops:
  0.6 1.2 %fusion.10 = f32[10,16,512]{2,0,1:T(8,128)S(1)} fusion(f32[10,16,512]{2,1,0:T(8,128)} %param.14), kind=kOutput, calls=%fused_computation.32 | output fusion | flops 1228800 | bytes 655360 | tf_op jit(solution)/shard_map/suffix_local/reduce_window_sum | solution.py:669
  1.8 0.2 copy.44.sloc_ref
  2.1 27.7 %shard_map.156 = (f32[40,128]{1,0:T(8,128)S(1)}, f32[40,128]{1,0:T(8,128)S(1)}, f32[10,16,512]{2,1,0:T(8,128)S(1)}, f32[10,6,512]{2,1,0:T(8,128)S(1)}, f32[10,6,512]{2,1,0:T(8,128)S(1)}) custom-call(f32[10,16,512]{2,1,0:T(8,128)S(1)} %copy.44.sloc_ref, f32[40,128]{1,0:T(8,128)S(1)} %reshape_squeeze.3.t_ref), custom_call_target="tpu_custom_call" | custom-call | tf_op jit(solution)/shard_map/pallas_call | solution.py:301
  29.8 0.1 broadcast_add_fusion.2
  29.8 0.0 copy-start.11
  29.9 0.6 copy-done.11
  30.5 0.4 fusion.53
  30.9 0.3 fusion.55
  31.2 0.2 fusion.62
  31.4 0.6 fusion.6
  32.0 0.2 broadcast_add_fusion.1
  32.2 0.6 fusion.8
  32.8 0.0 copy-start.10
  32.8 0.0 copy-start.1
  32.8 0.0 copy-start.2
  32.8 0.0 copy-start.4
  32.8 0.4 copy_add_fusion.2
  33.2 0.2 copy-done.10
  33.4 0.7 copy-done.12
  34.1 0.6 copy-done.9
  34.8 1.4 %multiply_reduce_fusion = (f32[16,512]{1,0:T(8,128)S(1)}, f32[10,16,512]{2,1,0:T(8,128)S(1)}, f32[10,16,512]{2,1,0:T(8,128)}) fusion(f32[10]{0:T(128)S(1)} %broadcast_multiply_fusion, f32[10,16,512]{2,1,0:T(8,128)S(1)} %copy-done.1, f32[16,512]{1,0:T(8,128)S(1)} %copy-done.4, f32[10,16,512]{2,1,0:T(8,128)S(1)} %copy-done.2, f32[10,6,512]{2,1,0:T(8,128)S(1)} %fusion.62, ...), kind=kLoop, calls=%fused_computation.78 | loop fusion | flops 2449408 | bytes 2175116 | tf_op jit(solution)/shard_map/reduce_sum | solution.py:648
  36.2 0.2 pad_slice_fusion.5
  36.4 0.1 fusion.57
  36.6 0.3 fusion.94
  36.9 0.3 fusion.39
  37.2 0.6 fusion.93
  37.8 0.0 copy-start.3
  37.8 0.5 fusion.2
  38.3 0.4 copy-done.3
  38.7 0.3 fusion.89
  39.0 0.3 fusion.92
  39.4 0.1 copy.64.rim_next_ref
  39.4 0.1 copy.63.rim_own_ref
  39.5 0.2 copy.62.main_ref
  39.7 30.9 %shard_map.157 = (f32[10,16,512]{2,1,0:T(8,128)S(1)}, f32[10,6,512]{2,1,0:T(8,128)S(1)}, f32[10,6,512]{2,1,0:T(8,128)S(1)}, f32[40,128]{1,0:T(8,128)S(1)}, f32[64,128]{1,0:T(8,128)S(1)}) custom-call(f32[10,16,512]{2,1,0:T(8,128)S(1)} %copy.62.main_ref, f32[10,6,512]{2,1,0:T(8,128)S(1)} %copy.63.rim_own_ref, f32[10,6,512]{2,1,0:T(8,128)S(1)} %copy.64.rim_next_ref, ...), custom_call_target="tpu_custom_call" | custom-call | tf_op jit(solution)/shard_map/pallas_call | solution.py:520
  70.6 0.1 fusion.91
  70.7 0.1 pad_add_fusion
  70.8 0.0 copy-start
  70.8 0.4 fusion.4
  71.2 0.0 copy-start.6
  71.2 0.0 copy-start.7
  71.3 0.5 copy-done
  71.8 0.1 copy-done.6
  71.9 0.0 copy-done.7
  71.9 0.0 copy-done.8
  71.9 1.2 %minimum_subtract_fusion = (f32[10,16,512]{2,1,0:T(8,128)}, f32[10,16,512]{2,1,0:T(8,128)}) fusion(f32[10]{0:T(128)S(1)} %copy-done.6, f32[10]{0:T(128)S(1)} %copy-done.7, f32[10,512]{1,0:T(8,128)S(1)} %subtract_subtract_fusion, f32[10,16,512]{2,0,1:T(8,128)S(1)} %fusion.4, f32[10]{0:T(128)S(1)} %copy-done.8, f32[10,16,512]{2,1,0:T(8,128)S(1)} %copy-done), kind=kLoop, calls=%fused_computation.75 | loop fusion | flops 1146880 | bytes 1331320 | tf_op jit(solution)/shard_map/sub | solution.py:663
  73.1 0.7 %copy-done.5 = f32[16,512]{1,0:T(8,128)S(1)} copy-done((f32[16,512]{1,0:T(8,128)S(1)}, f32[16,512]{1,0:T(8,128)}, u32[]{:S(2)}) %copy-start.5) | copy-done | bytes 32792
  73.9 0.6 add_minimum_fusion
  (24 shorter events, 0.2 us)
Async XLA Ops:
  29.8 0.7 copy-start.11
  32.8 0.7 copy-start.10
  32.8 1.3 %copy-start.1 = (f32[10,16,512]{2,1,0:T(8,128)S(1)}, f32[10,16,512]{2,1,0:T(8,128)}, u32[]{:S(2)}) copy-start(f32[10,16,512]{2,1,0:T(8,128)} %param.13) | copy-start | bytes 983044
  32.8 1.3 %copy-start.2 = (f32[10,16,512]{2,1,0:T(8,128)S(1)}, f32[10,16,512]{2,1,0:T(8,128)}, u32[]{:S(2)}) copy-start(f32[10,16,512]{2,1,0:T(8,128)} %param.16) | copy-start | bytes 983044
  32.8 1.3 %copy-start.4 = (f32[16,512]{1,0:T(8,128)S(1)}, f32[16,512]{1,0:T(8,128)}, u32[]{:S(2)}) copy-start(f32[16,512]{1,0:T(8,128)} %param.15) | copy-start | bytes 98308
  33.4 0.7 copy-start.12
  34.1 0.7 copy-start.9
  37.8 1.0 %copy-start.3 = (f32[10,16,512]{2,1,0:T(8,128)S(1)}, f32[10,16,512]{2,1,0:T(8,128)}, u32[]{:S(2)}) copy-start(f32[10,16,512]{2,1,0:T(8,128)} %param.17) | copy-start | bytes 983044
  70.8 1.0 %copy-start = (f32[10,16,512]{2,1,0:T(8,128)S(1)}, f32[10,16,512]{2,1,0:T(8,128)}, u32[]{:S(2)}) copy-start(f32[10,16,512]{2,1,0:T(8,128)} %param.14) | copy-start | bytes 983044
  71.2 0.7 copy-start.6
  71.2 0.7 copy-start.7
  71.2 0.7 copy-start.8
  73.1 0.8 %copy-start.5 = (f32[16,512]{1,0:T(8,128)S(1)}, f32[16,512]{1,0:T(8,128)}, u32[]{:S(2)}) copy-start(f32[16,512]{1,0:T(8,128)} %param.18) | copy-start | bytes 98308

commit v12 on v9

--- a/solution.py
+++ b/solution.py
@@ -9,6 +9,7 @@
 from jax.sharding import PartitionSpec as P
 
 DMAX = 6
+RIVER_INNER = 2
 
 
 primal_step = 1.0
@@ -329,7 +330,7 @@
     near_h, far_h, group_h, near_r, far_r, group_r, incoming_buf, rim_own_buf, rim_next_buf,
     a_src, b_buf, s1h, r1h, s2h, r2h, s1r, r1r, s2r, r2r, sems,
 ):
-    jobs = [Job("hours", "prefix", 8, lax.axis_size("hours")), Job("river", "sum", 8, lax.axis_size("river"))]
+    jobs = [Job("hours", "prefix", 8, lax.axis_size("hours")), Job("river", "sum", RIVER_INNER, lax.axis_size("river"))]
     for job in jobs:
         job.place()
     n_r = lax.axis_size("river")
@@ -505,8 +506,9 @@
     b = next_totals.reshape(-1, 128)
     flat_power = power.reshape(-1, 128)
     inner = 8
+    inner_r = RIVER_INNER
     outer_h = lax.axis_size("hours") // inner
-    outer_r = lax.axis_size("river") // inner
+    outer_r = lax.axis_size("river") // inner_r
     vmem = pl.BlockSpec(memory_space=pltpu.VMEM)
     shape = lambda x: jax.ShapeDtypeStruct(x.shape, x.dtype)
     incoming, rim_own_in, rim_next_in, pa, supplied = pl.pallas_call(
@@ -518,7 +520,7 @@
             pltpu.VMEM((inner,) + a.shape, a.dtype),
             pltpu.VMEM((outer_h,) + a.shape, a.dtype),
             pltpu.VMEM(a.shape, a.dtype),
-            pltpu.VMEM((inner,) + flat_power.shape, a.dtype),
+            pltpu.VMEM((inner_r,) + flat_power.shape, a.dtype),
             pltpu.VMEM((outer_r,) + flat_power.shape, a.dtype),
             pltpu.VMEM(flat_power.shape, a.dtype),
             pltpu.VMEM(main_next.shape, a.dtype),
@@ -530,8 +532,8 @@
             pltpu.SemaphoreType.DMA((inner,)),
             pltpu.SemaphoreType.DMA((outer_h,)),
             pltpu.SemaphoreType.DMA((outer_h,)),
-            pltpu.SemaphoreType.DMA((inner,)),
-            pltpu.SemaphoreType.DMA((inner,)),
+            pltpu.SemaphoreType.DMA((inner_r,)),
+            pltpu.SemaphoreType.DMA((inner_r,)),
             pltpu.SemaphoreType.DMA((outer_r,)),
             pltpu.SemaphoreType.DMA((outer_r,)),
             pltpu.SemaphoreType.DMA((8,)),

time: 71.3 us -> 75.7 us (1.062)
  the two profiles are of different devices: /device:TPU:8 before, /device:TPU:6 now
where the time goes in v12:
time: 75.7 us; the launch traced here: 75.4 us
  Pallas kernels  59.4 us (78%)
  other arithmetic  6.58 us (9%)
  local copies, waits for them, and re-layouts  4.87 us (6%)
  matrix products  3.52 us (5%)
  between operations  1.02 us (1%)
    pallas_call x1, Pallas kernels, flow_exchange(): pl.pallas_call(flow_kernel, out_shape=[shape(main_next), shape(rim_own),...  35.6 us
    pallas_call x1, Pallas kernels, dual_exchange(): pl.pallas_call(dual_kernel, out_shape=[jax.ShapeDtypeStruct(t.shape, t.dt...  23.8 us
    unnamed x26, local copies, waits for them, and re-layouts  4.04 us
    dot_general x4, matrix products, route_up(): jnp.einsum('ij,itw->jtw', matrix, field, precision=lax.Precision.HIGHEST)  1.82 us
    dot_general x4, matrix products, route_down(): jnp.einsum('ij,jtw->itw', matrix, field, precision=lax.Precision.HIGHEST)  1.69 us

profile of v12, /device:TPU:6, one launch (start us, length us, event | category | flops | bytes accessed | tf_op | source)
XLA Modules:
  0.0 75.4 jit_solution(2609633458610708082)
XLA Ops:
  0.6 1.2 %fusion.10 = f32[10,16,512]{2,0,1:T(8,128)S(1)} fusion(f32[10,16,512]{2,1,0:T(8,128)} %param.14), kind=kOutput, calls=%fused_computation.32 | output fusion | flops 1228800 | bytes 655360 | tf_op jit(solution)/shard_map/suffix_local/reduce_window_sum | solution.py:663
  1.8 0.2 copy.44.sloc_ref
  2.1 23.8 %shard_map.156 = (f32[40,128]{1,0:T(8,128)S(1)}, f32[40,128]{1,0:T(8,128)S(1)}, f32[10,16,512]{2,1,0:T(8,128)S(1)}, f32[10,6,512]{2,1,0:T(8,128)S(1)}, f32[10,6,512]{2,1,0:T(8,128)S(1)}) custom-call(f32[10,16,512]{2,1,0:T(8,128)S(1)} %copy.44.sloc_ref, f32[40,128]{1,0:T(8,128)S(1)} %reshape_squeeze.3.t_ref), custom_call_target="tpu_custom_call" | custom-call | tf_op jit(solution)/shard_map/pallas_call | solution.py:294
  25.9 0.1 broadcast_add_fusion.2
  26.0 0.0 copy-start.11
  26.0 0.6 copy-done.11
  26.6 0.4 fusion.53
  27.0 0.3 fusion.55
  27.3 0.2 fusion.62
  27.5 0.6 fusion.6
  28.1 0.2 broadcast_add_fusion.1
  28.3 0.6 fusion.8
  28.9 0.0 copy-start.10
  28.9 0.0 copy-start.1
  28.9 0.0 copy-start.2
  28.9 0.0 copy-start.4
  28.9 0.4 copy_add_fusion.2
  29.3 0.2 copy-done.10
  29.6 0.7 copy-done.12
  30.2 0.6 copy-done.9
  30.9 1.4 %multiply_reduce_fusion = (f32[16,512]{1,0:T(8,128)S(1)}, f32[10,16,512]{2,1,0:T(8,128)S(1)}, f32[10,16,512]{2,1,0:T(8,128)}) fusion(f32[10]{0:T(128)S(1)} %broadcast_multiply_fusion, f32[10,16,512]{2,1,0:T(8,128)S(1)} %copy-done.1, f32[16,512]{1,0:T(8,128)S(1)} %copy-done.4, f32[10,16,512]{2,1,0:T(8,128)S(1)} %copy-done.2, f32[10,6,512]{2,1,0:T(8,128)S(1)} %fusion.62, ...), kind=kLoop, calls=%fused_computation.78 | loop fusion | flops 2449408 | bytes 2175116 | tf_op jit(solution)/shard_map/reduce_sum | solution.py:642
  32.3 0.2 pad_slice_fusion.5
  32.5 0.1 fusion.57
  32.7 0.3 fusion.94
  33.0 0.3 fusion.39
  33.3 0.6 fusion.93
  33.9 0.0 copy-start.3
  33.9 0.5 fusion.2
  34.4 0.4 copy-done.3
  34.9 0.3 fusion.89
  35.1 0.3 fusion.92
  35.5 0.1 copy.64.rim_next_ref
  35.6 0.1 copy.63.rim_own_ref
  35.6 0.2 copy.62.main_ref
  35.9 35.6 %shard_map.157 = (f32[10,16,512]{2,1,0:T(8,128)S(1)}, f32[10,6,512]{2,1,0:T(8,128)S(1)}, f32[10,6,512]{2,1,0:T(8,128)S(1)}, f32[40,128]{1,0:T(8,128)S(1)}, f32[64,128]{1,0:T(8,128)S(1)}) custom-call(f32[10,16,512]{2,1,0:T(8,128)S(1)} %copy.62.main_ref, f32[10,6,512]{2,1,0:T(8,128)S(1)} %copy.63.rim_own_ref, f32[10,6,512]{2,1,0:T(8,128)S(1)} %copy.64.rim_next_ref, ...), custom_call_target="tpu_custom_call" | custom-call | tf_op jit(solution)/shard_map/pallas_call | solution.py:514
  71.5 0.1 fusion.91
  71.6 0.1 pad_add_fusion
  71.7 0.0 copy-start
  71.7 0.4 fusion.4
  72.1 0.0 copy-start.7
  72.1 0.0 copy-start.8
  72.1 0.5 copy-done
  72.6 0.1 copy-done.6
  72.8 0.0 copy-done.7
  72.8 0.0 copy-done.8
  72.8 1.2 %minimum_subtract_fusion = (f32[10,16,512]{2,1,0:T(8,128)}, f32[10,16,512]{2,1,0:T(8,128)}) fusion(f32[10]{0:T(128)S(1)} %copy-done.6, f32[10]{0:T(128)S(1)} %copy-done.7, f32[10,512]{1,0:T(8,128)S(1)} %subtract_subtract_fusion, f32[10,16,512]{2,0,1:T(8,128)S(1)} %fusion.4, f32[10]{0:T(128)S(1)} %copy-done.8, f32[10,16,512]{2,1,0:T(8,128)S(1)} %copy-done), kind=kLoop, calls=%fused_computation.75 | loop fusion | flops 1146880 | bytes 1331320 | tf_op jit(solution)/shard_map/sub | solution.py:657
  74.0 0.7 copy-done.5
  74.7 0.6 add_minimum_fusion
  (24 shorter events, 0.2 us)
Async XLA Ops:
  26.0 0.7 copy-start.11
  28.9 0.7 copy-start.10
  28.9 1.3 %copy-start.1 = (f32[10,16,512]{2,1,0:T(8,128)S(1)}, f32[10,16,512]{2,1,0:T(8,128)}, u32[]{:S(2)}) copy-start(f32[10,16,512]{2,1,0:T(8,128)} %param.13) | copy-start | bytes 983044
  28.9 1.3 %copy-start.2 = (f32[10,16,512]{2,1,0:T(8,128)S(1)}, f32[10,16,512]{2,1,0:T(8,128)}, u32[]{:S(2)}) copy-start(f32[10,16,512]{2,1,0:T(8,128)} %param.16) | copy-start | bytes 983044
  28.9 1.3 %copy-start.4 = (f32[16,512]{1,0:T(8,128)S(1)}, f32[16,512]{1,0:T(8,128)}, u32[]{:S(2)}) copy-start(f32[16,512]{1,0:T(8,128)} %param.15) | copy-start | bytes 98308
  29.6 0.7 copy-start.12
  30.2 0.7 copy-start.9
  33.9 1.0 %copy-start.3 = (f32[10,16,512]{2,1,0:T(8,128)S(1)}, f32[10,16,512]{2,1,0:T(8,128)}, u32[]{:S(2)}) copy-start(f32[10,16,512]{2,1,0:T(8,128)} %param.17) | copy-start | bytes 983044
  71.7 1.0 %copy-start = (f32[10,16,512]{2,1,0:T(8,128)S(1)}, f32[10,16,512]{2,1,0:T(8,128)}, u32[]{:S(2)}) copy-start(f32[10,16,512]{2,1,0:T(8,128)} %param.14) | copy-start | bytes 983044
  72.1 0.7 copy-start.6
  72.1 0.7 copy-start.7
  72.1 0.7 copy-start.8
  74.0 0.8 %copy-start.5 = (f32[16,512]{1,0:T(8,128)S(1)}, f32[16,512]{1,0:T(8,128)}, u32[]{:S(2)}) copy-start(f32[16,512]{1,0:T(8,128)} %param.18) | copy-start | bytes 98308

commit v13 on v9

--- a/solution.py
+++ b/solution.py
@@ -373,7 +373,6 @@
     @pl.when(has_down)
     def _():
         b_copy.start()
-        main_copy.start()
 
     @pl.when(has_after)
     def _():
@@ -404,6 +403,11 @@
 
         for s in range(1, job.inner):
             across(job, x_ref, near, s1, r1, lax.rem(job.i + s, job.inner), job.i).start()
+
+    @pl.when(has_down)
+    def _():
+        main_copy.start()
+
     parts = []
     for job, (x_ref, near, far, group, s1, r1, s2, r2) in zip(jobs, bufs):
         for s in range(1, job.inner):

time: 71.3 us -> 72.4 us (1.015)
  Pallas kernels: 55 us -> 56.1 us
    pallas_call x1, Pallas kernels: 32.4 us -> 33.5 us  [flow_exchange(): pl.pallas_call(flow_kernel, out_shape=[shape(main_next), shape(rim_own),...]
where the time goes in v13:
time: 72.4 us; the launch traced here: 72.1 us
  Pallas kernels  56.1 us (77%)
  other arithmetic  6.58 us (9%)
  local copies, waits for them, and re-layouts  4.87 us (7%)
  matrix products  3.51 us (5%)
  between operations  1.02 us (1%)
    pallas_call x1, Pallas kernels, flow_exchange(): pl.pallas_call(flow_kernel, out_shape=[shape(main_next), shape(rim_own),...  33.5 us
    pallas_call x1, Pallas kernels, dual_exchange(): pl.pallas_call(dual_kernel, out_shape=[jax.ShapeDtypeStruct(t.shape, t.dt...  22.6 us
    unnamed x26, local copies, waits for them, and re-layouts  4.04 us
    dot_general x4, matrix products, route_up(): jnp.einsum('ij,itw->jtw', matrix, field, precision=lax.Precision.HIGHEST)  1.83 us
    dot_general x4, matrix products, route_down(): jnp.einsum('ij,jtw->itw', matrix, field, precision=lax.Precision.HIGHEST)  1.69 us

profile of v13, /device:TPU:8, one launch (start us, length us, event | category | flops | bytes accessed | tf_op | source)
XLA Modules:
  0.0 72.1 jit_solution(10266943343615100880)
XLA Ops:
  0.6 1.2 %fusion.10 = f32[10,16,512]{2,0,1:T(8,128)S(1)} fusion(f32[10,16,512]{2,1,0:T(8,128)} %param.14), kind=kOutput, calls=%fused_computation.32 | output fusion | flops 1228800 | bytes 655360 | tf_op jit(solution)/shard_map/suffix_local/reduce_window_sum | solution.py:665
  1.8 0.2 copy.44.sloc_ref
  2.1 22.6 %shard_map.156 = (f32[40,128]{1,0:T(8,128)S(1)}, f32[40,128]{1,0:T(8,128)S(1)}, f32[10,16,512]{2,1,0:T(8,128)S(1)}, f32[10,6,512]{2,1,0:T(8,128)S(1)}, f32[10,6,512]{2,1,0:T(8,128)S(1)}) custom-call(f32[10,16,512]{2,1,0:T(8,128)S(1)} %copy.44.sloc_ref, f32[40,128]{1,0:T(8,128)S(1)} %reshape_squeeze.3.t_ref), custom_call_target="tpu_custom_call" | custom-call | tf_op jit(solution)/shard_map/pallas_call | solution.py:293
  24.7 0.1 broadcast_add_fusion.2
  24.8 0.0 copy-start.11
  24.8 0.6 copy-done.11
  25.5 0.4 fusion.53
  25.8 0.3 fusion.55
  26.1 0.2 fusion.62
  26.3 0.6 fusion.6
  27.0 0.2 broadcast_add_fusion.1
  27.2 0.6 fusion.8
  27.7 0.0 copy-start.10
  27.7 0.0 copy-start.1
  27.8 0.0 copy-start.2
  27.8 0.0 copy-start.4
  27.8 0.4 copy_add_fusion.2
  28.1 0.2 copy-done.10
  28.4 0.7 copy-done.12
  29.1 0.6 copy-done.9
  29.7 1.4 %multiply_reduce_fusion = (f32[16,512]{1,0:T(8,128)S(1)}, f32[10,16,512]{2,1,0:T(8,128)S(1)}, f32[10,16,512]{2,1,0:T(8,128)}) fusion(f32[10]{0:T(128)S(1)} %broadcast_multiply_fusion, f32[10,16,512]{2,1,0:T(8,128)S(1)} %copy-done.1, f32[16,512]{1,0:T(8,128)S(1)} %copy-done.4, f32[10,16,512]{2,1,0:T(8,128)S(1)} %copy-done.2, f32[10,6,512]{2,1,0:T(8,128)S(1)} %fusion.62, ...), kind=kLoop, calls=%fused_computation.78 | loop fusion | flops 2449408 | bytes 2175116 | tf_op jit(solution)/shard_map/reduce_sum | solution.py:644
  31.1 0.2 pad_slice_fusion.5
  31.4 0.1 fusion.57
  31.5 0.3 fusion.94
  31.8 0.3 fusion.39
  32.1 0.6 fusion.93
  32.7 0.0 copy-start.3
  32.7 0.5 fusion.2
  33.3 0.4 copy-done.3
  33.7 0.3 fusion.89
  34.0 0.3 fusion.92
  34.3 0.1 copy.64.rim_next_ref
  34.4 0.1 copy.63.rim_own_ref
  34.5 0.2 copy.62.main_ref
  34.7 33.5 %shard_map.157 = (f32[10,16,512]{2,1,0:T(8,128)S(1)}, f32[10,6,512]{2,1,0:T(8,128)S(1)}, f32[10,6,512]{2,1,0:T(8,128)S(1)}, f32[40,128]{1,0:T(8,128)S(1)}, f32[64,128]{1,0:T(8,128)S(1)}) custom-call(f32[10,16,512]{2,1,0:T(8,128)S(1)} %copy.62.main_ref, f32[10,6,512]{2,1,0:T(8,128)S(1)} %copy.63.rim_own_ref, f32[10,6,512]{2,1,0:T(8,128)S(1)} %copy.64.rim_next_ref, ...), custom_call_target="tpu_custom_call" | custom-call | tf_op jit(solution)/shard_map/pallas_call | solution.py:516
  68.2 0.1 fusion.91
  68.3 0.1 pad_add_fusion
  68.3 0.0 copy-start
  68.4 0.4 fusion.4
  68.8 0.0 copy-start.6
  68.8 0.0 copy-start.8
  68.8 0.5 copy-done
  69.3 0.1 copy-done.6
  69.5 0.0 copy-done.7
  69.5 0.0 copy-done.8
  69.5 1.2 %minimum_subtract_fusion = (f32[10,16,512]{2,1,0:T(8,128)}, f32[10,16,512]{2,1,0:T(8,128)}) fusion(f32[10]{0:T(128)S(1)} %copy-done.6, f32[10]{0:T(128)S(1)} %copy-done.7, f32[10,512]{1,0:T(8,128)S(1)} %subtract_subtract_fusion, f32[10,16,512]{2,0,1:T(8,128)S(1)} %fusion.4, f32[10]{0:T(128)S(1)} %copy-done.8, f32[10,16,512]{2,1,0:T(8,128)S(1)} %copy-done), kind=kLoop, calls=%fused_computation.75 | loop fusion | flops 1146880 | bytes 1331320 | tf_op jit(solution)/shard_map/sub | solution.py:659
  70.7 0.7 %copy-done.5 = f32[16,512]{1,0:T(8,128)S(1)} copy-done((f32[16,512]{1,0:T(8,128)S(1)}, f32[16,512]{1,0:T(8,128)}, u32[]{:S(2)}) %copy-start.5) | copy-done | bytes 32792
  71.4 0.6 add_minimum_fusion
  (24 shorter events, 0.2 us)
Async XLA Ops:
  24.8 0.7 copy-start.11
  27.7 0.7 copy-start.10
  27.7 1.3 %copy-start.1 = (f32[10,16,512]{2,1,0:T(8,128)S(1)}, f32[10,16,512]{2,1,0:T(8,128)}, u32[]{:S(2)}) copy-start(f32[10,16,512]{2,1,0:T(8,128)} %param.13) | copy-start | bytes 983044
  27.8 1.3 %copy-start.2 = (f32[10,16,512]{2,1,0:T(8,128)S(1)}, f32[10,16,512]{2,1,0:T(8,128)}, u32[]{:S(2)}) copy-start(f32[10,16,512]{2,1,0:T(8,128)} %param.16) | copy-start | bytes 983044
  27.8 1.3 %copy-start.4 = (f32[16,512]{1,0:T(8,128)S(1)}, f32[16,512]{1,0:T(8,128)}, u32[]{:S(2)}) copy-start(f32[16,512]{1,0:T(8,128)} %param.15) | copy-start | bytes 98308
  28.4 0.7 copy-start.12
  29.0 0.7 copy-start.9
  32.7 1.0 %copy-start.3 = (f32[10,16,512]{2,1,0:T(8,128)S(1)}, f32[10,16,512]{2,1,0:T(8,128)}, u32[]{:S(2)}) copy-start(f32[10,16,512]{2,1,0:T(8,128)} %param.17) | copy-start | bytes 983044
  68.3 1.0 %copy-start = (f32[10,16,512]{2,1,0:T(8,128)S(1)}, f32[10,16,512]{2,1,0:T(8,128)}, u32[]{:S(2)}) copy-start(f32[10,16,512]{2,1,0:T(8,128)} %param.14) | copy-start | bytes 983044
  68.8 0.7 copy-start.6
  68.8 0.7 copy-start.7
  68.8 0.7 copy-start.8
  70.7 0.8 %copy-start.5 = (f32[16,512]{1,0:T(8,128)S(1)}, f32[16,512]{1,0:T(8,128)}, u32[]{:S(2)}) copy-start(f32[16,512]{1,0:T(8,128)} %param.18) | copy-start | bytes 98308

commit v14 on v9

--- a/solution.py
+++ b/solution.py
@@ -615,9 +615,10 @@
     local = suffix_local(storage_dual)
     off, off_next, beyond, rim_own, rim_next = dual_exchange(local)
     suffix = local + off[:, None]
-    at_sink = route_up(to_own, suffix) + route_up(to_next, beyond + off_next[:, None])
+    both = jnp.concatenate([to_own, to_next], 0)
+    at_sink = route_up(both, jnp.concatenate([suffix, beyond + off_next[:, None]], 0))
     last = lax.axis_index("hours") == lax.axis_size("hours") - 1
-    rim_sink = route_up(to_own, rim_own + off[:, None]) + route_up(to_next, rim_next + off_next[:, None])
+    rim_sink = route_up(both, jnp.concatenate([rim_own + off[:, None], rim_next + off_next[:, None]], 0))
     later_duals = bring_forward(at_sink, travel_delay, jnp.where(last, 0.0, rim_sink))
     gradient = (
         cost
@@ -630,10 +631,11 @@
     tail = extrapolated[:, length - DMAX :]
     settled = hold_back(extrapolated, travel_delay, jnp.zeros_like(tail))
     rim_delayed = hold_back(jnp.zeros_like(extrapolated), travel_delay, tail)[:, :DMAX]
-    main_own = route_down(to_own, settled)
-    main_next = route_down(to_next, settled)
-    rim_own = route_down(to_own, rim_delayed)
-    rim_next = route_down(to_next, rim_delayed)
+    res = settled.shape[0]
+    main = route_down(both, settled)
+    main_own, main_next = main[:res], main[res:]
+    rims = route_down(both, rim_delayed)
+    rim_own, rim_next = rims[:res], rims[res:]
     base = inflow + main_own - extrapolated
     own_totals = jnp.sum(base, 1) + jnp.sum(rim_own, 1)
     next_totals = jnp.sum(main_next, 1) + jnp.sum(rim_next, 1)

time: 71.3 us -> 70.5 us (0.989)
  matrix products: 3.51 us -> 2.09 us
  local copies, waits for them, and re-layouts: 4.87 us -> 5.63 us
    unnamed x26 -> x29, local copies, waits for them, and re-layouts: 4.04 us -> 4.96 us
    dot_general x4 -> x2, matrix products: 1.69 us -> 0.95 us  [route_down(): jnp.einsum('ij,jtw->itw', matrix, field, precision=lax.Precision.HIGHEST)]
    dot_general x4 -> x2, matrix products: 1.83 us -> 1.14 us  [route_up(): jnp.einsum('ij,itw->jtw', matrix, field, precision=lax.Precision.HIGHEST)]
where the time goes in v14:
time: 70.5 us; the launch traced here: 70.1 us
  Pallas kernels  55 us (78%)
  other arithmetic  6.4 us (9%)
  local copies, waits for them, and re-layouts  5.63 us (8%)
  matrix products  2.09 us (3%)
  between operations  1.01 us (1%)
    pallas_call x1, Pallas kernels, flow_exchange(): pl.pallas_call(flow_kernel, out_shape=[shape(main_next), shape(rim_own),...  32.4 us
    pallas_call x1, Pallas kernels, dual_exchange(): pl.pallas_call(dual_kernel, out_shape=[jax.ShapeDtypeStruct(t.shape, t.dt...  22.6 us
    unnamed x29, local copies, waits for them, and re-layouts  4.96 us

profile of v14, /device:TPU:8, one launch (start us, length us, event | category | flops | bytes accessed | tf_op | source)
XLA Modules:
  0.0 70.1 jit_solution(12695650980456676806)
XLA Ops:
  0.6 1.2 %fusion.6 = f32[10,16,512]{2,0,1:T(8,128)S(1)} fusion(f32[10,16,512]{2,1,0:T(8,128)} %param.14), kind=kOutput, calls=%fused_computation.29 | output fusion | flops 1228800 | bytes 655360 | tf_op jit(solution)/shard_map/suffix_local/reduce_window_sum | solution.py:663
  1.8 0.2 copy.34.sloc_ref
  2.1 22.6 %shard_map.156 = (f32[40,128]{1,0:T(8,128)S(1)}, f32[40,128]{1,0:T(8,128)S(1)}, f32[10,16,512]{2,1,0:T(8,128)S(1)}, f32[10,6,512]{2,1,0:T(8,128)S(1)}, f32[10,6,512]{2,1,0:T(8,128)S(1)}) custom-call(f32[10,16,512]{2,1,0:T(8,128)S(1)} %copy.34.sloc_ref, f32[40,128]{1,0:T(8,128)S(1)} %reshape_squeeze.3.t_ref), custom_call_target="tpu_custom_call" | custom-call | tf_op jit(solution)/shard_map/pallas_call | solution.py:293
  24.7 0.1 broadcast_add_fusion.2
  24.8 0.0 copy-start.11
  24.8 0.6 copy-done.11
  25.5 0.1 iota_compare_fusion
  25.6 0.1 add_bitcast_fusion
  25.7 0.4 fusion.45
  26.0 0.1 copy_select_fusion
  26.1 0.2 broadcast_add_fusion
  26.4 0.1 pad_maximum_fusion
  26.5 0.8 %fusion = f32[10,16,512]{2,0,1:T(8,128)S(1)} fusion(pred[20,10,1]{0,1,2:T(8,128)(4,1)S(1)} %add_bitcast_fusion, f32[20,16,512]{2,1,0:T(8,128)S(1)} %pad_maximum_fusion), kind=kOutput, calls=%fused_computation.11 | convolution fusion | flops 19660800 | bytes 983240 | tf_op jit(solution)/shard_map/ij,itw->jtw/dot_general | solution.py:599
  27.2 0.0 copy-start.10
  27.2 0.0 copy-start.2
  27.3 0.0 copy-start.3
  27.3 0.0 copy-start.4
  27.3 0.2 copy.38
  27.5 0.4 copy-done.10
  27.9 0.7 copy-done.12
  28.6 0.6 copy-done.9
  29.2 1.2 %multiply_reduce_fusion = (f32[16,512]{1,0:T(8,128)S(1)}, f32[10,16,512]{2,1,0:T(8,128)S(1)}, f32[10,16,512]{2,1,0:T(8,128)}) fusion(f32[10]{0:T(128)S(1)} %broadcast_multiply_fusion, f32[10,16,512]{2,1,0:T(8,128)S(1)} %copy-done.2, f32[16,512]{1,0:T(8,128)S(1)} %copy-done.4, f32[10,16,512]{2,1,0:T(8,128)S(1)} %copy-done.3, ...), kind=kLoop, calls=%fused_computation.75 | loop fusion | flops 2367488 | bytes 2154636 | tf_op jit(solution)/shard_map/reduce_sum | solution.py:642
  30.5 0.2 pad_slice_fusion.5
  30.7 0.1 fusion.49
  30.8 0.3 fusion.47
  31.2 0.3 fusion.35
  31.5 0.6 fusion.4
  32.2 0.0 copy-start.1
  32.2 0.1 slice_reduce_fusion.2
  32.3 0.8 %copy-done.1 = f32[10,16,512]{2,1,0:T(8,128)S(1)} copy-done((f32[10,16,512]{2,1,0:T(8,128)S(1)}, f32[10,16,512]{2,1,0:T(8,128)}, u32[]{:S(2)}) %copy-start.1) | copy-done | bytes 327704
  33.1 0.3 fusion.55
  33.4 0.1 copy.49.rim_own_ref
  33.5 0.1 copy.50.rim_next_ref
  33.6 0.2 copy.48.main_ref
  33.8 32.4 %shard_map.157 = (f32[10,16,512]{2,1,0:T(8,128)S(1)}, f32[10,6,512]{2,1,0:T(8,128)S(1)}, f32[10,6,512]{2,1,0:T(8,128)S(1)}, f32[40,128]{1,0:T(8,128)S(1)}, f32[64,128]{1,0:T(8,128)S(1)}) custom-call(f32[10,16,512]{2,1,0:T(8,128)S(1)} %copy.48.main_ref, f32[10,6,512]{2,1,0:T(8,128)S(1)} %copy.49.rim_own_ref, f32[10,6,512]{2,1,0:T(8,128)S(1)} %copy.50.rim_next_ref, ...), custom_call_target="tpu_custom_call" | custom-call | tf_op jit(solution)/shard_map/pallas_call | solution.py:512
  66.2 0.1 fusion.57
  66.3 0.1 pad_add_fusion
  66.4 0.0 copy-start
  66.4 0.4 fusion.2
  66.8 0.0 copy-start.6
  66.8 0.0 copy-start.7
  66.9 0.5 copy-done
  67.4 0.1 copy-done.6
  67.5 0.0 copy-done.7
  67.5 0.0 copy-done.8
  67.5 1.2 %minimum_subtract_fusion = (f32[10,16,512]{2,1,0:T(8,128)}, f32[10,16,512]{2,1,0:T(8,128)}) fusion(f32[10]{0:T(128)S(1)} %copy-done.6, f32[10]{0:T(128)S(1)} %copy-done.7, f32[10,512]{1,0:T(8,128)S(1)} %subtract_subtract_fusion, f32[10,16,512]{2,0,1:T(8,128)S(1)} %fusion.2, f32[10]{0:T(128)S(1)} %copy-done.8, f32[10,16,512]{2,1,0:T(8,128)S(1)} %copy-done), kind=kLoop, calls=%fused_computation.72 | loop fusion | flops 1146880 | bytes 1331320 | tf_op jit(solution)/shard_map/sub | solution.py:657
  68.7 0.7 %copy-done.5 = f32[16,512]{1,0:T(8,128)S(1)} copy-done((f32[16,512]{1,0:T(8,128)S(1)}, f32[16,512]{1,0:T(8,128)}, u32[]{:S(2)}) %copy-start.5) | copy-done | bytes 32792
  69.5 0.6 add_minimum_fusion
  (25 shorter events, 0.2 us)
Async XLA Ops:
  24.8 0.7 copy-start.11
  27.2 0.7 copy-start.10
  27.2 1.3 %copy-start.2 = (f32[10,16,512]{2,1,0:T(8,128)S(1)}, f32[10,16,512]{2,1,0:T(8,128)}, u32[]{:S(2)}) copy-start(f32[10,16,512]{2,1,0:T(8,128)} %param.13) | copy-start | bytes 983044
  27.3 1.3 %copy-start.3 = (f32[10,16,512]{2,1,0:T(8,128)S(1)}, f32[10,16,512]{2,1,0:T(8,128)}, u32[]{:S(2)}) copy-start(f32[10,16,512]{2,1,0:T(8,128)} %param.16) | copy-start | bytes 983044
  27.3 1.3 %copy-start.4 = (f32[16,512]{1,0:T(8,128)S(1)}, f32[16,512]{1,0:T(8,128)}, u32[]{:S(2)}) copy-start(f32[16,512]{1,0:T(8,128)} %param.15) | copy-start | bytes 98308
  27.9 0.7 copy-start.12
  28.6 0.7 copy-start.9
  32.2 1.0 %copy-start.1 = (f32[10,16,512]{2,1,0:T(8,128)S(1)}, f32[10,16,512]{2,1,0:T(8,128)}, u32[]{:S(2)}) copy-start(f32[10,16,512]{2,1,0:T(8,128)} %param.17) | copy-start | bytes 983044
  66.4 1.0 %copy-start = (f32[10,16,512]{2,1,0:T(8,128)S(1)}, f32[10,16,512]{2,1,0:T(8,128)}, u32[]{:S(2)}) copy-start(f32[10,16,512]{2,1,0:T(8,128)} %param.14) | copy-start | bytes 983044
  66.8 0.7 copy-start.6
  66.8 0.7 copy-start.7
  66.8 0.7 copy-start.8
  68.7 0.8 %copy-start.5 = (f32[16,512]{1,0:T(8,128)S(1)}, f32[16,512]{1,0:T(8,128)}, u32[]{:S(2)}) copy-start(f32[16,512]{1,0:T(8,128)} %param.18) | copy-start | bytes 98308

commit v15 on v14

--- a/solution.py
+++ b/solution.py
@@ -133,10 +133,17 @@
 
 
 def dual_kernel(
-    sloc_ref, t_ref, off_ref, off_next_ref, beyond_ref, rim_own_ref, rim_next_ref,
-    near, far, group, beyond_buf, rim_src_own, rim_src_next, rim_own_buf, rim_next_buf,
-    off_src, off_next_buf, s1, r1, s2, r2, sems,
+    sloc_ref, t_ref, *refs,
 ):
+    count = (len(refs) - 21) // 2
+    held_in, refs = refs[:count], refs[count:]
+    off_ref, off_next_ref, beyond_ref, rim_own_ref, rim_next_ref = refs[:5]
+    held_out, refs = refs[5:5 + count], refs[5 + count:]
+    (near, far, group, beyond_buf, rim_src_own, rim_src_next, rim_own_buf, rim_next_buf,
+     off_src, off_next_buf, s1, r1, s2, r2, sems, local) = refs
+    fetches = [pltpu.make_async_copy(a, b, local.at[k]) for k, (a, b) in enumerate(zip(held_in, held_out))]
+    for fetch in fetches:
+        fetch.start()
     job = Job("hours", "suffix", 8, lax.axis_size("hours"))
     job.place()
     n_r = lax.axis_size("river")
@@ -282,15 +289,18 @@
         off_next_ref[...] = jnp.zeros_like(off_next_ref)
         beyond_ref[...] = jnp.zeros_like(beyond_ref)
 
-
-def dual_exchange(sloc):
+    for fetch in fetches:
+        fetch.wait()
+
+
+def dual_exchange(sloc, held):
     res, length, width = sloc.shape
     t = sloc[:, 0].reshape(-1, 128)
     inner = 8
     outer = lax.axis_size("hours") // inner
     rim = (res, DMAX, width)
     vmem = pl.BlockSpec(memory_space=pltpu.VMEM)
-    off, off_next, beyond, rim_own, rim_next = pl.pallas_call(
+    outs = pl.pallas_call(
         dual_kernel,
         out_shape=[
             jax.ShapeDtypeStruct(t.shape, t.dtype),
@@ -298,9 +308,9 @@
             jax.ShapeDtypeStruct(sloc.shape, sloc.dtype),
             jax.ShapeDtypeStruct(rim, sloc.dtype),
             jax.ShapeDtypeStruct(rim, sloc.dtype),
-        ],
-        in_specs=[vmem, vmem],
-        out_specs=[vmem] * 5,
+        ] + [jax.ShapeDtypeStruct(a.shape, a.dtype) for a in held],
+        in_specs=[vmem, vmem] + [pl.BlockSpec(memory_space=pl.ANY)] * len(held),
+        out_specs=[vmem] * (5 + len(held)),
         scratch_shapes=[
             pltpu.VMEM((inner,) + t.shape, t.dtype),
             pltpu.VMEM((outer,) + t.shape, t.dtype),
@@ -317,10 +327,12 @@
             pltpu.SemaphoreType.DMA((outer,)),
             pltpu.SemaphoreType.DMA((outer,)),
             pltpu.SemaphoreType.DMA((8,)),
+            pltpu.SemaphoreType.DMA((len(held),)),
         ],
         compiler_params=pltpu.CompilerParams(collective_id=0, has_side_effects=True, vmem_limit_bytes=48 * 1024 * 1024),
-    )(sloc, t)
-    return off.reshape(res, width), off_next.reshape(res, width), beyond, rim_own, rim_next
+    )(sloc, t, *held)
+    off, off_next, beyond, rim_own, rim_next = outs[:5]
+    return off.reshape(res, width), off_next.reshape(res, width), beyond, rim_own, rim_next, outs[5:]
 
 
 def flow_kernel(
@@ -613,7 +625,8 @@
     ) = statics
     scale_time, scale_sum = scales
     local = suffix_local(storage_dual)
-    off, off_next, beyond, rim_own, rim_next = dual_exchange(local)
+    off, off_next, beyond, rim_own, rim_next, held = dual_exchange(local, [release, cost, inflow, storage_dual])
+    release, cost, inflow, storage_dual = held
     suffix = local + off[:, None]
     both = jnp.concatenate([to_own, to_next], 0)
     at_sink = route_up(both, jnp.concatenate([suffix, beyond + off_next[:, None]], 0))

time: 70.5 us -> 70.7 us (level)
  no operation moved by 1% of the time
where the time goes in v15:
time: 70.7 us; the launch traced here: 70.3 us
  Pallas kernels  55.4 us (78%)
  other arithmetic  6.41 us (9%)
  local copies, waits for them, and re-layouts  5.38 us (8%)
  matrix products  2.09 us (3%)
  between operations  1.01 us (1%)
    pallas_call x1, Pallas kernels, flow_exchange(): pl.pallas_call(flow_kernel, out_shape=[shape(main_next), shape(rim_own),...  32.4 us
    pallas_call x1, Pallas kernels, dual_exchange(): pl.pallas_call(dual_kernel, out_shape=[jax.ShapeDtypeStruct(t.shape, t.dt...  23.1 us
    unnamed x29, local copies, waits for them, and re-layouts  4.71 us

profile of v15, /device:TPU:8, one launch (start us, length us, event | category | flops | bytes accessed | tf_op | source)
XLA Modules:
  0.0 70.3 jit_solution(7028276972565674544)
XLA Ops:
  0.6 0.0 copy-start.12
  0.6 0.6 copy-done.12
  1.3 0.7 copy-done.11
  2.0 0.7 copy-done.10
  2.6 0.1 iota_compare_fusion
  2.7 0.1 add_bitcast_fusion
  2.8 1.3 %fusion.6 = f32[10,16,512]{2,0,1:T(8,128)S(1)} fusion(f32[10,16,512]{2,1,0:T(8,128)} %refs_3_.1), kind=kOutput, calls=%fused_computation.29 | output fusion | flops 1228800 | bytes 655360 | tf_op jit(solution)/shard_map/suffix_local/reduce_window_sum | solution.py:676
  4.1 0.0 copy-start
  4.1 0.0 copy-start.1
  4.1 0.2 copy.33.sloc_ref
  4.3 0.0 copy-done.2
  4.3 0.7 %copy-done = f32[10,16,512]{2,1,0:T(8,128)S(1)} copy-done((f32[10,16,512]{2,1,0:T(8,128)S(1)}, f32[10,16,512]{2,1,0:T(8,128)}, u32[]{:S(2)}) %copy-start) | copy-done | bytes 327704
  5.1 0.1 copy-done.1
  5.2 23.1 %shard_map.156 = (f32[40,128]{1,0:T(8,128)S(1)}, f32[40,128]{1,0:T(8,128)S(1)}, f32[10,16,512]{2,1,0:T(8,128)S(1)}, f32[10,6,512]{2,1,0:T(8,128)S(1)}, f32[10,6,...) custom-call(f32[10,16,512]{2,1,0:T(8,128)S(1)} %copy.33.sloc_ref, ...), custom_call_target="tpu_custom_call" | custom-call | tf_op jit(solution)/shard_map/pallas_call | solution.py:303
  28.3 0.2 broadcast_add_fusion
  28.6 0.4 fusion.45
  29.0 0.1 copy_select_fusion
  29.1 0.1 pad_maximum_fusion
  29.1 0.8 %fusion = f32[10,16,512]{2,0,1:T(8,128)S(1)} fusion(pred[20,10,1]{0,1,2:T(8,128)(4,1)S(1)} %add_bitcast_fusion, f32[20,16,512]{2,1,0:T(8,128)S(1)} %pad_maximum_fusion), kind=kOutput, calls=%fused_computation.11 | convolution fusion | flops 19660800 | bytes 983240 | tf_op jit(solution)/shard_map/ij,itw->jtw/dot_general | solution.py:611
  29.9 0.0 copy-start.4
  29.9 0.0 copy-start.9
  29.9 0.2 copy.38
  30.1 0.5 copy-done.4
  30.7 1.2 %multiply_reduce_fusion = (f32[16,512]{1,0:T(8,128)S(1)}, f32[10,16,512]{2,1,0:T(8,128)S(1)}, f32[10,16,512]{2,1,0:T(8,128)}) fusion(f32[10]{0:T(128)S(1)} %broadcast_multiply_fusion, f32[10,16,512]{2,1,0:T(8,128)S(1)} %get-tuple-element.18, f32[16,512]{1,0:T(8,128)S(1)} %copy-done.4, f32[10,16,512]{2,1,0:T(8,128)S(1)} %get-tuple-element.19, ...), kind=kLoop, calls=%fused_computation.75 | loop fusion | flops 2367488 | bytes 2154636 | tf_op jit(solution)/shard_map/reduce_sum | solution.py:655
  31.9 0.3 fusion.35
  32.2 0.6 fusion.4
  32.9 0.1 slice_reduce_fusion.2
  33.0 0.3 fusion.55
  33.3 0.2 copy.48.main_ref
  33.5 0.2 pad_slice_fusion.5
  33.7 0.1 fusion.49
  33.9 0.3 fusion.47
  34.3 0.1 copy.49.rim_own_ref
  34.4 0.1 copy.50.rim_next_ref
  34.5 32.4 %shard_map.157 = (f32[10,16,512]{2,1,0:T(8,128)S(1)}, f32[10,6,512]{2,1,0:T(8,128)S(1)}, f32[10,6,512]{2,1,0:T(8,128)S(1)}, f32[40,128]{1,0:T(8,128)S(1)}, f32[64,128]{1,0:T(8,128)S(1)}) custom-call(f32[10,16,512]{2,1,0:T(8,128)S(1)} %copy.48.main_ref, f32[10,6,512]{2,1,0:T(8,128)S(1)} %copy.49.rim_own_ref, f32[10,6,512]{2,1,0:T(8,128)S(1)} %copy.50.rim_next_ref, ...), custom_call_target="tpu_custom_call" | custom-call | tf_op jit(solution)/shard_map/pallas_call | solution.py:524
  66.9 0.0 copy-start.5
  66.9 0.7 %copy-done.5 = f32[16,512]{1,0:T(8,128)S(1)} copy-done((f32[16,512]{1,0:T(8,128)S(1)}, f32[16,512]{1,0:T(8,128)}, u32[]{:S(2)}) %copy-start.5) | copy-done | bytes 32792
  67.6 0.6 add_minimum_fusion
  68.2 0.1 fusion.57
  68.4 0.1 pad_add_fusion
  68.4 0.0 copy-start.6
  68.5 0.0 copy-start.7
  68.5 0.0 copy-start.8
  68.5 0.4 fusion.2
  68.9 0.2 copy-done.6
  69.1 0.0 copy-done.7
  69.1 0.0 copy-done.8
  69.1 1.2 %minimum_subtract_fusion = (f32[10,16,512]{2,1,0:T(8,128)}, f32[10,16,512]{2,1,0:T(8,128)}) fusion(f32[10]{0:T(128)S(1)} %copy-done.6, f32[10]{0:T(128)S(1)} %copy-done.7, f32[10,512]{1,0:T(8,128)S(1)} %subtract_subtract_fusion, f32[10,16,512]{2,0,1:T(8,128)S(1)} %fusion.2, f32[10]{0:T(128)S(1)} %copy-done.8, f32[10,16,512]{2,1,0:T(8,128)S(1)} %get-tuple-element.25), kind=kLoop, calls=%fused_computation.72 | loop fusion | flops 1146880 | bytes 1331320 | tf_op jit(solution)/shard_map/sub | solution.py:670
  (25 shorter events, 0.2 us)
Async XLA Ops:
  0.6 0.7 copy-start.12
  1.3 0.7 copy-start.11
  2.0 0.7 copy-start.10
  2.8 1.5 %copy-start.2 = (f32[10,16,512]{2,1,0:T(8,128)S(1)}, f32[10,16,512]{2,1,0:T(8,128)}, u32[]{:S(2)}) copy-start(f32[10,16,512]{2,1,0:T(8,128)} %refs_1_.1) | copy-start | bytes 983044
  2.8 1.5 %copy-start.3 = (f32[10,16,512]{2,1,0:T(8,128)S(1)}, f32[10,16,512]{2,1,0:T(8,128)}, u32[]{:S(2)}) copy-start(f32[10,16,512]{2,1,0:T(8,128)} %refs_2_.1) | copy-start | bytes 983044
  4.1 1.0 %copy-start = (f32[10,16,512]{2,1,0:T(8,128)S(1)}, f32[10,16,512]{2,1,0:T(8,128)}, u32[]{:S(2)}) copy-start(f32[10,16,512]{2,1,0:T(8,128)} %refs_3_.1) | copy-start | bytes 983044
  4.1 1.1 %copy-start.1 = (f32[10,16,512]{2,1,0:T(8,128)S(1)}, f32[10,16,512]{2,1,0:T(8,128)}, u32[]{:S(2)}) copy-start(f32[10,16,512]{2,1,0:T(8,128)} %refs_0_.1) | copy-start | bytes 983044
  29.9 0.8 %copy-start.4 = (f32[16,512]{1,0:T(8,128)S(1)}, f32[16,512]{1,0:T(8,128)}, u32[]{:S(2)}) copy-start(f32[16,512]{1,0:T(8,128)} %param.15) | copy-start | bytes 98308
  29.9 0.8 %copy-start.9 = (f32[10]{0:T(128)S(1)}, f32[10]{0:T(128)}, u32[]{:S(2)}) copy-start(f32[10]{0:T(128)} %param.22) | copy-start | bytes 124
  66.9 0.8 %copy-start.5 = (f32[16,512]{1,0:T(8,128)S(1)}, f32[16,512]{1,0:T(8,128)}, u32[]{:S(2)}) copy-start(f32[16,512]{1,0:T(8,128)} %param.18) | copy-start | bytes 98308
  68.4 0.7 copy-start.6
  68.5 0.7 copy-start.7
  68.5 0.7 copy-start.8

commit v16 on v14

--- a/solution.py
+++ b/solution.py
@@ -616,9 +616,19 @@
     off, off_next, beyond, rim_own, rim_next = dual_exchange(local)
     suffix = local + off[:, None]
     both = jnp.concatenate([to_own, to_next], 0)
-    at_sink = route_up(both, jnp.concatenate([suffix, beyond + off_next[:, None]], 0))
+    length = suffix.shape[1]
+    sinks = route_up(
+        both,
+        jnp.concatenate(
+            [
+                jnp.concatenate([suffix, rim_own + off[:, None]], 1),
+                jnp.concatenate([beyond + off_next[:, None], rim_next + off_next[:, None]], 1),
+            ],
+            0,
+        ),
+    )
+    at_sink, rim_sink = sinks[:, :length], sinks[:, length:]
     last = lax.axis_index("hours") == lax.axis_size("hours") - 1
-    rim_sink = route_up(both, jnp.concatenate([rim_own + off[:, None], rim_next + off_next[:, None]], 0))
     later_duals = bring_forward(at_sink, travel_delay, jnp.where(last, 0.0, rim_sink))
     gradient = (
         cost
@@ -632,10 +642,9 @@
     settled = hold_back(extrapolated, travel_delay, jnp.zeros_like(tail))
     rim_delayed = hold_back(jnp.zeros_like(extrapolated), travel_delay, tail)[:, :DMAX]
     res = settled.shape[0]
-    main = route_down(both, settled)
-    main_own, main_next = main[:res], main[res:]
-    rims = route_down(both, rim_delayed)
-    rim_own, rim_next = rims[:res], rims[res:]
+    routed_all = route_down(both, jnp.concatenate([settled, rim_delayed], 1))
+    main_own, main_next = routed_all[:res, :length], routed_all[res:, :length]
+    rim_own, rim_next = routed_all[:res, length:], routed_all[res:, length:]
     base = inflow + main_own - extrapolated
     own_totals = jnp.sum(base, 1) + jnp.sum(rim_own, 1)
     next_totals = jnp.sum(main_next, 1) + jnp.sum(rim_next, 1)

time: 70.5 us -> 68.5 us (0.972)
  local copies, waits for them, and re-layouts: 5.63 us -> 3.32 us
    unnamed x29 -> x28, local copies, waits for them, and re-layouts: 4.96 us -> 2.8 us
where the time goes in v16:
time: 68.5 us; the launch traced here: 68.2 us
  Pallas kernels  55 us (80%)
  other arithmetic  6.99 us (10%)
  local copies, waits for them, and re-layouts  3.32 us (5%)
  matrix products  1.88 us (3%)
  between operations  1.02 us (1%)
    pallas_call x1, Pallas kernels, flow_exchange(): pl.pallas_call(flow_kernel, out_shape=[shape(main_next), shape(rim_own),...  32.4 us
    pallas_call x1, Pallas kernels, dual_exchange(): pl.pallas_call(dual_kernel, out_shape=[jax.ShapeDtypeStruct(t.shape, t.dt...  22.6 us
    unnamed x28, local copies, waits for them, and re-layouts  2.8 us

profile of v16, /device:TPU:8, one launch (start us, length us, event | category | flops | bytes accessed | tf_op | source)
XLA Modules:
  0.0 68.2 jit_solution(3026599628944524156)
XLA Ops:
  0.6 0.7 broadcast_multiply_fusion
  1.3 1.2 %fusion.6 = f32[10,16,512]{2,0,1:T(8,128)S(1)} fusion(f32[10,16,512]{2,1,0:T(8,128)} %param.14), kind=kOutput, calls=%fused_computation.29 | output fusion | flops 1228800 | bytes 655360 | tf_op jit(solution)/shard_map/suffix_local/reduce_window_sum | solution.py:672
  2.5 0.2 copy.32.sloc_ref
  2.7 22.6 %shard_map.156 = (f32[40,128]{1,0:T(8,128)S(1)}, f32[40,128]{1,0:T(8,128)S(1)}, f32[10,16,512]{2,1,0:T(8,128)S(1)}, f32[10,6,512]{2,1,0:T(8,128)S(1)}, f32[10,6,512]{2,1,0:T(8,128)S(1)}) custom-call(f32[10,16,512]{2,1,0:T(8,128)S(1)} %copy.32.sloc_ref, f32[40,128]{1,0:T(8,128)S(1)} %reshape_squeeze.3.t_ref), custom_call_target="tpu_custom_call" | custom-call | tf_op jit(solution)/shard_map/pallas_call | solution.py:293
  25.4 0.2 broadcast_add_fusion
  25.7 0.0 copy-start.11
  25.7 0.1 maximum_maximum_fusion
  25.8 0.5 copy-done.11
  26.3 0.1 iota_compare_fusion
  26.4 1.0 %fusion = f32[10,22,512]{2,0,1:T(8,128)S(1)} fusion(f32[20,22,512]{2,1,0:T(8,128)S(1)} %maximum_maximum_fusion, pred[10,10]{0,1:T(8,128)(4,1)S(1)} %get-tuple-element.54, pred[10,10]{0,1:T(8,128)(4,1)S(1)} %get-tuple-element.53), kind=kOutput, calls=%fused_computation.6 | convolution fusion | flops 27033800 | bytes 1351880 | tf_op jit(solution)/shard_map/ij,itw->jtw/dot_general | solution.py:599
  27.5 0.0 copy-start.10
  27.5 0.0 copy-start.2
  27.5 0.0 copy-start.3
  27.5 0.0 copy-start.4
  27.5 0.0 copy-start.9
  27.5 0.1 copy_select_fusion
  27.7 0.2 copy.43
  27.9 0.3 copy-done.10
  28.1 0.3 copy-done.2
  28.5 0.1 copy-done.3
  28.6 0.0 copy-done.4
  28.6 0.0 copy-done.9
  28.6 1.2 %multiply_reduce_fusion = (f32[16,512]{1,0:T(8,128)S(1)}, f32[10,16,512]{2,1,0:T(8,128)S(1)}, f32[10,16,512]{2,1,0:T(8,128)}) fusion(f32[10]{0:T(128)S(1)} %broadcast_multiply_fusion, f32[10,16,512]{2,1,0:T(8,128)S(1)} %copy-done.2, f32[16,512]{1,0:T(8,128)S(1)} %copy-done.4, f32[10,16,512]{2,1,0:T(8,128)S(1)} %copy-done.3, ...), kind=kLoop, calls=%fused_computation.75 | loop fusion | flops 2367488 | bytes 2154636 | tf_op jit(solution)/shard_map/reduce_sum | solution.py:651
  29.8 0.2 pad_slice_fusion.5
  30.1 0.1 fusion.45
  30.2 0.3 fusion.35
  30.6 0.9 %fusion.2 = f32[20,22,512]{2,0,1:T(8,128)S(1)} fusion(f32[10,22,512]{2,1,0:T(8,128)S(1)} %pad_maximum_fusion, pred[10,10]{0,1:T(8,128)(4,1)S(1)} %get-tuple-element.54, pred[10,10]{0,1:T(8,128)(4,1)S(1)} %get-tuple-element.53), kind=kOutput, calls=%fused_computation.20 | convolution fusion | flops 27033800 | bytes 1351880 | tf_op jit(solution)/shard_map/ij,jtw->itw/dot_general | solution.py:595
  31.4 0.1 slice_reduce_fusion.2
  31.6 0.0 copy-start.1
  31.6 0.2 copy.46.main_ref
  31.8 0.1 copy.47.rim_own_ref
  31.9 0.1 copy.48.rim_next_ref
  32.0 0.5 copy-done.1
  32.5 0.3 fusion.51
  32.9 32.4 %shard_map.157 = (f32[10,16,512]{2,1,0:T(8,128)S(1)}, f32[10,6,512]{2,1,0:T(8,128)S(1)}, f32[10,6,512]{2,1,0:T(8,128)S(1)}, f32[40,128]{1,0:T(8,128)S(1)}, f32[64,128]{1,0:T(8,128)S(1)}) custom-call(f32[10,16,512]{2,1,0:T(8,128)S(1)} %copy.46.main_ref, f32[10,6,512]{2,1,0:T(8,128)S(1)} %copy.47.rim_own_ref, f32[10,6,512]{2,1,0:T(8,128)S(1)} %copy.48.rim_next_ref, ...), custom_call_target="tpu_custom_call" | custom-call | tf_op jit(solution)/shard_map/pallas_call | solution.py:512
  65.3 0.1 fusion.53
  65.4 0.0 copy-start
  65.4 0.0 copy-start.6
  65.4 0.0 copy-start.7
  65.4 0.0 copy-start.8
  65.5 0.1 pad_add_fusion
  65.5 0.0 copy-start.5
  65.5 0.4 fusion.4
  65.9 0.4 copy-done
  66.4 0.0 copy-done.6
  66.4 0.0 copy-done.7
  66.4 1.2 %minimum_subtract_fusion = (f32[10,16,512]{2,1,0:T(8,128)}, f32[10,16,512]{2,1,0:T(8,128)}) fusion(f32[10]{0:T(128)S(1)} %copy-done.6, f32[10]{0:T(128)S(1)} %copy-done.7, f32[10,512]{1,0:T(8,128)S(1)} %subtract_subtract_fusion, f32[10,16,512]{2,0,1:T(8,128)S(1)} %fusion.4, f32[10]{0:T(128)S(1)} %copy-done.8, f32[10,16,512]{2,1,0:T(8,128)S(1)} %copy-done), kind=kLoop, calls=%fused_computation.72 | loop fusion | flops 1146880 | bytes 1331320 | tf_op jit(solution)/shard_map/sub | solution.py:666
  67.6 0.6 add_minimum_fusion
  (22 shorter events, 0.3 us)
Async XLA Ops:
  25.7 0.7 copy-start.11
  27.5 0.7 copy-start.10
  27.5 1.0 %copy-start.2 = (f32[10,16,512]{2,1,0:T(8,128)S(1)}, f32[10,16,512]{2,1,0:T(8,128)}, u32[]{:S(2)}) copy-start(f32[10,16,512]{2,1,0:T(8,128)} %param.13) | copy-start | bytes 983044
  27.5 1.1 %copy-start.3 = (f32[10,16,512]{2,1,0:T(8,128)S(1)}, f32[10,16,512]{2,1,0:T(8,128)}, u32[]{:S(2)}) copy-start(f32[10,16,512]{2,1,0:T(8,128)} %param.16) | copy-start | bytes 983044
  27.5 1.1 %copy-start.4 = (f32[16,512]{1,0:T(8,128)S(1)}, f32[16,512]{1,0:T(8,128)}, u32[]{:S(2)}) copy-start(f32[16,512]{1,0:T(8,128)} %param.15) | copy-start | bytes 98308
  27.5 1.0 %copy-start.9 = (f32[10]{0:T(128)S(1)}, f32[10]{0:T(128)}, u32[]{:S(2)}) copy-start(f32[10]{0:T(128)} %param.22) | copy-start | bytes 124
  31.6 1.0 %copy-start.1 = (f32[10,16,512]{2,1,0:T(8,128)S(1)}, f32[10,16,512]{2,1,0:T(8,128)}, u32[]{:S(2)}) copy-start(f32[10,16,512]{2,1,0:T(8,128)} %param.17) | copy-start | bytes 983044
  65.4 1.0 %copy-start = (f32[10,16,512]{2,1,0:T(8,128)S(1)}, f32[10,16,512]{2,1,0:T(8,128)}, u32[]{:S(2)}) copy-start(f32[10,16,512]{2,1,0:T(8,128)} %param.14) | copy-start | bytes 983044
  65.4 1.0 %copy-start.6 = (f32[10]{0:T(128)S(1)}, f32[10]{0:T(128)}, u32[]{:S(2)}) copy-start(f32[10]{0:T(128)} %param.20) | copy-start | bytes 124
  65.4 1.0 %copy-start.7 = (f32[10]{0:T(128)S(1)}, f32[10]{0:T(128)}, u32[]{:S(2)}) copy-start(f32[10]{0:T(128)} %param.21) | copy-start | bytes 124
  65.4 0.9 %copy-start.8 = (f32[10]{0:T(128)S(1)}, f32[10]{0:T(128)}, u32[]{:S(2)}) copy-start(f32[10]{0:T(128)} %param.19) | copy-start | bytes 124
  65.5 2.0 %copy-start.5 = (f32[16,512]{1,0:T(8,128)S(1)}, f32[16,512]{1,0:T(8,128)}, u32[]{:S(2)}) copy-start(f32[16,512]{1,0:T(8,128)} %param.18) | copy-start | bytes 98308

commit v17 on v16

--- a/solution.py
+++ b/solution.py
@@ -646,15 +646,16 @@
     main_own, main_next = routed_all[:res, :length], routed_all[res:, :length]
     rim_own, rim_next = routed_all[:res, length:], routed_all[res:, length:]
     base = inflow + main_own - extrapolated
-    own_totals = jnp.sum(base, 1) + jnp.sum(rim_own, 1)
-    next_totals = jnp.sum(main_next, 1) + jnp.sum(rim_next, 1)
+    own_totals = jnp.sum(inflow - extrapolated, 1) + jnp.sum(routed_all[:res], 1)
+    next_totals = jnp.sum(routed_all[res:], 1)
     partial_power = jnp.sum(scale_sum * efficiency[:, None, None] * extrapolated, 0)
     incoming, rim_own_in, rim_next_in, offset, supplied = flow_exchange(
         main_next, rim_own, rim_next, own_totals, next_totals, partial_power
     )
-    arrived = jnp.concatenate([rim_own_in + rim_next_in, jnp.zeros_like(base[:, DMAX:])], 1)
+    landed = rim_own_in + rim_next_in
+    arrived = jnp.concatenate([landed, jnp.zeros_like(base[:, DMAX:])], 1)
     local_sum = jnp.cumsum(base + incoming + arrived, 1)
-    offset = offset - jnp.sum(rim_own_in, 1) - jnp.sum(rim_next_in, 1)
+    offset = offset - jnp.sum(landed, 1)
     storage = storage_start[:, None, None] + scale_time * (local_sum + offset[:, None])
     lower_bound = storage_low[:, None, None]
     upper_bound = storage_high[:, None, None]

time: 68.5 us -> 67.1 us (0.980)
    unnamed x28 -> x30, local copies, waits for them, and re-layouts: 2.8 us -> 2.06 us
where the time goes in v17:
time: 67.1 us; the launch traced here: 66.9 us
  Pallas kernels  55 us (82%)
  other arithmetic  6.33 us (9%)
  local copies, waits for them, and re-layouts  2.68 us (4%)
  matrix products  1.88 us (3%)
  between operations  1.03 us (2%)
    pallas_call x1, Pallas kernels, flow_exchange(): pl.pallas_call(flow_kernel, out_shape=[shape(main_next), shape(rim_own),...  32.4 us
    pallas_call x1, Pallas kernels, dual_exchange(): pl.pallas_call(dual_kernel, out_shape=[jax.ShapeDtypeStruct(t.shape, t.dt...  22.6 us
    unnamed x30, local copies, waits for them, and re-layouts  2.06 us

profile of v17, /device:TPU:8, one launch (start us, length us, event | category | flops | bytes accessed | tf_op | source)
XLA Modules:
  0.0 66.9 jit_solution(3333063767481177977)
XLA Ops:
  0.6 1.2 %fusion.6 = f32[10,16,512]{2,0,1:T(8,128)S(1)} fusion(f32[10,16,512]{2,1,0:T(8,128)} %param.14), kind=kOutput, calls=%fused_computation.31 | output fusion | flops 1228800 | bytes 655360 | tf_op jit(solution)/shard_map/suffix_local/reduce_window_sum | solution.py:673
  1.8 0.2 copy.32.sloc_ref
  2.1 22.6 %shard_map.156 = (f32[40,128]{1,0:T(8,128)S(1)}, f32[40,128]{1,0:T(8,128)S(1)}, f32[10,16,512]{2,1,0:T(8,128)S(1)}, f32[10,6,512]{2,1,0:T(8,128)S(1)}, f32[10,6,512]{2,1,0:T(8,128)S(1)}) custom-call(f32[10,16,512]{2,1,0:T(8,128)S(1)} %copy.32.sloc_ref, f32[40,128]{1,0:T(8,128)S(1)} %reshape_squeeze.3.t_ref), custom_call_target="tpu_custom_call" | custom-call | tf_op jit(solution)/shard_map/pallas_call | solution.py:293
  24.8 0.2 broadcast_add_fusion
  25.0 0.0 copy-start.11
  25.0 0.1 maximum_maximum_fusion
  25.1 0.5 copy-done.11
  25.7 0.1 iota_compare_fusion
  25.8 1.0 %fusion = f32[10,22,512]{2,0,1:T(8,128)S(1)} fusion(f32[20,22,512]{2,1,0:T(8,128)S(1)} %maximum_maximum_fusion, pred[10,10]{0,1:T(8,128)(4,1)S(1)} %get-tuple-element.51, pred[10,10]{0,1:T(8,128)(4,1)S(1)} %get-tuple-element.50), kind=kOutput, calls=%fused_computation.6 | convolution fusion | flops 27033800 | bytes 1351880 | tf_op jit(solution)/shard_map/ij,itw->jtw/dot_general | solution.py:599
  26.8 0.0 copy-start.10
  26.8 0.0 copy-start.12
  26.8 0.0 copy-start.1
  26.8 0.0 copy-start.2
  26.8 0.0 copy-start.3
  26.9 0.0 copy-start.4
  26.9 0.0 copy-start.9
  26.9 0.2 copy.43
  27.2 0.1 copy_select_fusion
  27.3 0.2 copy-done.10
  27.5 0.0 copy-done.12
  27.5 0.3 copy-done.1
  27.8 0.1 copy-done.2
  27.9 0.1 copy-done.3
  28.0 0.0 copy-done.4
  28.0 0.0 copy-done.9
  28.0 1.3 %multiply_reduce_fusion = (f32[16,512]{1,0:T(8,128)S(1)}, f32[10,512]{1,0:T(8,128)S(1)}, f32[10,16,512]{2,1,0:T(8,128)S(1)}, f32[10,16,512]{2,1,0:T(8,128)}) fusion(f32[10]{0:T(128)S(1)} %broadcast_multiply_fusion, f32[10,16,512]{2,1,0:T(8,128)S(1)} %copy-done.1, f32[10,16,512]{2,1,0:T(8,128)S(1)} %copy-done.2, f32[16,512]{1,0:T(8,128)S(1)} %copy-done.4, ...), kind=kLoop, calls=%fused_computation.78 | loop fusion | flops 2526208 | bytes 2502796 | tf_op jit(solution)/shard_map/reduce_sum | solution.py:651
  29.4 0.2 pad_slice_fusion.5
  29.6 0.1 fusion.47
  29.7 0.3 fusion.35
  30.1 0.9 %fusion.2 = f32[20,22,512]{2,0,1:T(8,128)S(1)} fusion(f32[10,22,512]{2,1,0:T(8,128)S(1)} %pad_maximum_fusion, pred[10,10]{0,1:T(8,128)(4,1)S(1)} %get-tuple-element.51, pred[10,10]{0,1:T(8,128)(4,1)S(1)} %get-tuple-element.50), kind=kOutput, calls=%fused_computation.22 | convolution fusion | flops 27033800 | bytes 1351880 | tf_op jit(solution)/shard_map/ij,jtw->itw/dot_general | solution.py:595
  30.9 0.2 slice_reduce_fusion
  31.1 0.1 fusion.54
  31.2 0.2 copy.46.main_ref
  31.4 0.1 copy.47.rim_own_ref
  31.5 0.1 copy.48.rim_next_ref
  31.6 32.4 %shard_map.157 = (f32[10,16,512]{2,1,0:T(8,128)S(1)}, f32[10,6,512]{2,1,0:T(8,128)S(1)}, f32[10,6,512]{2,1,0:T(8,128)S(1)}, f32[40,128]{1,0:T(8,128)S(1)}, f32[64,128]{1,0:T(8,128)S(1)}) custom-call(f32[10,16,512]{2,1,0:T(8,128)S(1)} %copy.46.main_ref, f32[10,6,512]{2,1,0:T(8,128)S(1)} %copy.47.rim_own_ref, f32[10,6,512]{2,1,0:T(8,128)S(1)} %copy.48.rim_next_ref, ...), custom_call_target="tpu_custom_call" | custom-call | tf_op jit(solution)/shard_map/pallas_call | solution.py:512
  64.0 0.1 fusion.52
  64.1 0.0 copy-start
  64.1 0.0 copy-start.6
  64.1 0.0 copy-start.7
  64.1 0.0 copy-start.8
  64.1 0.3 fusion.44
  64.4 0.4 fusion.4
  64.8 0.0 copy-start.5
  64.9 0.2 copy-done
  65.0 0.0 copy-done.6
  65.1 1.2 %minimum_subtract_fusion = (f32[10,16,512]{2,1,0:T(8,128)}, f32[10,16,512]{2,1,0:T(8,128)}) fusion(f32[10]{0:T(128)S(1)} %copy-done.6, f32[10]{0:T(128)S(1)} %copy-done.7, f32[10,512]{1,0:T(8,128)S(1)} %sub.44, f32[10,16,512]{2,0,1:T(8,128)S(1)} %fusion.4, f32[10]{0:T(128)S(1)} %copy-done.8, f32[10,16,512]{2,1,0:T(8,128)S(1)} %copy-done), kind=kLoop, calls=%fused_computation.76 | loop fusion | flops 1146880 | bytes 1331320 | tf_op jit(solution)/shard_map/sub | solution.py:667
  66.3 0.6 add_minimum_fusion
  (23 shorter events, 0.3 us)
Async XLA Ops:
  25.0 0.7 copy-start.11
  26.8 0.7 copy-start.10
  26.8 0.7 copy-start.12
  26.8 1.0 %copy-start.1 = (f32[10,16,512]{2,1,0:T(8,128)S(1)}, f32[10,16,512]{2,1,0:T(8,128)}, u32[]{:S(2)}) copy-start(f32[10,16,512]{2,1,0:T(8,128)} %param.17) | copy-start | bytes 983044
  26.8 1.1 %copy-start.2 = (f32[10,16,512]{2,1,0:T(8,128)S(1)}, f32[10,16,512]{2,1,0:T(8,128)}, u32[]{:S(2)}) copy-start(f32[10,16,512]{2,1,0:T(8,128)} %param.13) | copy-start | bytes 983044
  26.8 1.2 %copy-start.3 = (f32[10,16,512]{2,1,0:T(8,128)S(1)}, f32[10,16,512]{2,1,0:T(8,128)}, u32[]{:S(2)}) copy-start(f32[10,16,512]{2,1,0:T(8,128)} %param.16) | copy-start | bytes 983044
  26.9 1.2 %copy-start.4 = (f32[16,512]{1,0:T(8,128)S(1)}, f32[16,512]{1,0:T(8,128)}, u32[]{:S(2)}) copy-start(f32[16,512]{1,0:T(8,128)} %param.15) | copy-start | bytes 98308
  26.9 1.1 %copy-start.9 = (f32[10]{0:T(128)S(1)}, f32[10]{0:T(128)}, u32[]{:S(2)}) copy-start(f32[10]{0:T(128)} %param.22) | copy-start | bytes 124
  64.1 1.0 %copy-start = (f32[10,16,512]{2,1,0:T(8,128)S(1)}, f32[10,16,512]{2,1,0:T(8,128)}, u32[]{:S(2)}) copy-start(f32[10,16,512]{2,1,0:T(8,128)} %param.14) | copy-start | bytes 983044
  64.1 1.0 %copy-start.6 = (f32[10]{0:T(128)S(1)}, f32[10]{0:T(128)}, u32[]{:S(2)}) copy-start(f32[10]{0:T(128)} %param.20) | copy-start | bytes 124
  64.1 1.0 %copy-start.7 = (f32[10]{0:T(128)S(1)}, f32[10]{0:T(128)}, u32[]{:S(2)}) copy-start(f32[10]{0:T(128)} %param.21) | copy-start | bytes 124
  64.1 0.9 %copy-start.8 = (f32[10]{0:T(128)S(1)}, f32[10]{0:T(128)}, u32[]{:S(2)}) copy-start(f32[10]{0:T(128)} %param.19) | copy-start | bytes 124
  64.8 1.4 %copy-start.5 = (f32[16,512]{1,0:T(8,128)S(1)}, f32[16,512]{1,0:T(8,128)}, u32[]{:S(2)}) copy-start(f32[16,512]{1,0:T(8,128)} %param.18) | copy-start | bytes 98308

commit v18 on v17

--- a/solution.py
+++ b/solution.py
@@ -621,12 +621,12 @@
         both,
         jnp.concatenate(
             [
-                jnp.concatenate([suffix, rim_own + off[:, None]], 1),
-                jnp.concatenate([beyond + off_next[:, None], rim_next + off_next[:, None]], 1),
+                jnp.concatenate([local, rim_own], 1),
+                jnp.concatenate([beyond, rim_next], 1),
             ],
             0,
         ),
-    )
+    ) + route_up(both, jnp.concatenate([off, off_next], 0)[:, None])
     at_sink, rim_sink = sinks[:, :length], sinks[:, length:]
     last = lax.axis_index("hours") == lax.axis_size("hours") - 1
     later_duals = bring_forward(at_sink, travel_delay, jnp.where(last, 0.0, rim_sink))

time: 67.1 us -> 66.8 us (level)
  local copies, waits for them, and re-layouts: 2.68 us -> 1.95 us
    unnamed x30 -> x29, local copies, waits for them, and re-layouts: 2.06 us -> 1.37 us
where the time goes in v18:
time: 66.8 us; the launch traced here: 66.6 us
  Pallas kernels  55.1 us (82%)
  other arithmetic  6.41 us (10%)
  matrix products  2.08 us (3%)
  local copies, waits for them, and re-layouts  1.95 us (3%)
  between operations  1.03 us (2%)
    pallas_call x1, Pallas kernels, flow_exchange(): pl.pallas_call(flow_kernel, out_shape=[shape(main_next), shape(rim_own),...  32.4 us
    pallas_call x1, Pallas kernels, dual_exchange(): pl.pallas_call(dual_kernel, out_shape=[jax.ShapeDtypeStruct(t.shape, t.dt...  22.8 us
    reduce_sum x1, other arithmetic, iterate(): jnp.sum(scale_sum * efficiency[:, None, None] * extrapolated, 0)  1.49 us
    unnamed x29, local copies, waits for them, and re-layouts  1.37 us

profile of v18, /device:TPU:8, one launch (start us, length us, event | category | flops | bytes accessed | tf_op | source)
XLA Modules:
  0.0 66.6 jit_solution(2534434797975864539)
XLA Ops:
  0.6 1.2 %fusion.6 = f32[10,16,512]{2,0,1:T(8,128)S(1)} fusion(f32[10,16,512]{2,1,0:T(8,128)} %param.14), kind=kOutput, calls=%fused_computation.31 | output fusion | flops 1228800 | bytes 655360 | tf_op jit(solution)/shard_map/suffix_local/reduce_window_sum | solution.py:673
  1.8 0.2 copy.32.sloc_ref
  2.1 0.0 copy-start.10
  2.1 22.8 %shard_map.156 = (f32[40,128]{1,0:T(8,128)S(1)}, f32[40,128]{1,0:T(8,128)S(1)}, f32[10,16,512]{2,1,0:T(8,128)S(1)}, f32[10,6,512]{2,1,0:T(8,128)S(1)}, f32[10,6,512]{2,1,0:T(8,128)S(1)}) custom-call(f32[10,16,512]{2,1,0:T(8,128)S(1)} %copy.32.sloc_ref, f32[40,128]{1,0:T(8,128)S(1)} %reshape_squeeze.3.t_ref), custom_call_target="tpu_custom_call" | custom-call | tf_op jit(solution)/shard_map/pallas_call | solution.py:293
  24.8 0.1 maximum_maximum_fusion
  25.0 0.0 copy-done.10
  25.0 0.1 iota_compare_fusion
  25.1 1.0 %fusion = f32[10,22,512]{2,0,1:T(8,128)S(1)} fusion(f32[20,22,512]{2,1,0:T(8,128)S(1)} %maximum_maximum_fusion, pred[10,10]{0,1:T(8,128)(4,1)S(1)} %get-tuple-element.51, pred[10,10]{0,1:T(8,128)(4,1)S(1)} %get-tuple-element.50), kind=kOutput, calls=%fused_computation.6 | convolution fusion | flops 27033800 | bytes 1351880 | tf_op jit(solution)/shard_map/ij,itw->jtw/dot_general | solution.py:599
  26.1 0.2 fusion.52
  26.3 0.0 copy-start.9
  26.3 0.0 copy-start.12
  26.3 0.0 copy-start.1
  26.3 0.0 copy-start.2
  26.4 0.0 copy-start.3
  26.4 0.0 copy-start.4
  26.4 0.0 copy-start.11
  26.4 0.3 copy_add_fusion
  26.7 0.2 copy-done.9
  27.0 0.0 copy-done.12
  27.0 0.3 copy-done.1
  27.3 0.1 copy-done.2
  27.4 0.1 copy-done.3
  27.5 0.0 copy-done.4
  27.5 0.0 copy-done.11
  27.5 1.5 %multiply_reduce_fusion = (f32[16,512]{1,0:T(8,128)S(1)}, f32[10,512]{1,0:T(8,128)S(1)}, f32[10,16,512]{2,1,0:T(8,128)S(1)}, f32[10,16,512]{2,1,0:T(8,128)}) fusion(f32[10]{0:T(128)S(1)} %broadcast_multiply_fusion, f32[10,16,512]{2,1,0:T(8,128)S(1)} %copy-done.1, f32[10,16,512]{2,1,0:T(8,128)S(1)} %copy-done.2, f32[16,512]{1,0:T(8,128)S(1)} %copy-done.4, ...), kind=kLoop, calls=%fused_computation.79 | loop fusion | flops 2608128 | bytes 2523276 | tf_op jit(solution)/shard_map/reduce_sum | solution.py:651
  29.0 0.2 pad_slice_fusion.5
  29.2 0.1 fusion.47
  29.4 0.3 fusion.35
  29.7 0.9 %fusion.2 = f32[20,22,512]{2,0,1:T(8,128)S(1)} fusion(f32[10,22,512]{2,1,0:T(8,128)S(1)} %pad_maximum_fusion, pred[10,10]{0,1:T(8,128)(4,1)S(1)} %get-tuple-element.51, pred[10,10]{0,1:T(8,128)(4,1)S(1)} %get-tuple-element.50), kind=kOutput, calls=%fused_computation.22 | convolution fusion | flops 27033800 | bytes 1351880 | tf_op jit(solution)/shard_map/ij,jtw->itw/dot_general | solution.py:595
  30.6 0.2 slice_reduce_fusion
  30.8 0.1 fusion.61
  30.9 0.2 copy.44.main_ref
  31.1 0.1 copy.45.rim_own_ref
  31.2 0.1 copy.46.rim_next_ref
  31.3 32.4 %shard_map.157 = (f32[10,16,512]{2,1,0:T(8,128)S(1)}, f32[10,6,512]{2,1,0:T(8,128)S(1)}, f32[10,6,512]{2,1,0:T(8,128)S(1)}, f32[40,128]{1,0:T(8,128)S(1)}, f32[64,128]{1,0:T(8,128)S(1)}) custom-call(f32[10,16,512]{2,1,0:T(8,128)S(1)} %copy.44.main_ref, f32[10,6,512]{2,1,0:T(8,128)S(1)} %copy.45.rim_own_ref, f32[10,6,512]{2,1,0:T(8,128)S(1)} %copy.46.rim_next_ref, ...), custom_call_target="tpu_custom_call" | custom-call | tf_op jit(solution)/shard_map/pallas_call | solution.py:512
  63.7 0.1 fusion.59
  63.8 0.0 copy-start
  63.8 0.0 copy-start.6
  63.8 0.0 copy-start.7
  63.8 0.0 copy-start.8
  63.8 0.3 fusion.44
  64.1 0.4 fusion.4
  64.5 0.0 copy-start.5
  64.6 0.2 copy-done
  64.7 0.0 copy-done.6
  64.7 0.0 copy-done.7
  64.7 1.2 %minimum_subtract_fusion = (f32[10,16,512]{2,1,0:T(8,128)}, f32[10,16,512]{2,1,0:T(8,128)}) fusion(f32[10]{0:T(128)S(1)} %copy-done.6, f32[10]{0:T(128)S(1)} %copy-done.7, f32[10,512]{1,0:T(8,128)S(1)} %sub.44, f32[10,16,512]{2,0,1:T(8,128)S(1)} %fusion.4, f32[10]{0:T(128)S(1)} %copy-done.8, f32[10,16,512]{2,1,0:T(8,128)S(1)} %copy-done), kind=kLoop, calls=%fused_computation.77 | loop fusion | flops 1146880 | bytes 1331320 | tf_op jit(solution)/shard_map/sub | solution.py:667
  66.0 0.6 add_minimum_fusion
  (21 shorter events, 0.2 us)
Async XLA Ops:
  2.1 22.9 %copy-start.10 = (s32[10]{0:T(128)S(1)}, s32[10]{0:T(128)}, u32[]{:S(2)}) copy-start(s32[10]{0:T(128)} %param.24) | copy-start | bytes 124
  26.3 0.7 copy-start.9
  26.3 0.7 %copy-start.12 = (f32[10]{0:T(128)S(1)}, f32[10]{0:T(128)}, u32[]{:S(2)}) copy-start(f32[10]{0:T(128)} %param.23) | copy-start | bytes 124
  26.3 1.0 %copy-start.1 = (f32[10,16,512]{2,1,0:T(8,128)S(1)}, f32[10,16,512]{2,1,0:T(8,128)}, u32[]{:S(2)}) copy-start(f32[10,16,512]{2,1,0:T(8,128)} %param.17) | copy-start | bytes 983044
  26.3 1.1 %copy-start.2 = (f32[10,16,512]{2,1,0:T(8,128)S(1)}, f32[10,16,512]{2,1,0:T(8,128)}, u32[]{:S(2)}) copy-start(f32[10,16,512]{2,1,0:T(8,128)} %param.13) | copy-start | bytes 983044
  26.4 1.2 %copy-start.3 = (f32[10,16,512]{2,1,0:T(8,128)S(1)}, f32[10,16,512]{2,1,0:T(8,128)}, u32[]{:S(2)}) copy-start(f32[10,16,512]{2,1,0:T(8,128)} %param.16) | copy-start | bytes 983044
  26.4 1.2 %copy-start.4 = (f32[16,512]{1,0:T(8,128)S(1)}, f32[16,512]{1,0:T(8,128)}, u32[]{:S(2)}) copy-start(f32[16,512]{1,0:T(8,128)} %param.15) | copy-start | bytes 98308
  26.4 1.1 %copy-start.11 = (f32[10]{0:T(128)S(1)}, f32[10]{0:T(128)}, u32[]{:S(2)}) copy-start(f32[10]{0:T(128)} %param.22) | copy-start | bytes 124
  63.8 1.0 %copy-start = (f32[10,16,512]{2,1,0:T(8,128)S(1)}, f32[10,16,512]{2,1,0:T(8,128)}, u32[]{:S(2)}) copy-start(f32[10,16,512]{2,1,0:T(8,128)} %param.14) | copy-start | bytes 983044
  63.8 1.0 %copy-start.6 = (f32[10]{0:T(128)S(1)}, f32[10]{0:T(128)}, u32[]{:S(2)}) copy-start(f32[10]{0:T(128)} %param.20) | copy-start | bytes 124
  63.8 1.0 %copy-start.7 = (f32[10]{0:T(128)S(1)}, f32[10]{0:T(128)}, u32[]{:S(2)}) copy-start(f32[10]{0:T(128)} %param.21) | copy-start | bytes 124
  63.8 0.9 %copy-start.8 = (f32[10]{0:T(128)S(1)}, f32[10]{0:T(128)}, u32[]{:S(2)}) copy-start(f32[10]{0:T(128)} %param.19) | copy-start | bytes 124
  64.5 1.4 %copy-start.5 = (f32[16,512]{1,0:T(8,128)S(1)}, f32[16,512]{1,0:T(8,128)}, u32[]{:S(2)}) copy-start(f32[16,512]{1,0:T(8,128)} %param.18) | copy-start | bytes 98308
